TPU v7x, 32 devices: a whole 2x2x4 slice. The times are simulated.
32 devices in a mesh: pipe: 4 (over y, x), ctx: 8 (over z, core).
Axes of the slice: x: 2, y: 2, z: 4, core: 2. Of those that a mesh axis runs over, the one named last changes fastest.
Arguments:
- queries: bfloat16 [4, 1024, 4096], P('pipe', 'ctx'), may hold values from -45 to 45
- keys_values: bfloat16 [4, 1024, 1024], P('pipe', 'ctx'), may hold values from -4 to 4
- out_grads: bfloat16 [4, 1024, 4096], P('pipe', 'ctx'), may hold values from -6 to 6
- doc_lengths: int32 [8], P('pipe'), may hold values from 1 to 384, 1024 in all
Outputs:
- query_grads: bfloat16 [4, 1024, 4096], P('pipe', 'ctx')
- key_value_grads: bfloat16 [4, 1024, 1024], P('pipe', 'ctx')
Inputs may be any that keep to these rules, and one draw needn't show every extreme that they name: `doc_lengths`: the 8 lengths sum to 1024; the longest document has exactly 384 positions.
All inputs are finite; a program needn't handle non-finite values. No bound on the sum of `doc_lengths` on one device may be relied on, other than what follows from the above.
Results may differ from a plain program's by a relative error of at most 0.009.
Values may be sent and summed in bfloat16 or wider, within the bound.
No kernel may reach another device: no remote copies, remote signals or barrier semaphores. Data moves between devices by JAX's collectives and lax.ppermute only.
A program may use at most 64 MiB of HBM per device.

v0:
```python
import math

import jax
import jax.numpy as jnp
from jax import lax
from jax.sharding import PartitionSpec as P

HQ = 32
HK = 4
HD = 128
REACH = 3


def passed_along(value, axis, steps):
    count = lax.axis_size(axis)
    first, last = (max(0, -steps), min(count, count - steps))
    return lax.ppermute(value, axis, [(source, source + steps) for source in range(first, last)])


def doc_of(starts, position):
    return jnp.sum((starts[None, :] <= position[:, None]).astype(jnp.int32), axis=1) - 1


def attend(q_block, kv_window, dout_block, allowed):
    q_rows = q_block.shape[0]
    key_rows = kv_window.shape[0]
    group_size = HQ // HK
    score_scale = 1.0 / math.sqrt(HD)

    def per_group(head_group):
        q_part = lax.dynamic_slice_in_dim(
            q_block, head_group * group_size * HD, group_size * HD, 1
        ).reshape(q_rows, group_size, HD)
        d_part = lax.dynamic_slice_in_dim(
            dout_block, head_group * group_size * HD, group_size * HD, 1
        ).reshape(q_rows, group_size, HD)
        k_part = lax.dynamic_slice_in_dim(kv_window, head_group * HD, HD, 1)
        v_part = lax.dynamic_slice_in_dim(kv_window, HK * HD + head_group * HD, HD, 1)
        scores = (
            jnp.einsum("tgd,kd->gtk", q_part, k_part, preferred_element_type=jnp.float32)
            * score_scale
        )
        scores = jnp.where(allowed[None], scores, -1e30)
        biggest = jnp.max(scores, axis=-1, keepdims=True)
        expo = jnp.where(allowed[None], jnp.exp(scores - biggest), 0.0)
        weights = expo / jnp.sum(expo, axis=-1, keepdims=True)
        weights_low = weights.astype(jnp.bfloat16)
        attended = jnp.einsum(
            "gtk,kd->tgd", weights_low, v_part, preferred_element_type=jnp.float32
        )
        delta = jnp.sum(d_part.astype(jnp.float32) * attended, axis=-1)
        dweights = jnp.einsum("tgd,kd->gtk", d_part, v_part, preferred_element_type=jnp.float32)
        dscores = (weights * (dweights - jnp.transpose(delta)[:, :, None])).astype(jnp.bfloat16)
        q_grad = (
            jnp.einsum("gtk,kd->tgd", dscores, k_part, preferred_element_type=jnp.float32)
            * score_scale
        )
        k_grad = (
            jnp.einsum("gtk,tgd->kd", dscores, q_part, preferred_element_type=jnp.float32)
            * score_scale
        )
        v_grad = jnp.einsum("gtk,tgd->kd", weights_low, d_part, preferred_element_type=jnp.float32)
        return (q_grad.reshape(q_rows, group_size * HD).astype(jnp.bfloat16), k_grad, v_grad)

    q_grads, k_grads, v_grads = lax.map(per_group, jnp.arange(HK, dtype=jnp.int32))
    q_grads = jnp.moveaxis(q_grads, 0, 1).reshape(q_rows, HQ * HD)
    k_grads = jnp.moveaxis(k_grads, 0, 1).reshape(key_rows, HK * HD)
    v_grads = jnp.moveaxis(v_grads, 0, 1).reshape(key_rows, HK * HD)
    return (q_grads, jnp.concatenate([k_grads, v_grads], axis=1))


def on_device(queries, keys_values, out_grads, doc_lengths):
    all_lengths = lax.all_gather(doc_lengths, "pipe", axis=0, tiled=True)
    starts = jnp.cumsum(all_lengths) - all_lengths
    q_local = queries[0]
    kv_local = keys_values[0]
    dout_local = out_grads[0]
    shard_rows = q_local.shape[0]
    here = lax.axis_index("ctx")
    earlier = [passed_along(kv_local, "ctx", offset) for offset in range(1, REACH + 1)]
    kv_window = jnp.concatenate(earlier[::-1] + [kv_local], axis=0)
    first = here * shard_rows
    q_position = first + jnp.arange(shard_rows, dtype=jnp.int32)
    k_position = first - REACH * shard_rows + jnp.arange(kv_window.shape[0], dtype=jnp.int32)
    allowed = (doc_of(starts, q_position)[:, None] == doc_of(starts, k_position)[None, :]) & (
        k_position[None, :] <= q_position[:, None]
    )
    q_grads, kv_grads = attend(q_local, kv_window, dout_local, allowed)

    def part_for(offset):
        return kv_grads[(REACH - offset) * shard_rows : (REACH - offset + 1) * shard_rows]

    own_part = part_for(0)
    total = own_part
    for offset in range(1, REACH + 1):
        total = total + passed_along(part_for(offset), "ctx", -offset)
    return (q_grads[None], total.astype(jnp.bfloat16)[None])


def solution(mesh):
    return jax.shard_map(
        on_device,
        mesh=mesh,
        in_specs=(
            P("pipe", "ctx", None),
            P("pipe", "ctx", None),
            P("pipe", "ctx", None),
            P("pipe"),
        ),
        out_specs=(P("pipe", "ctx", None), P("pipe", "ctx", None)),
        check_vma=False,
    )
```

profile of v0, /device:TPU:1, one launch (start us, length us, event | category | flops | bytes accessed | tf_op | source)
XLA Modules:
  0.0 130.8 jit_solution(12179704514041550974)
XLA Ops:
  0.6 6.4 %collective-permute-start = (bf16[128,1024]{1,0:T(8,128)(2,1)}, bf16[128,1024]{1,0:T(8,128)(2,1)}, u32[]{:S(2)}, u32[]{:S(2)}) collective-permute-start(bf16[128,1024]{1,0:T(8,128)(2,1)} %bitcast.146), channel_id=1, source_target_pairs={{0,3},{1,4},{2,5},{3,6},{4,7},{8,11},{9,12},{10,13},{11,14},{12,15... | collective-permute-start | bytes 786440 | tf_op jit(solution)/shard_map/ppermute | solution.py:17
  7.1 3.2 %collective-permute-start.1 = (bf16[128,1024]{1,0:T(8,128)(2,1)}, bf16[128,1024]{1,0:T(8,128)(2,1)}, u32[]{:S(2)}, u32[]{:S(2)}) collective-permute-start(bf16[128,1024]{1,0:T(8,128)(2,1)} %bitcast.147), channel_id=1, source_target_pairs={{0,2},{1,3},{2,4},{3,5},{4,6},{5,7},{8,10},{9,11},{10,12},{11,13},... | collective-permute-start | bytes 786440 | tf_op jit(solution)/shard_map/ppermute | solution.py:17
  10.3 1.2 dynamic-slice
  12.2 0.9 dynamic-update-slice
  13.0 1.9 %collective-permute-start.2 = (bf16[128,1024]{1,0:T(8,128)(2,1)}, bf16[128,1024]{1,0:T(8,128)(2,1)}, u32[]{:S(2)}, u32[]{:S(2)}) collective-permute-start(bf16[128,1024]{1,0:T(8,128)(2,1)} %bitcast.148), channel_id=1, source_target_pairs={{0,1},{1,2},{2,3},{3,4},{4,5},{5,6},{6,7},{8,9},{9,10},{10,11},{11... | collective-permute-start | bytes 786440 | tf_op jit(solution)/shard_map/ppermute | solution.py:17
  15.0 5.4 %all-reduce = s32[8]{0:T(128)S(1)} all-reduce(s32[8]{0:T(128)S(1)} %dynamic-update-slice), channel_id=1, replica_groups=mesh['pipe'=4,'ctx'=8] {'pipe'}, use_global_device_ids=true, to_apply=%add | all-reduce | flops 8 | bytes 64
  20.7 1.7 %copy.35 = bf16[1,128,4096]{1,2,0:T(8,128)(2,1)S(1)} copy(bf16[1,128,4096]{2,1,0:T(8,128)(2,1)} %param.6) | data formatting | bytes 2097152 | tf_op args[0]
  23.1 2.2 %pad_maximum_fusion = bf16[512,1024]{1,0:T(8,128)(2,1)} fusion(bf16[128,1024]{1,0:T(8,128)(2,1)S(1)} %bitcast.149, bf16[128,1024]{1,0:T(8,128)(2,1)} %collective-permute-done.2, bf16[128,1024]{1,0:T(8,128)(2,1)} %collective-permute-done.1, bf16[128,1024]{1,0:T(8,128)(2,1)} %collective-permute-done), kind=kLoop, calls=%fused_computation.49 | loop fusion | flops 4194304 | bytes 2097152 | tf_op jit(solution)/shard_map/concatenate | solution.py:81
  25.3 59.8 %while.17 = (s32[]{:T(128)}, bf16[4,128,1024]{1,2,0:T(8,128)(2,1)}, f32[4,512,128]{2,1,0:T(8,128)}, f32[4,512,128]{2,1,0:T(8,128)}, s32[4]{0:T(128)S(1)}, /*inde...) while((s32[]{:T(128)}, bf16[4,128,1024]{1,2,0:T(8,128)(2,1)}, ...), condition=%wide.region_7.8_spmd.clone, body=%wide.region_3.7_spmd.clone.sunk | while | flops 813039104 | bytes 24345468 | solution.py:65
  25.3 0.7 dynamic_slice.72
  27.6 3.1 %fusion.90 = (f32[8,128]{1,0:T(8,128)S(1)}, f32[8,128,512]{1,2,0:T(8,128)}) fusion(pred[128,512]{0,1:T(8,128)(4,1)S(1)} %compare_and_fusion.2, bf16[128,8,128]{0,2,1:T(8,128)(2,1)S(1)} %bitcast.138, bf16[512,1024]{1,0:T(8,128)(2,1)} %get-tuple-element.308, s32[]{:T(128)S(6)} %select_n.51), kind=kOutput, calls=%fused_computation.62.clone.1 | convolution fusion | flops 136839680 | bytes 2625540 | tf_op jit(solution)/shard_map/while/body/eval_jaxpr/sub | solution.py:45
  30.8 2.7 %fusion.95 = f32[4,512,128]{2,1,0:T(8,128)} fusion(f32[4,512,128]{2,1,0:T(8,128)} %get-tuple-element.286, s32[]{:T(128)} %get-tuple-element.283, bf16[128,8,128]{0,2,1:T(8,128)(2,1)S(1)} %bitcast.140, f32[8,128,512]{1,2,0:T(8,128)} %get-tuple-element.261, f32[8,128]{1,0:T(8,128)S(1)} %get-tuple-element.262), kind=kOutput, calls=%fused_computation.14.clone.1 | convolution fusion | flops 135266304 | bytes 2626048 | tf_op jit(solution)/shard_map/while/body/eval_jaxpr/gtk,tgd->kd/dot_general | solution.py:62
  33.5 2.2 %fusion.91 = f32[128,8]{0,1:T(8,128)S(1)} fusion(bf16[128,8,128]{0,2,1:T(8,128)(2,1)S(1)} %bitcast.141, bf16[512,1024]{1,0:T(8,128)(2,1)} %get-tuple-element.308, s32[]{:T(128)S(6)} %select_n.50, f32[8,128,512]{1,2,0:T(8,128)} %get-tuple-element.261, f32[8,128]{1,0:T(8,128)S(1)} %get-tuple-element.262), kind=kOutput, calls=%fused_computation.12.clone.1 | convolution fusion | flops 135658496 | bytes 2498564 | tf_op jit(solution)/shard_map/while/body/eval_jaxpr/gtk,kd->tgd/dot_general | solution.py:48
  35.8 1.3 %fusion.92 = bf16[8,128,512]{1,2,0:T(8,128)(2,1)S(1)} fusion(bf16[128,8,128]{0,2,1:T(8,128)(2,1)S(1)} %bitcast.142, f32[8,128]{1,0:T(8,128)S(1)} %bitcast.151, f32[8,128,512]{1,2,0:T(8,128)S(1)} %copy-done.4, f32[8,128]{1,0:T(8,128)S(1)} %get-tuple-element.262, bf16[512,1024]{1,0:T(8,128)(2,1)} %get-tuple-element.308, s32[]{:T(128)S(6)} %select_n.50), kind=kOutput, calls=%fused_computation.4.clone.1 | convolution fusion | flops 136314880 | bytes 3547140 | tf_op jit(solution)/shard_map/while/body/eval_jaxpr/tgd,kd->gtk/dot_general | solution.py:52
  37.1 1.2 fusion.94
  38.3 1.2 fusion.93
  39.5 0.7 constant_dynamic-update-slice_fusion.2
  42.6 3.1 %fusion.90 = (f32[8,128]{1,0:T(8,128)S(1)}, f32[8,128,512]{1,2,0:T(8,128)}) fusion(pred[128,512]{0,1:T(8,128)(4,1)S(1)} %compare_and_fusion.2, bf16[128,8,128]{0,2,1:T(8,128)(2,1)S(1)} %bitcast.138, bf16[512,1024]{1,0:T(8,128)(2,1)} %get-tuple-element.308, s32[]{:T(128)S(6)} %select_n.51), kind=kOutput, calls=%fused_computation.62.clone.1 | convolution fusion | flops 136839680 | bytes 2625540 | tf_op jit(solution)/shard_map/while/body/eval_jaxpr/sub | solution.py:45
  45.7 2.7 %fusion.95 = f32[4,512,128]{2,1,0:T(8,128)} fusion(f32[4,512,128]{2,1,0:T(8,128)} %get-tuple-element.286, s32[]{:T(128)} %get-tuple-element.283, bf16[128,8,128]{0,2,1:T(8,128)(2,1)S(1)} %bitcast.140, f32[8,128,512]{1,2,0:T(8,128)} %get-tuple-element.261, f32[8,128]{1,0:T(8,128)S(1)} %get-tuple-element.262), kind=kOutput, calls=%fused_computation.14.clone.1 | convolution fusion | flops 135266304 | bytes 2626048 | tf_op jit(solution)/shard_map/while/body/eval_jaxpr/gtk,tgd->kd/dot_general | solution.py:62
  48.5 2.2 %fusion.91 = f32[128,8]{0,1:T(8,128)S(1)} fusion(bf16[128,8,128]{0,2,1:T(8,128)(2,1)S(1)} %bitcast.141, bf16[512,1024]{1,0:T(8,128)(2,1)} %get-tuple-element.308, s32[]{:T(128)S(6)} %select_n.50, f32[8,128,512]{1,2,0:T(8,128)} %get-tuple-element.261, f32[8,128]{1,0:T(8,128)S(1)} %get-tuple-element.262), kind=kOutput, calls=%fused_computation.12.clone.1 | convolution fusion | flops 135658496 | bytes 2498564 | tf_op jit(solution)/shard_map/while/body/eval_jaxpr/gtk,kd->tgd/dot_general | solution.py:48
  50.7 1.3 %fusion.92 = bf16[8,128,512]{1,2,0:T(8,128)(2,1)S(1)} fusion(bf16[128,8,128]{0,2,1:T(8,128)(2,1)S(1)} %bitcast.142, f32[8,128]{1,0:T(8,128)S(1)} %bitcast.151, f32[8,128,512]{1,2,0:T(8,128)S(1)} %copy-done.4, f32[8,128]{1,0:T(8,128)S(1)} %get-tuple-element.262, bf16[512,1024]{1,0:T(8,128)(2,1)} %get-tuple-element.308, s32[]{:T(128)S(6)} %select_n.50), kind=kOutput, calls=%fused_computation.4.clone.1 | convolution fusion | flops 136314880 | bytes 3547140 | tf_op jit(solution)/shard_map/while/body/eval_jaxpr/tgd,kd->gtk/dot_general | solution.py:52
  52.1 1.2 fusion.94
  53.2 1.2 fusion.93
  54.5 0.7 constant_dynamic-update-slice_fusion.2
  57.5 3.1 %fusion.90 = (f32[8,128]{1,0:T(8,128)S(1)}, f32[8,128,512]{1,2,0:T(8,128)}) fusion(pred[128,512]{0,1:T(8,128)(4,1)S(1)} %compare_and_fusion.2, bf16[128,8,128]{0,2,1:T(8,128)(2,1)S(1)} %bitcast.138, bf16[512,1024]{1,0:T(8,128)(2,1)} %get-tuple-element.308, s32[]{:T(128)S(6)} %select_n.51), kind=kOutput, calls=%fused_computation.62.clone.1 | convolution fusion | flops 136839680 | bytes 2625540 | tf_op jit(solution)/shard_map/while/body/eval_jaxpr/sub | solution.py:45
  60.7 2.7 %fusion.95 = f32[4,512,128]{2,1,0:T(8,128)} fusion(f32[4,512,128]{2,1,0:T(8,128)} %get-tuple-element.286, s32[]{:T(128)} %get-tuple-element.283, bf16[128,8,128]{0,2,1:T(8,128)(2,1)S(1)} %bitcast.140, f32[8,128,512]{1,2,0:T(8,128)} %get-tuple-element.261, f32[8,128]{1,0:T(8,128)S(1)} %get-tuple-element.262), kind=kOutput, calls=%fused_computation.14.clone.1 | convolution fusion | flops 135266304 | bytes 2626048 | tf_op jit(solution)/shard_map/while/body/eval_jaxpr/gtk,tgd->kd/dot_general | solution.py:62
  63.4 2.1 %fusion.91 = f32[128,8]{0,1:T(8,128)S(1)} fusion(bf16[128,8,128]{0,2,1:T(8,128)(2,1)S(1)} %bitcast.141, bf16[512,1024]{1,0:T(8,128)(2,1)} %get-tuple-element.308, s32[]{:T(128)S(6)} %select_n.50, f32[8,128,512]{1,2,0:T(8,128)} %get-tuple-element.261, f32[8,128]{1,0:T(8,128)S(1)} %get-tuple-element.262), kind=kOutput, calls=%fused_computation.12.clone.1 | convolution fusion | flops 135658496 | bytes 2498564 | tf_op jit(solution)/shard_map/while/body/eval_jaxpr/gtk,kd->tgd/dot_general | solution.py:48
  65.7 1.3 %fusion.92 = bf16[8,128,512]{1,2,0:T(8,128)(2,1)S(1)} fusion(bf16[128,8,128]{0,2,1:T(8,128)(2,1)S(1)} %bitcast.142, f32[8,128]{1,0:T(8,128)S(1)} %bitcast.151, f32[8,128,512]{1,2,0:T(8,128)S(1)} %copy-done.4, f32[8,128]{1,0:T(8,128)S(1)} %get-tuple-element.262, bf16[512,1024]{1,0:T(8,128)(2,1)} %get-tuple-element.308, s32[]{:T(128)S(6)} %select_n.50), kind=kOutput, calls=%fused_computation.4.clone.1 | convolution fusion | flops 136314880 | bytes 3547140 | tf_op jit(solution)/shard_map/while/body/eval_jaxpr/tgd,kd->gtk/dot_general | solution.py:52
  67.0 1.1 fusion.94
  68.2 1.2 fusion.93
  69.4 0.7 constant_dynamic-update-slice_fusion.2
  72.5 3.1 %fusion.90 = (f32[8,128]{1,0:T(8,128)S(1)}, f32[8,128,512]{1,2,0:T(8,128)}) fusion(pred[128,512]{0,1:T(8,128)(4,1)S(1)} %compare_and_fusion.2, bf16[128,8,128]{0,2,1:T(8,128)(2,1)S(1)} %bitcast.138, bf16[512,1024]{1,0:T(8,128)(2,1)} %get-tuple-element.308, s32[]{:T(128)S(6)} %select_n.51), kind=kOutput, calls=%fused_computation.62.clone.1 | convolution fusion | flops 136839680 | bytes 2625540 | tf_op jit(solution)/shard_map/while/body/eval_jaxpr/sub | solution.py:45
  75.6 2.8 %fusion.95 = f32[4,512,128]{2,1,0:T(8,128)} fusion(f32[4,512,128]{2,1,0:T(8,128)} %get-tuple-element.286, s32[]{:T(128)} %get-tuple-element.283, bf16[128,8,128]{0,2,1:T(8,128)(2,1)S(1)} %bitcast.140, f32[8,128,512]{1,2,0:T(8,128)} %get-tuple-element.261, f32[8,128]{1,0:T(8,128)S(1)} %get-tuple-element.262), kind=kOutput, calls=%fused_computation.14.clone.1 | convolution fusion | flops 135266304 | bytes 2626048 | tf_op jit(solution)/shard_map/while/body/eval_jaxpr/gtk,tgd->kd/dot_general | solution.py:62
  78.4 2.2 %fusion.91 = f32[128,8]{0,1:T(8,128)S(1)} fusion(bf16[128,8,128]{0,2,1:T(8,128)(2,1)S(1)} %bitcast.141, bf16[512,1024]{1,0:T(8,128)(2,1)} %get-tuple-element.308, s32[]{:T(128)S(6)} %select_n.50, f32[8,128,512]{1,2,0:T(8,128)} %get-tuple-element.261, f32[8,128]{1,0:T(8,128)S(1)} %get-tuple-element.262), kind=kOutput, calls=%fused_computation.12.clone.1 | convolution fusion | flops 135658496 | bytes 2498564 | tf_op jit(solution)/shard_map/while/body/eval_jaxpr/gtk,kd->tgd/dot_general | solution.py:48
  80.7 1.3 %fusion.92 = bf16[8,128,512]{1,2,0:T(8,128)(2,1)S(1)} fusion(bf16[128,8,128]{0,2,1:T(8,128)(2,1)S(1)} %bitcast.142, f32[8,128]{1,0:T(8,128)S(1)} %bitcast.151, f32[8,128,512]{1,2,0:T(8,128)S(1)} %copy-done.4, f32[8,128]{1,0:T(8,128)S(1)} %get-tuple-element.262, bf16[512,1024]{1,0:T(8,128)(2,1)} %get-tuple-element.308, s32[]{:T(128)S(6)} %select_n.50), kind=kOutput, calls=%fused_computation.4.clone.1 | convolution fusion | flops 136314880 | bytes 3547140 | tf_op jit(solution)/shard_map/while/body/eval_jaxpr/tgd,kd->gtk/dot_general | solution.py:52
  82.0 1.1 fusion.94
  83.2 1.2 fusion.93
  84.4 0.7 constant_dynamic-update-slice_fusion.2
  85.1 1.4 %bitcast_dynamic-update-slice_fusion.1 = f32[512,1024]{1,0:T(8,128)S(1)} fusion(f32[4,512,128]{2,1,0:T(8,128)} %get-tuple-element.119), kind=kLoop, calls=%fused_computation.48 | loop fusion | bytes 2097152
  86.8 1.2 fusion.51
  88.0 5.1 %collective-permute-start.3 = (f32[128,1024]{1,0:T(8,128)}, f32[128,1024]{1,0:T(8,128)}, u32[]{:S(2)}, u32[]{:S(2)}) collective-permute-start(f32[128,1024]{1,0:T(8,128)} %get-tuple-element.179), channel_id=1, source_target_pairs={{1,0},{2,1},{3,2},{4,3},{5,4},{6,5},{7,6},{9,8},{10,9},{11,10},{12... | collective-permute-start | bytes 1572872 | tf_op jit(solution)/shard_map/ppermute | solution.py:17
  93.1 1.3 collective-permute-start.4
  94.4 1.3 collective-permute-start.5
  95.7 1.3 %copy.48 = bf16[1,128,4096]{2,1,0:T(8,128)(2,1)} copy(bf16[1,128,4096]{1,2,0:T(8,128)(2,1)S(1)} %bitcast.145) | data formatting | bytes 2097152 | tf_op jit(solution)/shard_map/broadcast_in_dim;reshape | solution.py:97
  97.0 2.9 %collective-permute-done.3 = f32[128,1024]{1,0:T(8,128)} collective-permute-done((f32[128,1024]{1,0:T(8,128)}, f32[128,1024]{1,0:T(8,128)}, u32[]{:S(2)}, u32[]{:S(2)}) %collective-permute-start.3) | collective-permute-done | bytes 524320 | tf_op jit(solution)/shard_map/ppermute | solution.py:17
  99.9 9.3 %collective-permute-done.4 = f32[128,1024]{1,0:T(8,128)} collective-permute-done((f32[128,1024]{1,0:T(8,128)}, f32[128,1024]{1,0:T(8,128)}, u32[]{:S(2)}, u32[]{:S(2)}) %collective-permute-start.4) | collective-permute-done | bytes 524320 | tf_op jit(solution)/shard_map/ppermute | solution.py:17
  109.3 19.3 %collective-permute-done.5 = f32[128,1024]{1,0:T(8,128)} collective-permute-done((f32[128,1024]{1,0:T(8,128)}, f32[128,1024]{1,0:T(8,128)}, u32[]{:S(2)}, u32[]{:S(2)}) %collective-permute-start.5) | collective-permute-done | bytes 524320 | tf_op jit(solution)/shard_map/ppermute | solution.py:17
  128.6 2.2 %fusion.47 = bf16[1,128,1024]{2,1,0:T(8,128)(2,1)} fusion(f32[128,1024]{1,0:T(8,128)} %collective-permute-done.5, f32[128,1024]{1,0:T(8,128)} %collective-permute-done.4, f32[128,1024]{1,0:T(8,128)} %collective-permute-done.3, f32[512,1024]{1,0:T(8,128)S(1)} %bitcast_dynamic-update-slice_fusion), kind=kLoop, calls=%fused_computation.54 | loop fusion | flops 524288 | bytes 2359296 | tf_op jit(solution)/shard_map/broadcast_in_dim | solution.py:97
  (45 shorter events, 4.8 us)
Async XLA Ops:
  0.6 21.8 %copy-start = (bf16[1,128,4096]{2,1,0:T(8,128)(2,1)S(1)}, bf16[1,128,4096]{2,1,0:T(8,128)(2,1)}, u32[]{:S(2)}) copy-start(bf16[1,128,4096]{2,1,0:T(8,128)(2,1)} %param.8) | copy-start | bytes 3145732
  0.6 22.5 %collective-permute-start = (bf16[128,1024]{1,0:T(8,128)(2,1)}, bf16[128,1024]{1,0:T(8,128)(2,1)}, u32[]{:S(2)}, u32[]{:S(2)}) collective-permute-start(bf16[128,1024]{1,0:T(8,128)(2,1)} %bitcast.146), channel_id=1, source_target_pairs={{0,3},{1,4},{2,5},{3,6},{4,7},{8,11},{9,12},{10,13},{11,14},{12,15... | collective-permute-start | bytes 786440 | tf_op jit(solution)/shard_map/ppermute | solution.py:17
  7.1 16.0 %collective-permute-start.1 = (bf16[128,1024]{1,0:T(8,128)(2,1)}, bf16[128,1024]{1,0:T(8,128)(2,1)}, u32[]{:S(2)}, u32[]{:S(2)}) collective-permute-start(bf16[128,1024]{1,0:T(8,128)(2,1)} %bitcast.147), channel_id=1, source_target_pairs={{0,2},{1,3},{2,4},{3,5},{4,6},{5,7},{8,10},{9,11},{10,12},{11,13},... | collective-permute-start | bytes 786440 | tf_op jit(solution)/shard_map/ppermute | solution.py:17
  13.0 10.1 %collective-permute-start.2 = (bf16[128,1024]{1,0:T(8,128)(2,1)}, bf16[128,1024]{1,0:T(8,128)(2,1)}, u32[]{:S(2)}, u32[]{:S(2)}) collective-permute-start(bf16[128,1024]{1,0:T(8,128)(2,1)} %bitcast.148), channel_id=1, source_target_pairs={{0,1},{1,2},{2,3},{3,4},{4,5},{5,6},{6,7},{8,9},{9,10},{10,11},{11... | collective-permute-start | bytes 786440 | tf_op jit(solution)/shard_map/ppermute | solution.py:17
  20.7 2.4 %copy-start.3 = (bf16[1,128,1024]{2,1,0:T(8,128)(2,1)S(1)}, bf16[1,128,1024]{2,1,0:T(8,128)(2,1)}, u32[]{:S(2)}) copy-start(bf16[1,128,1024]{2,1,0:T(8,128)(2,1)} %param.7) | copy-start | bytes 786436
  33.5 2.3 %copy-start.4 = (f32[8,128,512]{1,2,0:T(8,128)S(1)}, f32[8,128,512]{1,2,0:T(8,128)}, u32[]{:S(2)}) copy-start(f32[8,128,512]{1,2,0:T(8,128)} %get-tuple-element.261) | copy-start | bytes 6291460 | tf_op jit(solution)/shard_map/while
  48.4 2.3 %copy-start.4 = (f32[8,128,512]{1,2,0:T(8,128)S(1)}, f32[8,128,512]{1,2,0:T(8,128)}, u32[]{:S(2)}) copy-start(f32[8,128,512]{1,2,0:T(8,128)} %get-tuple-element.261) | copy-start | bytes 6291460 | tf_op jit(solution)/shard_map/while
  63.4 2.3 %copy-start.4 = (f32[8,128,512]{1,2,0:T(8,128)S(1)}, f32[8,128,512]{1,2,0:T(8,128)}, u32[]{:S(2)}) copy-start(f32[8,128,512]{1,2,0:T(8,128)} %get-tuple-element.261) | copy-start | bytes 6291460 | tf_op jit(solution)/shard_map/while
  78.4 2.3 %copy-start.4 = (f32[8,128,512]{1,2,0:T(8,128)S(1)}, f32[8,128,512]{1,2,0:T(8,128)}, u32[]{:S(2)}) copy-start(f32[8,128,512]{1,2,0:T(8,128)} %get-tuple-element.261) | copy-start | bytes 6291460 | tf_op jit(solution)/shard_map/while
  85.1 1.5 %copy-start.2 = (f32[4,512,128]{2,1,0:T(8,128)S(1)}, f32[4,512,128]{2,1,0:T(8,128)}, u32[]{:S(2)}) copy-start(f32[4,512,128]{2,1,0:T(8,128)} %get-tuple-element.120) | copy-start | bytes 3145732
  86.8 8.9 %copy-start.1 = (bf16[4,128,1024]{1,2,0:T(8,128)(2,1)S(1)}, bf16[4,128,1024]{1,2,0:T(8,128)(2,1)}, u32[]{:S(2)}) copy-start(bf16[4,128,1024]{1,2,0:T(8,128)(2,1)} %get-tuple-element.118) | copy-start | bytes 3145732
  88.0 11.9 %collective-permute-start.3 = (f32[128,1024]{1,0:T(8,128)}, f32[128,1024]{1,0:T(8,128)}, u32[]{:S(2)}, u32[]{:S(2)}) collective-permute-start(f32[128,1024]{1,0:T(8,128)} %get-tuple-element.179), channel_id=1, source_target_pairs={{1,0},{2,1},{3,2},{4,3},{5,4},{6,5},{7,6},{9,8},{10,9},{11,10},{12... | collective-permute-start | bytes 1572872 | tf_op jit(solution)/shard_map/ppermute | solution.py:17
  93.1 16.2 %collective-permute-start.4 = (f32[128,1024]{1,0:T(8,128)}, f32[128,1024]{1,0:T(8,128)}, u32[]{:S(2)}, u32[]{:S(2)}) collective-permute-start(f32[128,1024]{1,0:T(8,128)} %get-tuple-element.181), channel_id=1, source_target_pairs={{2,0},{3,1},{4,2},{5,3},{6,4},{7,5},{10,8},{11,9},{12,10},{13,11},... | collective-permute-start | bytes 1572872 | tf_op jit(solution)/shard_map/ppermute | solution.py:17
  94.4 34.2 %collective-permute-start.5 = (f32[128,1024]{1,0:T(8,128)}, f32[128,1024]{1,0:T(8,128)}, u32[]{:S(2)}, u32[]{:S(2)}) collective-permute-start(f32[128,1024]{1,0:T(8,128)} %get-tuple-element.180), channel_id=1, source_target_pairs={{3,0},{4,1},{5,2},{6,3},{7,4},{11,8},{12,9},{13,10},{14,11},{15,12... | collective-permute-start | bytes 1572872 | tf_op jit(solution)/shard_map/ppermute | solution.py:17
where the time goes:
time: 132 us; the launch traced here: 131 us
  matrix products  47 us (36%)
  waiting for transfers between devices  31.6 us (24%)
  starting transfers between devices  19.2 us (15%)
  local copies, waits for them, and re-layouts  14.8 us (11%)
  loops' own time  5.75 us (4%)
  other arithmetic  5.54 us (4%)
  blocking collectives  5.39 us (4%)
  between operations  1.44 us (1%)
    ppermute x6, waiting for transfers between devices, passed_along(): lax.ppermute(value, axis, [(source, source + steps) for source in range(f...  31.6 us
    ppermute x6, starting transfers between devices, passed_along(): lax.ppermute(value, axis, [(source, source + steps) for source in range(f...  19.2 us
    sub x4, matrix products, per_group(): expo = jnp.where(allowed[None], jnp.exp(scores - biggest), 0.0)  12.6 us
    dot_general x4, matrix products, per_group(): jnp.einsum('gtk,tgd->kd', weights_low, d_part, preferred_element_type=jnp...  10.9 us
    dot_general x4, matrix products, per_group(): jnp.einsum('gtk,kd->tgd', weights_low, v_part, preferred_element_type=jnp...  8.6 us
    unnamed x14, local copies, waits for them, and re-layouts  5.96 us
    another operation x1, loops' own time, attend(): lax.map(per_group, jnp.arange(HK, dtype=jnp.int32))  5.75 us
    unnamed x1, blocking collectives  5.39 us
  transfers between devices with their start and end apart: 6, of which 3 were waited for; matrix products, arithmetic and copies ran while one was open for 5% of the time, Pallas kernels for 0%

commit v1 on v0

v1 whole, which is shorter than its diff:
```python
import functools
import math

import jax
import jax.numpy as jnp
from jax import lax
from jax.experimental import pallas as pl
from jax.experimental.pallas import tpu as pltpu
from jax.sharding import PartitionSpec as P

HQ = 32
HK = 4
HD = 128
REACH = 3
GROUP = HQ // HK
F32 = jnp.float32
BF16 = jnp.bfloat16
NT = (((1,), (1,)), ((), ()))
NN = (((1,), (0,)), ((), ()))


def moved(value, target_of):
    count = lax.axis_size("ctx")
    pairs = [(i, target_of(i)) for i in range(count)]
    return lax.ppermute(value, "ctx", [(s, t) for s, t in pairs if 0 <= t < count])


def one_three(value):
    return moved(value, lambda i: i + 1 if i % 2 else i + 3)


def one_three_back(value):
    return moved(value, lambda i: i - 3 if i % 2 else i - 1)


def three_one(value):
    return moved(value, lambda i: i + 3 if i % 2 else i + 1)


def three_one_back(value):
    return moved(value, lambda i: i - 1 if i % 2 else i - 3)


def swapped(value):
    return moved(value, lambda i: i ^ 1)


def all_lengths_by_xor(lengths):
    count = lax.axis_size("pipe")
    stride = 1
    while stride < count:
        other = lax.ppermute(lengths, "pipe", [(i, i ^ stride) for i in range(count)])
        lengths = jnp.concatenate([lengths, other])
        stride *= 2
    return lengths


def kernel(per_pipe, lens_ref, q_ref, d_ref, kv0_ref, kv1_ref, kv2_ref, kv3_ref,
           dq_ref, g0_ref, g1_ref, g2_ref, g3_ref,
           bias_scr, kt_scr, s_scr, p_scr, dp_scr, ds_scr, w_scr):
    rows = q_ref.shape[0]
    blocks = REACH + 1
    g = pl.program_id(0)
    here = lax.axis_index("ctx")
    pipe = lax.axis_index("pipe")
    odd = lax.rem(here, 2)
    offsets = (0, 1 + 2 * odd, 2, 3 - 2 * odd)
    kv_refs = (kv0_ref, kv1_ref, kv2_ref, kv3_ref)
    g_refs = (g0_ref, g1_ref, g2_ref, g3_ref)

    @pl.when(g == 0)
    def _():
        t_pos = here * rows + lax.broadcasted_iota(jnp.int32, (1, rows), 1)
        total = lens_ref.shape[0]

        def step(d, carry):
            start, doc_start = carry
            slot = ((d // per_pipe) ^ pipe) * per_pipe + d % per_pipe
            doc_start = jnp.where(t_pos >= start, start, doc_start)
            return start + lens_ref[slot], doc_start

        _, doc_start = lax.fori_loop(
            0, total, step, (jnp.int32(0), jnp.zeros((1, rows), jnp.int32))
        )
        for b in range(blocks):
            u_pos = (here - offsets[b]) * rows + lax.broadcasted_iota(jnp.int32, (rows, rows), 0)
            ok = (u_pos >= doc_start) & (u_pos <= t_pos)
            bias_scr[b] = jnp.where(ok, 0.0, -1e30).astype(F32)

    kcol = pl.ds(pl.multiple_of(g * HD, HD), HD)
    vcol = pl.ds(pl.multiple_of(HK * HD + g * HD, HD), HD)
    for b in range(blocks):
        kt_scr[:, b * rows:(b + 1) * rows] = kv_refs[b][:, kcol].T
    scale = 1.0 / math.sqrt(HD)
    c = scale * math.log2(math.e)
    for pair in range(GROUP // 2):
        lo, hi = 2 * pair * HD, (2 * pair + 1) * HD
        q2 = jnp.concatenate([q_ref[:, lo:lo + HD], q_ref[:, hi:hi + HD]], axis=0)
        d2 = jnp.concatenate([d_ref[:, lo:lo + HD], d_ref[:, hi:hi + HD]], axis=0)
        biggest = None
        for b in range(blocks):
            s = lax.dot_general(kv_refs[b][:, kcol], q2, NT, preferred_element_type=F32)
            s = s + jnp.concatenate([bias_scr[b]] * 2, axis=1)
            s_scr[b] = s
            top = jnp.max(s, axis=0, keepdims=True)
            biggest = top if biggest is None else jnp.maximum(biggest, top)
        total = dot = None
        for b in range(blocks):
            p = jnp.exp2((s_scr[b] - biggest) * c)
            dp = lax.dot_general(kv_refs[b][:, vcol], d2, NT, preferred_element_type=F32)
            p_scr[b] = p
            dp_scr[b] = dp
            sp = jnp.sum(p, axis=0, keepdims=True)
            sd = jnp.sum(p * dp, axis=0, keepdims=True)
            total = sp if total is None else total + sp
            dot = sd if dot is None else dot + sd
        inv = 1.0 / total
        delta = dot * inv
        columns = slice(2 * pair * rows, 2 * (pair + 1) * rows)
        for b in range(blocks):
            w = p_scr[b] * inv
            ds_scr[b * rows:(b + 1) * rows, columns] = (w * (dp_scr[b] - delta)).astype(BF16)
            w_scr[b * rows:(b + 1) * rows, columns] = w.astype(BF16)
        dqt = lax.dot_general(kt_scr[...], ds_scr[:, columns], NN, preferred_element_type=F32)
        dq = (dqt * scale).astype(BF16).T
        dq_ref[:, lo:lo + HD] = dq[:rows]
        dq_ref[:, hi:hi + HD] = dq[rows:]
    qs = jnp.concatenate([q_ref[:, h * HD:(h + 1) * HD] for h in range(GROUP)], axis=0)
    dk = lax.dot_general(ds_scr[...], qs, NN, preferred_element_type=F32) * scale
    dos = jnp.concatenate([d_ref[:, h * HD:(h + 1) * HD] for h in range(GROUP)], axis=0)
    dv = lax.dot_general(w_scr[...], dos, NN, preferred_element_type=F32)
    for b in range(blocks):
        part = slice(b * rows, (b + 1) * rows)
        g_refs[b][:, kcol] = dk[part].astype(g_refs[b].dtype)
        g_refs[b][:, vcol] = dv[part].astype(g_refs[b].dtype)


def attention(per_pipe, lens, q, dout, kv0, kv1, kv2, kv3):
    rows = q.shape[0]
    wide = kv0.shape[1]
    keys = (REACH + 1) * rows
    head = pl.BlockSpec((rows, GROUP * HD), lambda g: (0, g))
    whole = pl.BlockSpec((rows, wide), lambda g: (0, 0))
    like = lambda dtype: jax.ShapeDtypeStruct((rows, wide), dtype)
    return pl.pallas_call(
        functools.partial(kernel, per_pipe),
        grid=(HK,),
        in_specs=[pl.BlockSpec(memory_space=pltpu.SMEM), head, head, whole, whole, whole, whole],
        out_specs=[head, whole, whole, whole, whole],
        out_shape=[jax.ShapeDtypeStruct(q.shape, BF16), like(F32), like(BF16), like(BF16), like(BF16)],
        scratch_shapes=[
            pltpu.VMEM((REACH + 1, rows, rows), F32),
            pltpu.VMEM((HD, keys), BF16),
            pltpu.VMEM((REACH + 1, rows, 2 * rows), F32),
            pltpu.VMEM((REACH + 1, rows, 2 * rows), F32),
            pltpu.VMEM((REACH + 1, rows, 2 * rows), F32),
            pltpu.VMEM((keys, GROUP * rows), BF16),
            pltpu.VMEM((keys, GROUP * rows), BF16),
        ],
        name="attention",
    )(lens, q, dout, kv0, kv1, kv2, kv3)


def on_device(queries, keys_values, out_grads, doc_lengths):
    kv = keys_values[0]
    near = one_three(kv)
    far = three_one(kv)
    lens = all_lengths_by_xor(doc_lengths)
    side = swapped(near)
    dq, own, g_near, g_side, g_far = attention(
        doc_lengths.shape[0], lens, queries[0], out_grads[0], kv, near, side, far
    )
    back = three_one_back(g_far)
    joined = (g_near.astype(F32) + swapped(g_side).astype(F32)).astype(BF16)
    total = own + back.astype(F32) + one_three_back(joined).astype(F32)
    return (dq[None], total.astype(BF16)[None])


def solution(mesh):
    spec = P("pipe", "ctx", None)
    return jax.shard_map(
        on_device,
        mesh=mesh,
        in_specs=(spec, spec, spec, P("pipe")),
        out_specs=(spec, spec),
        check_vma=False,
    )
```

time: 132 us -> 52.7 us (0.40)
  matrix products: 47 us -> 0 us
  waiting for transfers between devices: 31.6 us -> 17.1 us
  local copies, waits for them, and re-layouts: 14.8 us -> 0.78 us
  Pallas kernels: 0 us -> 13.5 us
  loops' own time: 5.75 us -> 0 us
  blocking collectives: 5.39 us -> 0 us
  other arithmetic: 5.54 us -> 2.56 us
  starting transfers between devices: 19.2 us -> 17.2 us
    dot_general x20 -> x0, matrix products: 34.4 us -> none  [the longest x4 10.9 us: per_group(): jnp.einsum('gtk,tgd->kd', weights_low, d_part, preferred_element_type=jnp...]
    ppermute x6 -> x8, waiting for transfers between devices: 31.6 us -> 17.1 us  [the longest x6 14.7 us: moved(): lax.ppermute(value, 'ctx', [(s, t) for s, t in pairs if 0 <= t < count])]
    pallas_call x0 -> x1, Pallas kernels: none -> 13.5 us  [attention(): pl.pallas_call(functools.partial(kernel, per_pipe), grid=(HK,), in_specs=...]
    sub x4 -> x0, matrix products: 12.6 us -> none  [per_group(): expo = jnp.where(allowed[None], jnp.exp(scores - biggest), 0.0)]
    another operation x1 -> x0, loops' own time: 5.75 us -> none  [attend(): lax.map(per_group, jnp.arange(HK, dtype=jnp.int32))]
    unnamed x1 -> x0, blocking collectives: 5.39 us -> none
    unnamed x14 -> x10, local copies, waits for them, and re-layouts: 5.96 us -> 0.78 us
    dynamic_update_slice x4 -> x0, local copies, waits for them, and re-layouts: 2.9 us -> none  [attend(): lax.map(per_group, jnp.arange(HK, dtype=jnp.int32))]
  transfers between devices with their start and end apart: 6 -> 8, of which waited for: 3 -> 5; matrix products, arithmetic and copies ran while one was open for 5% -> 3% of each run, Pallas kernels for 0% -> 0%
where the time goes in v1:
time: 52.7 us; the launch traced here: 51.8 us
  starting transfers between devices  17.2 us (33%)
  waiting for transfers between devices  17.1 us (32%)
  Pallas kernels  13.5 us (26%)
  other arithmetic  2.56 us (5%)
  local copies, waits for them, and re-layouts  0.78 us (1%)
  between operations  0.72 us (1%)
    ppermute x6, starting transfers between devices, moved(): lax.ppermute(value, 'ctx', [(s, t) for s, t in pairs if 0 <= t < count])  14.7 us
    ppermute x6, waiting for transfers between devices, moved(): lax.ppermute(value, 'ctx', [(s, t) for s, t in pairs if 0 <= t < count])  14.7 us
    pallas_call x1, Pallas kernels, attention(): pl.pallas_call(functools.partial(kernel, per_pipe), grid=(HK,), in_specs=...  13.5 us
    ppermute x2, starting transfers between devices, all_lengths_by_xor(): lax.ppermute(lengths, 'pipe', [(i, i ^ stride) for i in range(count)])  2.45 us
    ppermute x2, waiting for transfers between devices, all_lengths_by_xor(): lax.ppermute(lengths, 'pipe', [(i, i ^ stride) for i in range(count)])  2.39 us
  transfers between devices with their start and end apart: 8, of which 5 were waited for; matrix products, arithmetic and copies ran while one was open for 3% of the time, Pallas kernels for 0%

profile of v1, /device:TPU:1, one launch (start us, length us, event | category | flops | bytes accessed | tf_op | source)
XLA Modules:
  0.0 51.8 jit_solution(93828005839110635)
XLA Ops:
  0.6 0.0 copy-start.4
  0.6 4.6 %collective-permute-start.2 = (bf16[128,1024]{1,0:T(8,128)(2,1)}, bf16[128,1024]{1,0:T(8,128)(2,1)S(1)}, u32[]{:S(2)}, u32[]{:S(2)}) collective-permute-start(bf16[128,1024]{1,0:T(8,128)(2,1)} %bitcast.8), channel_id=1, source_target_pairs={{0,3},{1,2},{2,5},{3,4},{4,7},{5,6},{8,11},{9,10},{10,13},{11,12},... | collective-permute-start | bytes 786440 | tf_op jit(solution)/shard_map/ppermute | solution.py:25
  5.2 3.9 %collective-permute-start.4 = (bf16[128,1024]{1,0:T(8,128)(2,1)}, bf16[128,1024]{1,0:T(8,128)(2,1)S(1)}, u32[]{:S(2)}, u32[]{:S(2)}) collective-permute-start(bf16[128,1024]{1,0:T(8,128)(2,1)} %bitcast.9), channel_id=1, source_target_pairs={{0,1},{1,4},{2,3},{3,6},{4,5},{6,7},{8,9},{9,12},{10,11},{11,14},{... | collective-permute-start | bytes 786440 | tf_op jit(solution)/shard_map/ppermute | solution.py:25
  9.2 2.5 %collective-permute-done.2.kv1_ref = bf16[128,1024]{1,0:T(8,128)(2,1)S(1)} collective-permute-done((bf16[128,1024]{1,0:T(8,128)(2,1)}, bf16[128,1024]{1,0:T(8,128)(2,1)S(1)}, u32[]{:S(2)}, u32[]{:S(2)}) %collective-permute-start.2) | collective-permute-done | bytes 262176 | tf_op jit(solution)/shard_map/ppermute | solution.py:25
  11.6 0.0 copy-start.1
  11.6 0.4 collective-permute-start.3
  12.1 0.0 copy-done.4
  12.1 1.2 %collective-permute-start = (s32[2]{0:T(128)S(1)}, s32[2]{0:T(128)S(1)}, u32[]{:S(2)}, u32[]{:S(2)}) collective-permute-start(s32[2]{0:T(128)S(1)} %copy-done.4), channel_id=1, source_target_pairs={{0,8},{8,0},{16,24},{24,16},{1,9},{9,1},{17,25},{25,17},{2,10},{10... | collective-permute-start | bytes 32 | tf_op jit(solution)/shard_map/ppermute | solution.py:52
  13.3 1.2 %collective-permute-done = s32[2]{0:T(128)S(1)} collective-permute-done((s32[2]{0:T(128)S(1)}, s32[2]{0:T(128)S(1)}, u32[]{:S(2)}, u32[]{:S(2)}) %collective-permute-start) | collective-permute-done | bytes 40 | tf_op jit(solution)/shard_map/ppermute | solution.py:52
  14.5 0.1 pad_add_fusion
  14.6 1.2 %collective-permute-start.1 = (s32[4]{0:T(128)S(1)}, s32[4]{0:T(128)S(1)}, u32[]{:S(2)}, u32[]{:S(2)}) collective-permute-start(s32[4]{0:T(128)S(1)} %pad_add_fusion), channel_id=1, source_target_pairs={{0,16},{8,24},{16,0},{24,8},{1,17},{9,25},{17,1},{25,9},{2,18},{10... | collective-permute-start | bytes 56 | tf_op jit(solution)/shard_map/ppermute | solution.py:52
  15.8 1.2 %collective-permute-done.1 = s32[4]{0:T(128)S(1)} collective-permute-done((s32[4]{0:T(128)S(1)}, s32[4]{0:T(128)S(1)}, u32[]{:S(2)}, u32[]{:S(2)}) %collective-permute-start.1) | collective-permute-done | bytes 48 | tf_op jit(solution)/shard_map/ppermute | solution.py:52
  17.0 0.7 %pad_add_fusion.1.lens_ref = s32[8]{0:T(128)} fusion(s32[4]{0:T(128)S(1)} %collective-permute-done.1, s32[2]{0:T(128)S(1)} %collective-permute-done, s32[2]{0:T(128)S(1)} %copy-done.4), kind=kLoop, calls=%fused_computation.4 | loop fusion | flops 16 | bytes 64 | tf_op jit(solution)/shard_map/concatenate | solution.py:53
  17.6 0.0 collective-permute-done.4.kv3_ref
  17.6 0.0 copy-start.2
  17.6 0.0 collective-permute-done.3.kv2_ref
  17.7 0.0 copy-start.3
  17.7 0.0 copy-done.1
  17.7 0.7 %copy-done.2 = bf16[128,1024]{1,0:T(8,128)(2,1)} copy-done((bf16[128,1024]{1,0:T(8,128)(2,1)}, bf16[128,1024]{1,0:T(8,128)(2,1)S(1)}, u32[]{:S(2)}) %copy-start.2) | copy-done | bytes 262168
  18.4 0.1 copy-done.3
  18.4 13.5 %attention.1 = (bf16[128,4096]{1,0:T(8,128)(2,1)}, f32[128,1024]{1,0:T(8,128)}, bf16[128,1024]{1,0:T(8,128)(2,1)}, bf16[128,1024]{1,0:T(8,128)(2,1)}, bf16[128,1024]{1,0:T(8,128)(2,1)}) custom-call(s32[8]{0:T(128)} %pad_add_fusion.1.lens_ref, bf16[128,4096]{1,0:T(8,128)(2,1)} %bitcast.6, bf16[128,4096]{1,0:T(8,128)(2,1)} %bitcast.7, ...), custom_call_target="tpu_custom_call" | custom-call | tf_op jit(solution)/shard_map/attention/pallas_call | solution.py:145
  31.9 0.0 copy-start
  31.9 2.4 %collective-permute-start.6 = (bf16[128,1024]{1,0:T(8,128)(2,1)}, bf16[128,1024]{1,0:T(8,128)(2,1)S(1)}, u32[]{:S(2)}, u32[]{:S(2)}) collective-permute-start(bf16[128,1024]{1,0:T(8,128)(2,1)} %get-tuple-element.11), channel_id=1, source_target_pairs={{0,1},{1,0},{2,3},{3,2},{4,5},{5,4},{6,7},{7,6},{8,9},{9,8},{10,11... | collective-permute-start | bytes 786440 | tf_op jit(solution)/shard_map/ppermute | solution.py:25
  34.4 2.1 %collective-permute-start.5 = (bf16[128,1024]{1,0:T(8,128)(2,1)}, bf16[128,1024]{1,0:T(8,128)(2,1)S(1)}, u32[]{:S(2)}, u32[]{:S(2)}) collective-permute-start(bf16[128,1024]{1,0:T(8,128)(2,1)} %get-tuple-element.9), channel_id=1, source_target_pairs={{1,0},{3,2},{4,1},{5,4},{6,3},{7,6},{9,8},{11,10},{12,9},{13,12},{... | collective-permute-start | bytes 786440 | tf_op jit(solution)/shard_map/ppermute | solution.py:25
  36.4 0.0 collective-permute-done.6
  36.4 1.0 %add_convert_fusion.1 = bf16[128,1024]{1,0:T(8,128)(2,1)S(1)} fusion(bf16[128,1024]{1,0:T(8,128)(2,1)S(1)} %collective-permute-done.6, bf16[128,1024]{1,0:T(8,128)(2,1)} %get-tuple-element.10), kind=kLoop, calls=%fused_computation.1 | loop fusion | flops 524288 | bytes 786432 | tf_op jit(solution)/shard_map/convert_element_type | solution.py:174
  37.5 1.3 %collective-permute-start.7 = (bf16[128,1024]{1,0:T(8,128)(2,1)S(1)}, bf16[128,1024]{1,0:T(8,128)(2,1)S(1)}, u32[]{:S(2)}, u32[]{:S(2)}) collective-permute-start(bf16[128,1024]{1,0:T(8,128)(2,1)S(1)} %add_convert_fusion.1), channel_id=1, source_target_pairs={{2,1},{3,0},{4,3},{5,2},{6,5},{7,4},{10,9},{11,8},{12,11},{13,10},... | collective-permute-start | bytes 786440 | tf_op jit(solution)/shard_map/ppermute | solution.py:25
  38.8 10.7 %collective-permute-done.5 = bf16[128,1024]{1,0:T(8,128)(2,1)S(1)} collective-permute-done((bf16[128,1024]{1,0:T(8,128)(2,1)}, bf16[128,1024]{1,0:T(8,128)(2,1)S(1)}, u32[]{:S(2)}, u32[]{:S(2)}) %collective-permute-start.5) | collective-permute-done | bytes 262176 | tf_op jit(solution)/shard_map/ppermute | solution.py:25
  49.4 1.6 %collective-permute-done.7 = bf16[128,1024]{1,0:T(8,128)(2,1)S(1)} collective-permute-done((bf16[128,1024]{1,0:T(8,128)(2,1)S(1)}, bf16[128,1024]{1,0:T(8,128)(2,1)S(1)}, u32[]{:S(2)}, u32[]{:S(2)}) %collective-permute-start.7) | collective-permute-done | bytes 262176 | tf_op jit(solution)/shard_map/ppermute | solution.py:25
  51.0 0.0 copy-done
  51.0 0.8 %fusion = bf16[1,128,1024]{2,1,0:T(8,128)(2,1)} fusion(bf16[128,1024]{1,0:T(8,128)(2,1)S(1)} %collective-permute-done.7, f32[128,1024]{1,0:T(8,128)S(1)} %copy-done, bf16[128,1024]{1,0:T(8,128)(2,1)S(1)} %collective-permute-done.5), kind=kLoop, calls=%fused_computation.2 | loop fusion | flops 655360 | bytes 1310720 | tf_op jit(solution)/shard_map/broadcast_in_dim | solution.py:176
Async XLA Ops:
  0.6 11.4 %copy-start.4 = (s32[2]{0:T(128)S(1)}, s32[2]{0:T(128)}, u32[]{:S(2)}) copy-start(s32[2]{0:T(128)} %param.7) | copy-start | bytes 28
  0.6 11.0 %collective-permute-start.2 = (bf16[128,1024]{1,0:T(8,128)(2,1)}, bf16[128,1024]{1,0:T(8,128)(2,1)S(1)}, u32[]{:S(2)}, u32[]{:S(2)}) collective-permute-start(bf16[128,1024]{1,0:T(8,128)(2,1)} %bitcast.8), channel_id=1, source_target_pairs={{0,3},{1,2},{2,5},{3,4},{4,7},{5,6},{8,11},{9,10},{10,13},{11,12},... | collective-permute-start | bytes 786440 | tf_op jit(solution)/shard_map/ppermute | solution.py:25
  5.2 12.4 %collective-permute-start.4 = (bf16[128,1024]{1,0:T(8,128)(2,1)}, bf16[128,1024]{1,0:T(8,128)(2,1)S(1)}, u32[]{:S(2)}, u32[]{:S(2)}) collective-permute-start(bf16[128,1024]{1,0:T(8,128)(2,1)} %bitcast.9), channel_id=1, source_target_pairs={{0,1},{1,4},{2,3},{3,6},{4,5},{6,7},{8,9},{9,12},{10,11},{11,14},{... | collective-permute-start | bytes 786440 | tf_op jit(solution)/shard_map/ppermute | solution.py:25
  11.6 6.0 %copy-start.1 = (bf16[128,1024]{1,0:T(8,128)(2,1)}, bf16[128,1024]{1,0:T(8,128)(2,1)S(1)}, u32[]{:S(2)}) copy-start(bf16[128,1024]{1,0:T(8,128)(2,1)S(1)} %collective-permute-done.2.kv1_ref) | copy-start | bytes 786436
  11.6 6.0 %collective-permute-start.3 = (bf16[128,1024]{1,0:T(8,128)(2,1)S(1)}, bf16[128,1024]{1,0:T(8,128)(2,1)S(1)}, u32[]{:S(2)}, u32[]{:S(2)}) collective-permute-start(bf16[128,1024]{1,0:T(8,128)(2,1)S(1)} %collective-permute-done.2.kv1_ref), channel_id=1, source_target_pairs={{0,1},{1,0},{2,3},{3,2},{4,5},{5,4},{6,7},{7,6},{8,9},{9,8},{10,11... | collective-permute-start | bytes 786440 | tf_op jit(solution)/shard_map/ppermute | solution.py:25
  12.1 2.4 %collective-permute-start = (s32[2]{0:T(128)S(1)}, s32[2]{0:T(128)S(1)}, u32[]{:S(2)}, u32[]{:S(2)}) collective-permute-start(s32[2]{0:T(128)S(1)} %copy-done.4), channel_id=1, source_target_pairs={{0,8},{8,0},{16,24},{24,16},{1,9},{9,1},{17,25},{25,17},{2,10},{10... | collective-permute-start | bytes 32 | tf_op jit(solution)/shard_map/ppermute | solution.py:52
  14.6 2.4 %collective-permute-start.1 = (s32[4]{0:T(128)S(1)}, s32[4]{0:T(128)S(1)}, u32[]{:S(2)}, u32[]{:S(2)}) collective-permute-start(s32[4]{0:T(128)S(1)} %pad_add_fusion), channel_id=1, source_target_pairs={{0,16},{8,24},{16,0},{24,8},{1,17},{9,25},{17,1},{25,9},{2,18},{10... | collective-permute-start | bytes 56 | tf_op jit(solution)/shard_map/ppermute | solution.py:52
  17.6 0.7 %copy-start.2 = (bf16[128,1024]{1,0:T(8,128)(2,1)}, bf16[128,1024]{1,0:T(8,128)(2,1)S(1)}, u32[]{:S(2)}) copy-start(bf16[128,1024]{1,0:T(8,128)(2,1)S(1)} %collective-permute-done.4.kv3_ref) | copy-start | bytes 786436
  17.7 0.8 %copy-start.3 = (bf16[128,1024]{1,0:T(8,128)(2,1)}, bf16[128,1024]{1,0:T(8,128)(2,1)S(1)}, u32[]{:S(2)}) copy-start(bf16[128,1024]{1,0:T(8,128)(2,1)S(1)} %collective-permute-done.3.kv2_ref) | copy-start | bytes 786436
  31.9 19.1 %copy-start = (f32[128,1024]{1,0:T(8,128)S(1)}, f32[128,1024]{1,0:T(8,128)}, u32[]{:S(2)}) copy-start(f32[128,1024]{1,0:T(8,128)} %get-tuple-element.8) | copy-start | bytes 1572868
  31.9 4.5 %collective-permute-start.6 = (bf16[128,1024]{1,0:T(8,128)(2,1)}, bf16[128,1024]{1,0:T(8,128)(2,1)S(1)}, u32[]{:S(2)}, u32[]{:S(2)}) collective-permute-start(bf16[128,1024]{1,0:T(8,128)(2,1)} %get-tuple-element.11), channel_id=1, source_target_pairs={{0,1},{1,0},{2,3},{3,2},{4,5},{5,4},{6,7},{7,6},{8,9},{9,8},{10,11... | collective-permute-start | bytes 786440 | tf_op jit(solution)/shard_map/ppermute | solution.py:25
  34.4 15.1 %collective-permute-start.5 = (bf16[128,1024]{1,0:T(8,128)(2,1)}, bf16[128,1024]{1,0:T(8,128)(2,1)S(1)}, u32[]{:S(2)}, u32[]{:S(2)}) collective-permute-start(bf16[128,1024]{1,0:T(8,128)(2,1)} %get-tuple-element.9), channel_id=1, source_target_pairs={{1,0},{3,2},{4,1},{5,4},{6,3},{7,6},{9,8},{11,10},{12,9},{13,12},{... | collective-permute-start | bytes 786440 | tf_op jit(solution)/shard_map/ppermute | solution.py:25
  37.5 13.5 %collective-permute-start.7 = (bf16[128,1024]{1,0:T(8,128)(2,1)S(1)}, bf16[128,1024]{1,0:T(8,128)(2,1)S(1)}, u32[]{:S(2)}, u32[]{:S(2)}) collective-permute-start(bf16[128,1024]{1,0:T(8,128)(2,1)S(1)} %add_convert_fusion.1), channel_id=1, source_target_pairs={{2,1},{3,0},{4,3},{5,2},{6,5},{7,4},{10,9},{11,8},{12,11},{13,10},... | collective-permute-start | bytes 786440 | tf_op jit(solution)/shard_map/ppermute | solution.py:25

commit v2 on v1

v2 whole, which is shorter than its diff:
```python
import functools
import math

import jax
import jax.numpy as jnp
from jax import lax
from jax.experimental import pallas as pl
from jax.experimental.pallas import tpu as pltpu
from jax.sharding import PartitionSpec as P


HQ = 32
HK = 4
HD = 128
REACH = 3
GROUP = HQ // HK
F32 = jnp.float32
BF16 = jnp.bfloat16
NT = (((1,), (1,)), ((), ()))
NN = (((1,), (0,)), ((), ()))
SCALE = 1.0 / math.sqrt(HD)
RATE = SCALE * math.log2(math.e)
PAIRS = HQ // 2


def moved(value, target_of):
    count = lax.axis_size("ctx")
    pairs = [(i, target_of(i)) for i in range(count)]
    return lax.ppermute(value, "ctx", [(s, t) for s, t in pairs if 0 <= t < count])


def one_three(value):
    return moved(value, lambda i: i + 1 if i % 2 else i + 3)


def one_three_back(value):
    return moved(value, lambda i: i - 3 if i % 2 else i - 1)


def three_one(value):
    return moved(value, lambda i: i + 3 if i % 2 else i + 1)


def three_one_back(value):
    return moved(value, lambda i: i - 1 if i % 2 else i - 3)


def swapped(value):
    return moved(value, lambda i: i ^ 1)


def all_lengths_by_xor(lengths):
    count = lax.axis_size("pipe")
    stride = 1
    while stride < count:
        other = lax.ppermute(lengths, "pipe", [(i, i ^ stride) for i in range(count)])
        lengths = jnp.concatenate([lengths, other])
        stride *= 2
    return lengths


def fill_bias(per_pipe, lens_ref, bias_scr, offsets, rows):
    here = lax.axis_index("ctx")
    pipe = lax.axis_index("pipe")
    t_pos = here * rows + lax.broadcasted_iota(jnp.int32, (1, rows), 1)

    def step(d, carry):
        start, doc_start = carry
        slot = ((d // per_pipe) ^ pipe) * per_pipe + d % per_pipe
        doc_start = jnp.where(t_pos >= start, start, doc_start)
        return start + lens_ref[slot], doc_start

    _, doc_start = lax.fori_loop(
        0, lens_ref.shape[0], step, (jnp.int32(0), jnp.zeros((1, rows), jnp.int32))
    )
    for b, offset in enumerate(offsets):
        u_pos = (here - offset) * rows + lax.broadcasted_iota(jnp.int32, (rows, rows), 0)
        ok = (u_pos >= doc_start) & (u_pos <= t_pos)
        bias_scr[b * rows:(b + 1) * rows] = jnp.where(ok, 0.0, -1e30).astype(F32)


def offsets_of_moved():
    odd = lax.rem(lax.axis_index("ctx"), 2)
    return (1 + 2 * odd, 2, 3 - 2 * odd)


def at(i, width):
    return pl.ds(pl.multiple_of(i * width, width), width)


def stacked(ref, i):
    return jnp.concatenate([ref[:, at(2 * i, HD)], ref[:, at(2 * i + 1, HD)]], axis=0)


def tall(refs, column):
    return jnp.concatenate([ref[:, at(column, HD)] for ref in refs], axis=0)


def keys_of(refs, i):
    return tall(refs, i // (GROUP // 2))


def values_of(refs, i):
    return tall(refs, HK + i // (GROUP // 2))


def scores_of(refs, q_ref, bias_scr, i):
    s = lax.dot_general(keys_of(refs, i), stacked(q_ref, i), NT, preferred_element_type=F32)
    bias = bias_scr[...]
    return s + jnp.concatenate([bias, bias], axis=1)


def dweights_of(refs, d_ref, i):
    return lax.dot_general(values_of(refs, i), stacked(d_ref, i), NT, preferred_element_type=F32)


def pipelined(stages, count):
    depth = len(stages)
    for i in range(depth - 1):
        for k in range(i + 1):
            stages[k](i - k)

    def body(i, _):
        for k in range(depth):
            stages[k](i - k)
        return 0

    lax.fori_loop(depth - 1, count, body, 0)
    for i in range(count, count + depth - 1):
        for k in range(i - count + 1, depth):
            stages[k](i - k)


def own_stats_kernel(per_pipe, lens_ref, q_ref, d_ref, kv_ref, stats_ref, bias_scr, s_scr, dp_scr):
    rows = q_ref.shape[0]
    fill_bias(per_pipe, lens_ref, bias_scr, (0,), rows)

    def first(i):
        s_scr[i % 2] = scores_of([kv_ref], q_ref, bias_scr, i)
        dp_scr[i % 2] = dweights_of([kv_ref], d_ref, i)

    def second(i):
        s = s_scr[i % 2]
        top = jnp.max(s, axis=0, keepdims=True)
        p = jnp.exp2((s - top) * RATE)
        column = at(i, 2 * rows)
        stats_ref[0:1, column] = top
        stats_ref[1:2, column] = jnp.sum(p, axis=0, keepdims=True)
        stats_ref[2:3, column] = jnp.sum(p * dp_scr[i % 2], axis=0, keepdims=True)

    pipelined([first, second], PAIRS)


def moved_kernel(per_pipe, lens_ref, q_ref, d_ref, kv1_ref, kv2_ref, kv3_ref, stats_ref,
                 final_ref, g1_ref, g2_ref, g3_ref,
                 bias_scr, s_scr, dp_scr, p_scr, top_scr, acc_scr):
    rows = q_ref.shape[0]
    refs = [kv1_ref, kv2_ref, kv3_ref]
    fill_bias(per_pipe, lens_ref, bias_scr, offsets_of_moved(), rows)
    acc_scr[...] = jnp.zeros_like(acc_scr)

    def first(i):
        s = scores_of(refs, q_ref, bias_scr, i)
        s_scr[i % 2] = s
        own = stats_ref[0:1, at(i, 2 * rows)]
        top_scr[pl.ds(i % 2, 1)] = jnp.maximum(own, jnp.max(s, axis=0, keepdims=True))
        dp_scr[i % 3] = dweights_of(refs, d_ref, i)

    def second(i):
        column = at(i, 2 * rows)
        top = top_scr[pl.ds(i % 2, 1)]
        p = jnp.exp2((s_scr[i % 2] - top) * RATE)
        p_scr[i % 2] = p
        own = jnp.exp2((stats_ref[0:1, column] - top) * RATE)
        total = stats_ref[1:2, column] * own + jnp.sum(p, axis=0, keepdims=True)
        dot = stats_ref[2:3, column] * own + jnp.sum(p * dp_scr[i % 3], axis=0, keepdims=True)
        inv = 1.0 / total
        final_ref[0:1, column] = top
        final_ref[1:2, column] = inv
        final_ref[2:3, column] = dot * inv

    def third(i):
        column = at(i, 2 * rows)
        w = p_scr[i % 2] * final_ref[1:2, column]
        ds = (w * (dp_scr[i % 3] - final_ref[2:3, column])).astype(BF16)
        group = i // (GROUP // 2)
        acc_scr[:, at(group, HD)] += lax.dot_general(
            ds, stacked(q_ref, i), NN, preferred_element_type=F32
        )
        acc_scr[:, at(HK + group, HD)] += lax.dot_general(
            w.astype(BF16), stacked(d_ref, i), NN, preferred_element_type=F32
        )

    pipelined([first, second, third], PAIRS)
    for b, g_ref in enumerate((g1_ref, g2_ref, g3_ref)):
        part = slice(b * rows, (b + 1) * rows)
        g_ref[:, :HK * HD] = (acc_scr[part, :HK * HD] * SCALE).astype(BF16)
        g_ref[:, HK * HD:] = acc_scr[part, HK * HD:].astype(BF16)


def query_kernel(per_pipe, lens_ref, q_ref, d_ref, kv0_ref, kv1_ref, kv2_ref, kv3_ref, final_ref,
                 dq_ref, own_ref, bias_scr, kt_scr, s_scr, dp_scr, ds_scr, w_scr):
    rows = q_ref.shape[0]
    refs = [kv0_ref, kv1_ref, kv2_ref, kv3_ref]
    fill_bias(per_pipe, lens_ref, bias_scr, (0,) + offsets_of_moved(), rows)
    own_ref[...] = jnp.zeros_like(own_ref)
    for group in range(HK):
        for b, ref in enumerate(refs):
            kt_scr[group, :, b * rows:(b + 1) * rows] = ref[:, group * HD:(group + 1) * HD].T

    def first(i):
        s_scr[i % 2] = scores_of(refs, q_ref, bias_scr, i)
        dp_scr[i % 2] = dweights_of(refs, d_ref, i)

    def second(i):
        column = at(i, 2 * rows)
        p = jnp.exp2((s_scr[i % 2] - final_ref[0:1, column]) * RATE)
        w = p * final_ref[1:2, column]
        ds_scr[i % 2] = (w * (dp_scr[i % 2] - final_ref[2:3, column])).astype(BF16)
        w_scr[i % 2] = w[:rows].astype(BF16)

    def third(i):
        group = i // (GROUP // 2)
        own_ref[:, at(group, HD)] += SCALE * lax.dot_general(
            ds_scr[i % 2, :rows], stacked(q_ref, i), NN, preferred_element_type=F32
        )
        own_ref[:, at(HK + group, HD)] += lax.dot_general(
            w_scr[i % 2], stacked(d_ref, i), NN, preferred_element_type=F32
        )
        dqt = lax.dot_general(kt_scr[group], ds_scr[i % 2], NN, preferred_element_type=F32)
        dq = (dqt * SCALE).astype(BF16).T
        dq_ref[:, at(2 * i, HD)] = dq[:rows]
        dq_ref[:, at(2 * i + 1, HD)] = dq[rows:]

    pipelined([first, second, third], PAIRS)


def call(body, per_pipe, args, outs, scratch, matmul_rows):
    specs = [pl.BlockSpec(memory_space=pltpu.SMEM)]
    specs += [pl.BlockSpec(memory_space=pltpu.VMEM)] * (len(args) - 1)
    return pl.pallas_call(
        functools.partial(body, per_pipe),
        in_specs=specs,
        out_specs=[pl.BlockSpec(memory_space=pltpu.VMEM)] * len(outs),
        out_shape=outs,
        scratch_shapes=scratch,
        cost_estimate=pl.CostEstimate(
            flops=2 * HQ * HD * HD * matmul_rows,
            bytes_accessed=sum(x.size * x.dtype.itemsize for x in list(args) + list(outs)),
            transcendentals=0,
        ),
    )(*args)


def on_device(queries, keys_values, out_grads, doc_lengths):
    kv, q, dout = keys_values[0], queries[0], out_grads[0]
    rows, wide = kv.shape
    per_pipe = doc_lengths.shape[0]
    array = jax.ShapeDtypeStruct
    stat = array((8, HQ * rows), F32)
    blocks = REACH * rows
    keys = blocks + rows
    near = one_three(kv)
    far = three_one(kv)
    lens = all_lengths_by_xor(doc_lengths)
    (stats,) = call(
        own_stats_kernel, per_pipe, (lens, q, dout, kv), [stat],
        [pltpu.VMEM((rows, rows), F32)] + [pltpu.VMEM((2, rows, 2 * rows), F32)] * 2,
        2 * rows,
    )
    side = swapped(near)
    final, g_near, g_side, g_far = call(
        moved_kernel, per_pipe, (lens, q, dout, near, side, far, stats),
        [stat] + [array((rows, wide), BF16)] * 3,
        [
            pltpu.VMEM((blocks, rows), F32),
            pltpu.VMEM((2, blocks, 2 * rows), F32),
            pltpu.VMEM((3, blocks, 2 * rows), F32),
            pltpu.VMEM((2, blocks, 2 * rows), F32),
            pltpu.VMEM((2, 2 * rows), F32),
            pltpu.VMEM((blocks, wide), F32),
        ],
        4 * blocks,
    )
    back = three_one_back(g_far)
    side_back = swapped(g_side)
    joined = (g_near.astype(F32) + side_back.astype(F32)).astype(BF16)
    near_back = one_three_back(joined)
    dq, own = call(
        query_kernel, per_pipe, (lens, q, dout, kv, near, side, far, final),
        [array(q.shape, BF16), array((rows, wide), F32)],
        [
            pltpu.VMEM((keys, rows), F32),
            pltpu.VMEM((HK, HD, keys), BF16),
            pltpu.VMEM((2, keys, 2 * rows), F32),
            pltpu.VMEM((2, keys, 2 * rows), F32),
            pltpu.VMEM((2, keys, 2 * rows), BF16),
            pltpu.VMEM((2, rows, 2 * rows), BF16),
        ],
        4 * keys,
    )
    total = own + back.astype(F32) + near_back.astype(F32)
    return (dq[None], total.astype(BF16)[None])


def solution(mesh):
    spec = P("pipe", "ctx", None)
    return jax.shard_map(
        on_device,
        mesh=mesh,
        in_specs=(spec, spec, spec, P("pipe")),
        out_specs=(spec, spec),
        check_vma=False,
    )
```

time: 52.7 us -> 66.9 us (1.27)
  the two profiles are of different devices: /device:TPU:1 before, /device:TPU:29 now
where the time goes in v2:
time: 66.9 us; the launch traced here: 66.6 us
  Pallas kernels  35.7 us (53%)
  starting transfers between devices  13.2 us (20%)
  waiting for transfers between devices  12.1 us (18%)
  other arithmetic  3.54 us (5%)
  local copies, waits for them, and re-layouts  1.41 us (2%)
  between operations  0.71 us (1%)
    pallas_call x3, Pallas kernels, call(): pl.pallas_call(functools.partial(body, per_pipe), in_specs=specs, out_spe...  35.7 us
    ppermute x6, starting transfers between devices, moved(): lax.ppermute(value, 'ctx', [(s, t) for s, t in pairs if 0 <= t < count])  11.8 us
    ppermute x6, waiting for transfers between devices, moved(): lax.ppermute(value, 'ctx', [(s, t) for s, t in pairs if 0 <= t < count])  8.39 us
    ppermute x2, waiting for transfers between devices, all_lengths_by_xor(): lax.ppermute(lengths, 'pipe', [(i, i ^ stride) for i in range(count)])  3.7 us
    broadcast_in_dim x1, other arithmetic, on_device(): return (dq[None], total.astype(BF16)[None])  1.84 us
    ppermute x2, starting transfers between devices, all_lengths_by_xor(): lax.ppermute(lengths, 'pipe', [(i, i ^ stride) for i in range(count)])  1.44 us
    unnamed x8, local copies, waits for them, and re-layouts  1.41 us
  transfers between devices with their start and end apart: 8, of which 3 were waited for; matrix products, arithmetic and copies ran while one was open for 3% of the time, Pallas kernels for 33%

profile of v2, /device:TPU:29, one launch (start us, length us, event | category | flops | bytes accessed | tf_op | source)
XLA Modules:
  0.0 66.6 jit_solution(786983954716897534)
XLA Ops:
  0.6 0.0 copy-start
  0.6 1.3 %collective-permute-start.2 = (bf16[128,1024]{1,0:T(8,128)(2,1)}, bf16[128,1024]{1,0:T(8,128)(2,1)S(1)}, u32[]{:S(2)}, u32[]{:S(2)}) collective-permute-start(bf16[128,1024]{1,0:T(8,128)(2,1)} %bitcast.12), channel_id=1, source_target_pairs={{0,3},{1,2},{2,5},{3,4},{4,7},{5,6},{8,11},{9,10},{10,13},{11,12},... | collective-permute-start | bytes 786440 | tf_op jit(solution)/shard_map/ppermute | solution.py:29
  1.9 1.3 %collective-permute-start.4 = (bf16[128,1024]{1,0:T(8,128)(2,1)}, bf16[128,1024]{1,0:T(8,128)(2,1)S(1)}, u32[]{:S(2)}, u32[]{:S(2)}) collective-permute-start(bf16[128,1024]{1,0:T(8,128)(2,1)} %bitcast.13), channel_id=1, source_target_pairs={{0,1},{1,4},{2,3},{3,6},{4,5},{6,7},{8,9},{9,12},{10,11},{11,14},{... | collective-permute-start | bytes 786440 | tf_op jit(solution)/shard_map/ppermute | solution.py:29
  3.2 8.4 %collective-permute-done.2.kv1_ref = bf16[128,1024]{1,0:T(8,128)(2,1)S(1)} collective-permute-done((bf16[128,1024]{1,0:T(8,128)(2,1)}, bf16[128,1024]{1,0:T(8,128)(2,1)S(1)}, u32[]{:S(2)}, u32[]{:S(2)}) %collective-permute-start.2) | collective-permute-done | bytes 262176 | tf_op jit(solution)/shard_map/ppermute | solution.py:29
  11.6 0.0 copy-start.1
  11.6 0.4 collective-permute-start.3
  12.0 0.0 copy-done
  12.0 1.2 %collective-permute-start = (s32[2]{0:T(128)S(1)}, s32[2]{0:T(128)S(1)}, u32[]{:S(2)}, u32[]{:S(2)}) collective-permute-start(s32[2]{0:T(128)S(1)} %copy-done), channel_id=1, source_target_pairs={{0,8},{8,0},{16,24},{24,16},{1,9},{9,1},{17,25},{25,17},{2,10},{10... | collective-permute-start | bytes 32 | tf_op jit(solution)/shard_map/ppermute | solution.py:56
  13.2 1.5 %collective-permute-done = s32[2]{0:T(128)S(1)} collective-permute-done((s32[2]{0:T(128)S(1)}, s32[2]{0:T(128)S(1)}, u32[]{:S(2)}, u32[]{:S(2)}) %collective-permute-start) | collective-permute-done | bytes 40 | tf_op jit(solution)/shard_map/ppermute | solution.py:56
  14.7 0.1 pad_add_fusion
  14.8 0.2 collective-permute-start.1
  15.0 2.2 %collective-permute-done.1 = s32[4]{0:T(128)S(1)} collective-permute-done((s32[4]{0:T(128)S(1)}, s32[4]{0:T(128)S(1)}, u32[]{:S(2)}, u32[]{:S(2)}) %collective-permute-start.1) | collective-permute-done | bytes 48 | tf_op jit(solution)/shard_map/ppermute | solution.py:56
  17.2 0.6 pad_add_fusion.1.lens_ref
  17.8 6.4 %shard_map.59.stats_ref = f32[8,4096]{1,0:T(8,128)} custom-call(s32[8]{0:T(128)} %pad_add_fusion.1.lens_ref, bf16[128,4096]{1,0:T(8,128)(2,1)} %bitcast.6, bf16[128,4096]{1,0:T(8,128)(2,1)} %bitcast.9, bf16[128,1024]{1,0:T(8,128)(2,1)} %bitcast.14), custom_call_target="tpu_custom_call" | custom-call | flops 268435456 | bytes 2490400 | tf_op jit(solution)/shard_map/pallas_call | solution.py:241
  24.2 0.0 copy-done.1
  24.2 0.0 collective-permute-done.4.kv3_ref
  24.2 0.0 copy-start.2
  24.2 0.0 collective-permute-done.3.kv2_ref
  24.2 0.7 %copy-done.2 = bf16[128,1024]{1,0:T(8,128)(2,1)} copy-done((bf16[128,1024]{1,0:T(8,128)(2,1)}, bf16[128,1024]{1,0:T(8,128)(2,1)S(1)}, u32[]{:S(2)}) %copy-start.2) | copy-done | bytes 262168
  24.9 0.0 copy-start.3
  24.9 0.7 %copy-done.3 = bf16[128,1024]{1,0:T(8,128)(2,1)} copy-done((bf16[128,1024]{1,0:T(8,128)(2,1)}, bf16[128,1024]{1,0:T(8,128)(2,1)S(1)}, u32[]{:S(2)}) %copy-start.3) | copy-done | bytes 262168
  25.6 13.5 %shard_map.60 = (f32[8,4096]{1,0:T(8,128)}, bf16[128,1024]{1,0:T(8,128)(2,1)}, bf16[128,1024]{1,0:T(8,128)(2,1)}, bf16[128,1024]{1,0:T(8,128)(2,1)}) custom-call(s32[8]{0:T(128)} %pad_add_fusion.1.lens_ref, bf16[128,4096]{1,0:T(8,128)(2,1)} %bitcast.7, bf16[128,4096]{1,0:T(8,128)(2,1)} %bitcast.10, bf16[128,1024]{1,0:T(8,128)(2,1)} %copy-done.1, ...), custom_call_target="tpu_custom_call" | custom-call | flops 1610612736 | bytes 3932192 | tf_op jit(solution)/shard_map/pallas_call | solution.py:241
  39.1 2.1 %collective-permute-start.6 = (bf16[128,1024]{1,0:T(8,128)(2,1)}, bf16[128,1024]{1,0:T(8,128)(2,1)S(1)}, u32[]{:S(2)}, u32[]{:S(2)}) collective-permute-start(bf16[128,1024]{1,0:T(8,128)(2,1)} %get-tuple-element.13), channel_id=1, source_target_pairs={{0,1},{1,0},{2,3},{3,2},{4,5},{5,4},{6,7},{7,6},{8,9},{9,8},{10,11... | collective-permute-start | bytes 786440 | tf_op jit(solution)/shard_map/ppermute | solution.py:29
  41.3 1.9 %collective-permute-start.5 = (bf16[128,1024]{1,0:T(8,128)(2,1)}, bf16[128,1024]{1,0:T(8,128)(2,1)S(1)}, u32[]{:S(2)}, u32[]{:S(2)}) collective-permute-start(bf16[128,1024]{1,0:T(8,128)(2,1)} %get-tuple-element.11), channel_id=1, source_target_pairs={{1,0},{3,2},{4,1},{5,4},{6,3},{7,6},{9,8},{11,10},{12,9},{13,12},{... | collective-permute-start | bytes 786440 | tf_op jit(solution)/shard_map/ppermute | solution.py:29
  43.2 0.0 collective-permute-done.6
  43.2 1.0 %add_convert_fusion.1 = bf16[128,1024]{1,0:T(8,128)(2,1)S(1)} fusion(bf16[128,1024]{1,0:T(8,128)(2,1)S(1)} %collective-permute-done.6, bf16[128,1024]{1,0:T(8,128)(2,1)} %get-tuple-element.12), kind=kLoop, calls=%fused_computation.1 | loop fusion | flops 524288 | bytes 786432 | tf_op jit(solution)/shard_map/convert_element_type | solution.py:287
  44.2 4.7 %collective-permute-start.7 = (bf16[128,1024]{1,0:T(8,128)(2,1)S(1)}, bf16[128,1024]{1,0:T(8,128)(2,1)S(1)}, u32[]{:S(2)}, u32[]{:S(2)}) collective-permute-start(bf16[128,1024]{1,0:T(8,128)(2,1)S(1)} %add_convert_fusion.1), channel_id=1, source_target_pairs={{2,1},{3,0},{4,3},{5,2},{6,5},{7,4},{10,9},{11,8},{12,11},{13,10},... | collective-permute-start | bytes 786440 | tf_op jit(solution)/shard_map/ppermute | solution.py:29
  49.0 15.8 %shard_map.61 = (bf16[128,4096]{1,0:T(8,128)(2,1)}, f32[128,1024]{1,0:T(8,128)}) custom-call(s32[8]{0:T(128)} %pad_add_fusion.1.lens_ref, bf16[128,4096]{1,0:T(8,128)(2,1)} %bitcast.8, bf16[128,4096]{1,0:T(8,128)(2,1)} %bitcast.11, bf16[128,1024]{1,0:T(8,128)(2,1)} %bitcast.15, bf16[128,1024]{1,0:T(8,128)(2,1)} %copy-done.1, bf16[128,1024]{1,0:T(8,128)(2,1)} %copy-done.3, ...), custom_call_target="tpu_custom_call" | custom-call | flops 2147483648 | bytes 4849696 | tf_op jit(solution)/shard_map/pallas_call | solution.py:241
  64.7 0.0 collective-permute-done.5
  64.7 0.0 collective-permute-done.7
  64.7 1.8 %fusion = bf16[1,128,1024]{2,1,0:T(8,128)(2,1)} fusion(bf16[128,1024]{1,0:T(8,128)(2,1)S(1)} %collective-permute-done.7, f32[128,1024]{1,0:T(8,128)} %get-tuple-element.10, bf16[128,1024]{1,0:T(8,128)(2,1)S(1)} %collective-permute-done.5), kind=kLoop, calls=%fused_computation.2 | loop fusion | flops 655360 | bytes 1310720 | tf_op jit(solution)/shard_map/broadcast_in_dim | solution.py:303
Async XLA Ops:
  0.6 11.4 %copy-start = (s32[2]{0:T(128)S(1)}, s32[2]{0:T(128)}, u32[]{:S(2)}) copy-start(s32[2]{0:T(128)} %param.7) | copy-start | bytes 28
  0.6 11.0 %collective-permute-start.2 = (bf16[128,1024]{1,0:T(8,128)(2,1)}, bf16[128,1024]{1,0:T(8,128)(2,1)S(1)}, u32[]{:S(2)}, u32[]{:S(2)}) collective-permute-start(bf16[128,1024]{1,0:T(8,128)(2,1)} %bitcast.12), channel_id=1, source_target_pairs={{0,3},{1,2},{2,5},{3,4},{4,7},{5,6},{8,11},{9,10},{10,13},{11,12},... | collective-permute-start | bytes 786440 | tf_op jit(solution)/shard_map/ppermute | solution.py:29
  1.9 22.3 %collective-permute-start.4 = (bf16[128,1024]{1,0:T(8,128)(2,1)}, bf16[128,1024]{1,0:T(8,128)(2,1)S(1)}, u32[]{:S(2)}, u32[]{:S(2)}) collective-permute-start(bf16[128,1024]{1,0:T(8,128)(2,1)} %bitcast.13), channel_id=1, source_target_pairs={{0,1},{1,4},{2,3},{3,6},{4,5},{6,7},{8,9},{9,12},{10,11},{11,14},{... | collective-permute-start | bytes 786440 | tf_op jit(solution)/shard_map/ppermute | solution.py:29
  11.6 12.6 %copy-start.1 = (bf16[128,1024]{1,0:T(8,128)(2,1)}, bf16[128,1024]{1,0:T(8,128)(2,1)S(1)}, u32[]{:S(2)}) copy-start(bf16[128,1024]{1,0:T(8,128)(2,1)S(1)} %collective-permute-done.2.kv1_ref) | copy-start | bytes 786436
  11.6 12.6 %collective-permute-start.3 = (bf16[128,1024]{1,0:T(8,128)(2,1)S(1)}, bf16[128,1024]{1,0:T(8,128)(2,1)S(1)}, u32[]{:S(2)}, u32[]{:S(2)}) collective-permute-start(bf16[128,1024]{1,0:T(8,128)(2,1)S(1)} %collective-permute-done.2.kv1_ref), channel_id=1, source_target_pairs={{0,1},{1,0},{2,3},{3,2},{4,5},{5,4},{6,7},{7,6},{8,9},{9,8},{10,11... | collective-permute-start | bytes 786440 | tf_op jit(solution)/shard_map/ppermute | solution.py:29
  12.0 2.7 %collective-permute-start = (s32[2]{0:T(128)S(1)}, s32[2]{0:T(128)S(1)}, u32[]{:S(2)}, u32[]{:S(2)}) collective-permute-start(s32[2]{0:T(128)S(1)} %copy-done), channel_id=1, source_target_pairs={{0,8},{8,0},{16,24},{24,16},{1,9},{9,1},{17,25},{25,17},{2,10},{10... | collective-permute-start | bytes 32 | tf_op jit(solution)/shard_map/ppermute | solution.py:56
  14.8 2.4 %collective-permute-start.1 = (s32[4]{0:T(128)S(1)}, s32[4]{0:T(128)S(1)}, u32[]{:S(2)}, u32[]{:S(2)}) collective-permute-start(s32[4]{0:T(128)S(1)} %pad_add_fusion), channel_id=1, source_target_pairs={{0,16},{8,24},{16,0},{24,8},{1,17},{9,25},{17,1},{25,9},{2,18},{10... | collective-permute-start | bytes 56 | tf_op jit(solution)/shard_map/ppermute | solution.py:56
  24.2 0.7 %copy-start.2 = (bf16[128,1024]{1,0:T(8,128)(2,1)}, bf16[128,1024]{1,0:T(8,128)(2,1)S(1)}, u32[]{:S(2)}) copy-start(bf16[128,1024]{1,0:T(8,128)(2,1)S(1)} %collective-permute-done.4.kv3_ref) | copy-start | bytes 786436
  24.9 0.7 %copy-start.3 = (bf16[128,1024]{1,0:T(8,128)(2,1)}, bf16[128,1024]{1,0:T(8,128)(2,1)S(1)}, u32[]{:S(2)}) copy-start(bf16[128,1024]{1,0:T(8,128)(2,1)S(1)} %collective-permute-done.3.kv2_ref) | copy-start | bytes 786436
  39.1 4.0 %collective-permute-start.6 = (bf16[128,1024]{1,0:T(8,128)(2,1)}, bf16[128,1024]{1,0:T(8,128)(2,1)S(1)}, u32[]{:S(2)}, u32[]{:S(2)}) collective-permute-start(bf16[128,1024]{1,0:T(8,128)(2,1)} %get-tuple-element.13), channel_id=1, source_target_pairs={{0,1},{1,0},{2,3},{3,2},{4,5},{5,4},{6,7},{7,6},{8,9},{9,8},{10,11... | collective-permute-start | bytes 786440 | tf_op jit(solution)/shard_map/ppermute | solution.py:29
  41.3 23.5 %collective-permute-start.5 = (bf16[128,1024]{1,0:T(8,128)(2,1)}, bf16[128,1024]{1,0:T(8,128)(2,1)S(1)}, u32[]{:S(2)}, u32[]{:S(2)}) collective-permute-start(bf16[128,1024]{1,0:T(8,128)(2,1)} %get-tuple-element.11), channel_id=1, source_target_pairs={{1,0},{3,2},{4,1},{5,4},{6,3},{7,6},{9,8},{11,10},{12,9},{13,12},{... | collective-permute-start | bytes 786440 | tf_op jit(solution)/shard_map/ppermute | solution.py:29
  44.2 20.5 %collective-permute-start.7 = (bf16[128,1024]{1,0:T(8,128)(2,1)S(1)}, bf16[128,1024]{1,0:T(8,128)(2,1)S(1)}, u32[]{:S(2)}, u32[]{:S(2)}) collective-permute-start(bf16[128,1024]{1,0:T(8,128)(2,1)S(1)} %add_convert_fusion.1), channel_id=1, source_target_pairs={{2,1},{3,0},{4,3},{5,2},{6,5},{7,4},{10,9},{11,8},{12,11},{13,10},... | collective-permute-start | bytes 786440 | tf_op jit(solution)/shard_map/ppermute | solution.py:29

commit v3 on v2

v3 whole, which is shorter than its diff:
```python
import functools
import math

import jax
import jax.numpy as jnp
from jax import lax
from jax.experimental import pallas as pl
from jax.experimental.pallas import tpu as pltpu
from jax.sharding import PartitionSpec as P


HQ = 32
HK = 4
HD = 128
REACH = 3
GROUP = HQ // HK
F32 = jnp.float32
BF16 = jnp.bfloat16
NT = (((1,), (1,)), ((), ()))
NN = (((1,), (0,)), ((), ()))
SCALE = 1.0 / math.sqrt(HD)
PAIRS = HQ // 2
SLOTS = GROUP // 2


def moved(value, target_of):
    count = lax.axis_size("ctx")
    pairs = [(i, target_of(i)) for i in range(count)]
    return lax.ppermute(value, "ctx", [(s, t) for s, t in pairs if 0 <= t < count])


def one_three(value):
    return moved(value, lambda i: i + 1 if i % 2 else i + 3)


def one_three_back(value):
    return moved(value, lambda i: i - 3 if i % 2 else i - 1)


def three_one(value):
    return moved(value, lambda i: i + 3 if i % 2 else i + 1)


def three_one_back(value):
    return moved(value, lambda i: i - 1 if i % 2 else i - 3)


def swapped(value):
    return moved(value, lambda i: i ^ 1)


def all_lengths(lengths):
    count = lax.axis_size("pipe")
    pieces, stride = [lengths], 1
    while stride < count:
        pieces.append(
            lax.ppermute(jnp.concatenate(pieces), "pipe", [(i, i ^ stride) for i in range(count)])
        )
        stride *= 2
    return pieces


def fill_bias(lens_refs, starts_scr, bias_scr, offsets, rows):
    here = lax.axis_index("ctx")
    pipe = lax.axis_index("pipe")
    t_pos = here * rows + lax.broadcasted_iota(jnp.int32, (1, rows), 1)
    per_pipe = lens_refs[0].shape[0]
    place = 0
    for ref in lens_refs:
        for k in range(ref.shape[0]):
            starts_scr[((place // per_pipe) ^ pipe) * per_pipe + place % per_pipe] = ref[k]
            place += 1

    def step(d, carry):
        start, doc_start = carry
        doc_start = jnp.where(t_pos >= start, start, doc_start)
        return start + starts_scr[d], doc_start

    _, doc_start = lax.fori_loop(0, place, step, (jnp.int32(0), jnp.zeros((1, rows), jnp.int32)))
    for b, offset in enumerate(offsets):
        u_pos = (here - offset) * rows + lax.broadcasted_iota(jnp.int32, (rows, rows), 0)
        ok = (u_pos >= doc_start) & (u_pos <= t_pos)
        bias_scr[b * rows:(b + 1) * rows] = jnp.where(ok, 0.0, -1e30).astype(F32)


def offsets_of_moved():
    odd = lax.rem(lax.axis_index("ctx"), 2)
    return (1 + 2 * odd, 2, 3 - 2 * odd)


def at(i, width):
    return pl.ds(pl.multiple_of(i * width, width), width)


def stacked(ref, i):
    return jnp.concatenate([ref[:, at(2 * i, HD)], ref[:, at(2 * i + 1, HD)]], axis=0)


def tall(refs, column):
    return jnp.concatenate([ref[:, at(column, HD)] for ref in refs], axis=0)


def keys_of(refs, i):
    return tall(refs, i // (GROUP // 2))


def values_of(refs, i):
    return tall(refs, HK + i // (GROUP // 2))


def scores_of(refs, q_ref, bias_scr, i):
    s = lax.dot_general(keys_of(refs, i), stacked(q_ref, i), NT, preferred_element_type=F32)
    bias = bias_scr[...]
    return s + jnp.concatenate([bias, bias], axis=1)


def dweights_of(refs, d_ref, i):
    return lax.dot_general(values_of(refs, i), stacked(d_ref, i), NT, preferred_element_type=F32)


def pipelined(stages):
    depth = len(stages)

    def steps(base, count, first, last):
        for j in range(count):
            for k in range(depth):
                if first <= j - k < last:
                    stages[k](base + (j - k), (j - k) % SLOTS)

    steps(0, SLOTS, 0, SLOTS)

    def body(trip, _):
        steps(trip * SLOTS, SLOTS, -SLOTS, SLOTS)
        return 0

    lax.fori_loop(1, PAIRS // SLOTS, body, 0)
    steps(PAIRS, depth - 1, -SLOTS, 0)


def own_stats_kernel(n_lens, *refs):
    lens_refs, refs = refs[:n_lens], refs[n_lens:]
    q_ref, d_ref, kv_ref, stats_ref, starts_scr, bias_scr, s_scr, dp_scr = refs
    rows = q_ref.shape[0]
    fill_bias(lens_refs, starts_scr, bias_scr, (0,), rows)

    def first(i, slot):
        s_scr[slot] = scores_of([kv_ref], q_ref, bias_scr, i)
        dp_scr[slot] = dweights_of([kv_ref], d_ref, i)

    def second(i, slot):
        s = s_scr[slot]
        top = jnp.max(s, axis=0, keepdims=True)
        p = jnp.exp((s - top) * SCALE)
        column = at(i, 2 * rows)
        stats_ref[0:1, column] = top
        stats_ref[1:2, column] = jnp.sum(p, axis=0, keepdims=True)
        stats_ref[2:3, column] = jnp.sum(p * dp_scr[slot], axis=0, keepdims=True)

    pipelined([first, second])


def moved_kernel(n_lens, *refs):
    lens_refs, refs = refs[:n_lens], refs[n_lens:]
    q_ref, d_ref, kv1_ref, kv2_ref, kv3_ref, stats_ref = refs[:6]
    final_ref, g1_ref, g2_ref, g3_ref = refs[6:10]
    starts_scr, bias_scr, s_scr, dp_scr, p_scr, row_scr, acc_scr = refs[10:]
    rows = q_ref.shape[0]
    refs = [kv1_ref, kv2_ref, kv3_ref]
    fill_bias(lens_refs, starts_scr, bias_scr, offsets_of_moved(), rows)
    acc_scr[...] = jnp.zeros_like(acc_scr)

    def first(i, slot):
        s = scores_of(refs, q_ref, bias_scr, i)
        s_scr[slot] = s
        own = stats_ref[0:1, at(i, 2 * rows)]
        row_scr[slot, 0:1] = jnp.maximum(own, jnp.max(s, axis=0, keepdims=True))
        dp_scr[slot] = dweights_of(refs, d_ref, i)

    def second(i, slot):
        column = at(i, 2 * rows)
        top = row_scr[slot, 0:1]
        p = jnp.exp((s_scr[slot] - top) * SCALE)
        p_scr[slot] = p
        own = jnp.exp((stats_ref[0:1, column] - top) * SCALE)
        total = stats_ref[1:2, column] * own + jnp.sum(p, axis=0, keepdims=True)
        dot = stats_ref[2:3, column] * own + jnp.sum(p * dp_scr[slot], axis=0, keepdims=True)
        inv = 1.0 / total
        delta = dot * inv
        row_scr[slot, 1:2] = inv
        row_scr[slot, 2:3] = delta
        final_ref[0:1, column] = top
        final_ref[1:2, column] = inv
        final_ref[2:3, column] = delta

    def third(i, slot):
        w = p_scr[slot] * row_scr[slot, 1:2]
        ds = (w * (dp_scr[slot] - row_scr[slot, 2:3])).astype(BF16)
        group = i // SLOTS
        acc_scr[:, at(group, HD)] += lax.dot_general(
            ds, stacked(q_ref, i), NN, preferred_element_type=F32
        )
        acc_scr[:, at(HK + group, HD)] += lax.dot_general(
            w.astype(BF16), stacked(d_ref, i), NN, preferred_element_type=F32
        )

    pipelined([first, second, third])
    for b, g_ref in enumerate((g1_ref, g2_ref, g3_ref)):
        part = slice(b * rows, (b + 1) * rows)
        g_ref[:, :HK * HD] = (acc_scr[part, :HK * HD] * SCALE).astype(BF16)
        g_ref[:, HK * HD:] = acc_scr[part, HK * HD:].astype(BF16)


def query_kernel(n_lens, *refs):
    lens_refs, refs = refs[:n_lens], refs[n_lens:]
    q_ref, d_ref, kv0_ref, kv1_ref, kv2_ref, kv3_ref, final_ref, dq_ref, own_ref = refs[:9]
    starts_scr, bias_scr, kt_scr, s_scr, dp_scr, ds_scr, w_scr = refs[9:]
    rows = q_ref.shape[0]
    refs = [kv0_ref, kv1_ref, kv2_ref, kv3_ref]
    fill_bias(lens_refs, starts_scr, bias_scr, (0,) + offsets_of_moved(), rows)
    own_ref[...] = jnp.zeros_like(own_ref)
    for group in range(HK):
        for b, ref in enumerate(refs):
            kt_scr[group, :, b * rows:(b + 1) * rows] = ref[:, group * HD:(group + 1) * HD].T

    def first(i, slot):
        s_scr[slot] = scores_of(refs, q_ref, bias_scr, i)
        dp_scr[slot] = dweights_of(refs, d_ref, i)

    def second(i, slot):
        column = at(i, 2 * rows)
        p = jnp.exp((s_scr[slot] - final_ref[0:1, column]) * SCALE)
        w = p * final_ref[1:2, column]
        ds_scr[slot] = (w * (dp_scr[slot] - final_ref[2:3, column])).astype(BF16)
        w_scr[slot] = w[:rows].astype(BF16)

    def third(i, slot):
        group = i // SLOTS
        own_ref[:, at(group, HD)] += SCALE * lax.dot_general(
            ds_scr[slot, :rows], stacked(q_ref, i), NN, preferred_element_type=F32
        )
        own_ref[:, at(HK + group, HD)] += lax.dot_general(
            w_scr[slot], stacked(d_ref, i), NN, preferred_element_type=F32
        )
        dqt = lax.dot_general(kt_scr[group], ds_scr[slot], NN, preferred_element_type=F32)
        dq = (dqt * SCALE).astype(BF16).T
        dq_ref[:, at(2 * i, HD)] = dq[:rows]
        dq_ref[:, at(2 * i + 1, HD)] = dq[rows:]

    pipelined([first, second, third])


def call(body, lens, args, outs, scratch, matmul_rows, grant):
    specs = [pl.BlockSpec(memory_space=pltpu.SMEM)] * len(lens)
    specs += [pl.BlockSpec(memory_space=pltpu.VMEM)] * len(args)
    docs = sum(x.shape[0] for x in lens)
    return pl.pallas_call(
        functools.partial(body, len(lens)),
        in_specs=specs,
        out_specs=[pl.BlockSpec(memory_space=pltpu.VMEM)] * len(outs),
        out_shape=outs,
        scratch_shapes=[pltpu.SMEM((docs,), jnp.int32)] + scratch,
        cost_estimate=pl.CostEstimate(
            flops=2 * HQ * HD * HD * matmul_rows,
            bytes_accessed=sum(x.size * x.dtype.itemsize for x in list(args) + list(outs)),
            transcendentals=0,
        ),
        compiler_params=pltpu.CompilerParams(vmem_limit_bytes=grant << 20),
    )(*lens, *args)


def on_device(queries, keys_values, out_grads, doc_lengths):
    kv, q, dout = keys_values[0], queries[0], out_grads[0]
    rows, wide = kv.shape
    array = jax.ShapeDtypeStruct
    stat = array((8, HQ * rows), F32)
    blocks = REACH * rows
    keys = blocks + rows
    near = one_three(kv)
    far = three_one(kv)
    lens = all_lengths(doc_lengths)
    side = swapped(near)
    (stats,) = call(
        own_stats_kernel, lens, (q, dout, kv), [stat],
        [pltpu.VMEM((rows, rows), F32)] + [pltpu.VMEM((SLOTS, rows, 2 * rows), F32)] * 2,
        2 * rows, 8,
    )
    final, g_near, g_side, g_far = call(
        moved_kernel, lens, (q, dout, near, side, far, stats),
        [stat] + [array((rows, wide), BF16)] * 3,
        [pltpu.VMEM((blocks, rows), F32)]
        + [pltpu.VMEM((SLOTS, blocks, 2 * rows), F32)] * 3
        + [pltpu.VMEM((SLOTS, 8, 2 * rows), F32), pltpu.VMEM((blocks, wide), F32)],
        4 * blocks, 20,
    )
    back = three_one_back(g_far)
    side_back = swapped(g_side)
    joined = (g_near.astype(F32) + side_back.astype(F32)).astype(BF16)
    near_back = one_three_back(joined)
    dq, own = call(
        query_kernel, lens, (q, dout, kv, near, side, far, final),
        [array(q.shape, BF16), array((rows, wide), F32)],
        [pltpu.VMEM((keys, rows), F32), pltpu.VMEM((HK, HD, keys), BF16)]
        + [pltpu.VMEM((SLOTS, keys, 2 * rows), F32)] * 2
        + [pltpu.VMEM((SLOTS, keys, 2 * rows), BF16)]
        + [pltpu.VMEM((SLOTS, rows, 2 * rows), BF16)],
        4 * keys, 20,
    )
    total = own + back.astype(F32) + near_back.astype(F32)
    return (dq[None], total.astype(BF16)[None])


def solution(mesh):
    spec = P("pipe", "ctx", None)
    return jax.shard_map(
        on_device,
        mesh=mesh,
        in_specs=(spec, spec, spec, P("pipe")),
        out_specs=(spec, spec),
        check_vma=False,
    )
```

time: 66.9 us -> 51.5 us (0.77)
  the two profiles are of different devices: /device:TPU:29 before, /device:TPU:9 now
where the time goes in v3:
time: 51.5 us; the launch traced here: 51.2 us
  Pallas kernels  18.2 us (35%)
  starting transfers between devices  15.2 us (30%)
  waiting for transfers between devices  12.7 us (25%)
  local copies, waits for them, and re-layouts  3.42 us (7%)
  other arithmetic  0.95 us (2%)
  between operations  0.76 us (1%)
    pallas_call x3, Pallas kernels, call(): pl.pallas_call(functools.partial(body, len(lens)), in_specs=specs, out_sp...  18.2 us
    ppermute x6, starting transfers between devices, moved(): lax.ppermute(value, 'ctx', [(s, t) for s, t in pairs if 0 <= t < count])  12.8 us
    ppermute x6, waiting for transfers between devices, moved(): lax.ppermute(value, 'ctx', [(s, t) for s, t in pairs if 0 <= t < count])  10.3 us
    unnamed x14, local copies, waits for them, and re-layouts  3.42 us
    ppermute x2, starting transfers between devices, all_lengths(): lax.ppermute(jnp.concatenate(pieces), 'pipe', [(i, i ^ stride) for i in r...  2.45 us
    ppermute x2, waiting for transfers between devices, all_lengths(): lax.ppermute(jnp.concatenate(pieces), 'pipe', [(i, i ^ stride) for i in r...  2.39 us
  transfers between devices with their start and end apart: 8, of which 4 were waited for; matrix products, arithmetic and copies ran while one was open for 0% of the time, Pallas kernels for 19%

profile of v3, /device:TPU:9, one launch (start us, length us, event | category | flops | bytes accessed | tf_op | source)
XLA Modules:
  0.0 51.2 jit_solution(12664907010770698150)
XLA Ops:
  0.6 0.0 copy-start.6
  0.6 3.8 %collective-permute-start.2 = (bf16[128,1024]{1,0:T(8,128)(2,1)}, bf16[128,1024]{1,0:T(8,128)(2,1)S(1)}, u32[]{:S(2)}, u32[]{:S(2)}) collective-permute-start(bf16[128,1024]{1,0:T(8,128)(2,1)} %bitcast.12), channel_id=1, source_target_pairs={{0,3},{1,2},{2,5},{3,4},{4,7},{5,6},{8,11},{9,10},{10,13},{11,12},... | collective-permute-start | bytes 786440 | tf_op jit(solution)/shard_map/ppermute | solution.py:29
  4.4 2.3 %collective-permute-start.4 = (bf16[128,1024]{1,0:T(8,128)(2,1)}, bf16[128,1024]{1,0:T(8,128)(2,1)S(1)}, u32[]{:S(2)}, u32[]{:S(2)}) collective-permute-start(bf16[128,1024]{1,0:T(8,128)(2,1)} %bitcast.13), channel_id=1, source_target_pairs={{0,1},{1,4},{2,3},{3,6},{4,5},{6,7},{8,9},{9,12},{10,11},{11,14},{... | collective-permute-start | bytes 786440 | tf_op jit(solution)/shard_map/ppermute | solution.py:29
  6.7 4.9 %collective-permute-done.2.refs_5_.refs_6_ = bf16[128,1024]{1,0:T(8,128)(2,1)S(1)} collective-permute-done((bf16[128,1024]{1,0:T(8,128)(2,1)}, bf16[128,1024]{1,0:T(8,128)(2,1)S(1)}, u32[]{:S(2)}, u32[]{:S(2)}) %collective-permute-start.2) | collective-permute-done | bytes 262176 | tf_op jit(solution)/shard_map/ppermute | solution.py:29
  11.6 0.4 collective-permute-start.3
  12.0 0.0 copy-done.6
  12.0 1.2 %collective-permute-start = (s32[2]{0:T(128)S(1)}, s32[2]{0:T(128)S(1)}, u32[]{:S(2)}, u32[]{:S(2)}) collective-permute-start(s32[2]{0:T(128)S(1)} %copy-done.6), channel_id=1, source_target_pairs={{0,8},{8,0},{16,24},{24,16},{1,9},{9,1},{17,25},{25,17},{2,10},{10... | collective-permute-start | bytes 32 | tf_op jit(solution)/shard_map/ppermute | solution.py:57
  13.2 1.2 %collective-permute-done.refs_1_ = s32[2]{0:T(128)S(1)} collective-permute-done((s32[2]{0:T(128)S(1)}, s32[2]{0:T(128)S(1)}, u32[]{:S(2)}, u32[]{:S(2)}) %collective-permute-start) | collective-permute-done | bytes 40 | tf_op jit(solution)/shard_map/ppermute | solution.py:57
  14.4 0.1 pad_add_fusion
  14.5 1.2 %collective-permute-start.1 = (s32[4]{0:T(128)S(1)}, s32[4]{0:T(128)S(1)}, u32[]{:S(2)}, u32[]{:S(2)}) collective-permute-start(s32[4]{0:T(128)S(1)} %pad_add_fusion), channel_id=1, source_target_pairs={{0,16},{8,24},{16,0},{24,8},{1,17},{9,25},{17,1},{25,9},{2,18},{10... | collective-permute-start | bytes 56 | tf_op jit(solution)/shard_map/ppermute | solution.py:57
  15.8 1.2 %collective-permute-done.1.refs_2_ = s32[4]{0:T(128)S(1)} collective-permute-done((s32[4]{0:T(128)S(1)}, s32[4]{0:T(128)S(1)}, u32[]{:S(2)}, u32[]{:S(2)}) %collective-permute-start.1) | collective-permute-done | bytes 48 | tf_op jit(solution)/shard_map/ppermute | solution.py:57
  16.9 0.0 copy-start
  16.9 1.2 %copy-done = bf16[1,128,4096]{2,1,0:T(8,128)(2,1)S(1)} copy-done((bf16[1,128,4096]{2,1,0:T(8,128)(2,1)S(1)}, bf16[1,128,4096]{2,1,0:T(8,128)(2,1)}, u32[]{:S(2)}) %copy-start) | copy-done | bytes 1048600
  18.2 0.0 copy-start.2
  18.2 1.2 %copy-done.2 = bf16[1,128,4096]{2,1,0:T(8,128)(2,1)S(1)} copy-done((bf16[1,128,4096]{2,1,0:T(8,128)(2,1)S(1)}, bf16[1,128,4096]{2,1,0:T(8,128)(2,1)}, u32[]{:S(2)}) %copy-start.2) | copy-done | bytes 1048600
  19.4 0.0 copy-start.4
  19.4 0.9 %copy-done.4 = bf16[1,128,1024]{2,1,0:T(8,128)(2,1)S(1)} copy-done((bf16[1,128,1024]{2,1,0:T(8,128)(2,1)S(1)}, bf16[1,128,1024]{2,1,0:T(8,128)(2,1)}, u32[]{:S(2)}) %copy-start.4) | copy-done | bytes 262168
  20.3 0.0 copy-start.1
  20.3 0.0 copy-start.3
  20.3 2.2 %shard_map.59.refs_8_ = f32[8,4096]{1,0:T(8,128)S(1)} custom-call(s32[2]{0:T(128)S(1)} %copy-done.6, s32[2]{0:T(128)S(1)} %collective-permute-done.refs_1_, s32[4]{0:T(128)S(1)} %collective-permute-done.1.refs_2_, bf16[128,4096]{1,0:T(8,128)(2,1)S(1)} %bitcast.6, bf16[128,4096]{1,0:T(8,128)(2,1)S(1)} %bitcast.9, bf16[128,1024]{1,0:T(8,128)(2,1)S(1)} %bitcast.14), custom_call_target="tpu_custom_call" | custom-call | flops 268435456 | bytes 2490368 | tf_op jit(solution)/shard_map/pallas_call | solution.py:256
  22.6 0.0 collective-permute-done.4.refs_7_.refs_8_
  22.6 0.0 collective-permute-done.3.refs_6_.refs_7_
  22.6 0.0 copy-done.1
  22.6 0.0 copy-done.3
  22.6 8.3 %shard_map.60 = (f32[8,4096]{1,0:T(8,128)S(1)}, bf16[128,1024]{1,0:T(8,128)(2,1)S(1)}, bf16[128,1024]{1,0:T(8,128)(2,1)S(1)}, bf16[128,1024]{1,0:T(8,128)(2,1)S(1)}) custom-call(s32[2]{0:T(128)S(1)} %copy-done.6, s32[2]{0:T(128)S(1)} %collective-permute-done.refs_1_, s32[4]{0:T(128)S(1)} %collective-permute-done.1.refs_2_, bf16[128,4096]{1,0:T(8,128)(2,1)S(1)} %bitcast.7, ...), custom_call_target="tpu_custom_call" | custom-call | flops 1610612736 | bytes 3932160 | tf_op jit(solution)/shard_map/pallas_call | solution.py:256
  30.9 2.5 %collective-permute-start.6 = (bf16[128,1024]{1,0:T(8,128)(2,1)S(1)}, bf16[128,1024]{1,0:T(8,128)(2,1)S(1)}, u32[]{:S(2)}, u32[]{:S(2)}) collective-permute-start(bf16[128,1024]{1,0:T(8,128)(2,1)S(1)} %get-tuple-element.13), channel_id=1, source_target_pairs={{0,1},{1,0},{2,3},{3,2},{4,5},{5,4},{6,7},{7,6},{8,9},{9,8},{10,11... | collective-permute-start | bytes 786440 | tf_op jit(solution)/shard_map/ppermute | solution.py:29
  33.4 1.9 %collective-permute-start.5 = (bf16[128,1024]{1,0:T(8,128)(2,1)S(1)}, bf16[128,1024]{1,0:T(8,128)(2,1)S(1)}, u32[]{:S(2)}, u32[]{:S(2)}) collective-permute-start(bf16[128,1024]{1,0:T(8,128)(2,1)S(1)} %get-tuple-element.11), channel_id=1, source_target_pairs={{1,0},{3,2},{4,1},{5,4},{6,3},{7,6},{9,8},{11,10},{12,9},{13,12},{... | collective-permute-start | bytes 786440 | tf_op jit(solution)/shard_map/ppermute | solution.py:29
  35.4 0.0 collective-permute-done.6
  35.4 0.0 copy-start.5
  35.4 0.1 add_convert_fusion.1
  35.5 1.9 %collective-permute-start.7 = (bf16[128,1024]{1,0:T(8,128)(2,1)S(1)}, bf16[128,1024]{1,0:T(8,128)(2,1)S(1)}, u32[]{:S(2)}, u32[]{:S(2)}) collective-permute-start(bf16[128,1024]{1,0:T(8,128)(2,1)S(1)} %add_convert_fusion.1), channel_id=1, source_target_pairs={{2,1},{3,0},{4,3},{5,2},{6,5},{7,4},{10,9},{11,8},{12,11},{13,10},... | collective-permute-start | bytes 786440 | tf_op jit(solution)/shard_map/ppermute | solution.py:29
  37.4 0.0 copy-done.5
  37.4 7.6 %shard_map.61 = (bf16[128,4096]{1,0:T(8,128)(2,1)}, f32[128,1024]{1,0:T(8,128)S(1)}) custom-call(s32[2]{0:T(128)S(1)} %copy-done.6, s32[2]{0:T(128)S(1)} %collective-permute-done.refs_1_, s32[4]{0:T(128)S(1)} %collective-permute-done.1.refs_2_, bf16[128,4096]{1,0:T(8,128)(2,1)S(1)} %bitcast.8, bf16[128,4096]{1,0:T(8,128)(2,1)S(1)} %bitcast.11, ...), custom_call_target="tpu_custom_call" | custom-call | flops 2147483648 | bytes 4849664 | tf_op jit(solution)/shard_map/pallas_call | solution.py:256
  45.0 0.0 collective-permute-done.5
  45.0 5.4 %collective-permute-done.7 = bf16[128,1024]{1,0:T(8,128)(2,1)S(1)} collective-permute-done((bf16[128,1024]{1,0:T(8,128)(2,1)S(1)}, bf16[128,1024]{1,0:T(8,128)(2,1)S(1)}, u32[]{:S(2)}, u32[]{:S(2)}) %collective-permute-start.7) | collective-permute-done | bytes 262176 | tf_op jit(solution)/shard_map/ppermute | solution.py:29
  50.4 0.8 %fusion = bf16[1,128,1024]{2,1,0:T(8,128)(2,1)} fusion(bf16[128,1024]{1,0:T(8,128)(2,1)S(1)} %collective-permute-done.7, f32[128,1024]{1,0:T(8,128)S(1)} %get-tuple-element.10, bf16[128,1024]{1,0:T(8,128)(2,1)S(1)} %collective-permute-done.5), kind=kLoop, calls=%fused_computation.2 | loop fusion | flops 655360 | bytes 1310720 | tf_op jit(solution)/shard_map/broadcast_in_dim | solution.py:309
Async XLA Ops:
  0.6 11.4 %copy-start.6 = (s32[2]{0:T(128)S(1)}, s32[2]{0:T(128)}, u32[]{:S(2)}) copy-start(s32[2]{0:T(128)} %refs_0_.5) | copy-start | bytes 28
  0.6 11.0 %collective-permute-start.2 = (bf16[128,1024]{1,0:T(8,128)(2,1)}, bf16[128,1024]{1,0:T(8,128)(2,1)S(1)}, u32[]{:S(2)}, u32[]{:S(2)}) collective-permute-start(bf16[128,1024]{1,0:T(8,128)(2,1)} %bitcast.12), channel_id=1, source_target_pairs={{0,3},{1,2},{2,5},{3,4},{4,7},{5,6},{8,11},{9,10},{10,13},{11,12},... | collective-permute-start | bytes 786440 | tf_op jit(solution)/shard_map/ppermute | solution.py:29
  4.4 18.1 %collective-permute-start.4 = (bf16[128,1024]{1,0:T(8,128)(2,1)}, bf16[128,1024]{1,0:T(8,128)(2,1)S(1)}, u32[]{:S(2)}, u32[]{:S(2)}) collective-permute-start(bf16[128,1024]{1,0:T(8,128)(2,1)} %bitcast.13), channel_id=1, source_target_pairs={{0,1},{1,4},{2,3},{3,6},{4,5},{6,7},{8,9},{9,12},{10,11},{11,14},{... | collective-permute-start | bytes 786440 | tf_op jit(solution)/shard_map/ppermute | solution.py:29
  11.6 11.0 %collective-permute-start.3 = (bf16[128,1024]{1,0:T(8,128)(2,1)S(1)}, bf16[128,1024]{1,0:T(8,128)(2,1)S(1)}, u32[]{:S(2)}, u32[]{:S(2)}) collective-permute-start(bf16[128,1024]{1,0:T(8,128)(2,1)S(1)} %collective-permute-done.2.refs_5_.refs_6_), channel_id=1, source_target_pairs={{0,1},{1,0},{2,3},{3,2},{4,5},{5,4},{6,7},{7,6},{8,9},{9,8},{10,11... | collective-permute-start | bytes 786440 | tf_op jit(solution)/shard_map/ppermute | solution.py:29
  12.0 2.4 %collective-permute-start = (s32[2]{0:T(128)S(1)}, s32[2]{0:T(128)S(1)}, u32[]{:S(2)}, u32[]{:S(2)}) collective-permute-start(s32[2]{0:T(128)S(1)} %copy-done.6), channel_id=1, source_target_pairs={{0,8},{8,0},{16,24},{24,16},{1,9},{9,1},{17,25},{25,17},{2,10},{10... | collective-permute-start | bytes 32 | tf_op jit(solution)/shard_map/ppermute | solution.py:57
  14.5 2.4 %collective-permute-start.1 = (s32[4]{0:T(128)S(1)}, s32[4]{0:T(128)S(1)}, u32[]{:S(2)}, u32[]{:S(2)}) collective-permute-start(s32[4]{0:T(128)S(1)} %pad_add_fusion), channel_id=1, source_target_pairs={{0,16},{8,24},{16,0},{24,8},{1,17},{9,25},{17,1},{25,9},{2,18},{10... | collective-permute-start | bytes 56 | tf_op jit(solution)/shard_map/ppermute | solution.py:57
  16.9 1.2 %copy-start = (bf16[1,128,4096]{2,1,0:T(8,128)(2,1)S(1)}, bf16[1,128,4096]{2,1,0:T(8,128)(2,1)}, u32[]{:S(2)}) copy-start(bf16[1,128,4096]{2,1,0:T(8,128)(2,1)} %param.4) | copy-start | bytes 3145732
  18.2 1.2 %copy-start.2 = (bf16[1,128,4096]{2,1,0:T(8,128)(2,1)S(1)}, bf16[1,128,4096]{2,1,0:T(8,128)(2,1)}, u32[]{:S(2)}) copy-start(bf16[1,128,4096]{2,1,0:T(8,128)(2,1)} %param.6) | copy-start | bytes 3145732
  19.4 0.9 %copy-start.4 = (bf16[1,128,1024]{2,1,0:T(8,128)(2,1)S(1)}, bf16[1,128,1024]{2,1,0:T(8,128)(2,1)}, u32[]{:S(2)}) copy-start(bf16[1,128,1024]{2,1,0:T(8,128)(2,1)} %param.5) | copy-start | bytes 786436
  20.3 2.2 %copy-start.1 = (bf16[1,128,4096]{2,1,0:T(8,128)(2,1)S(1)}, bf16[1,128,4096]{2,1,0:T(8,128)(2,1)}, u32[]{:S(2)}) copy-start(bf16[1,128,4096]{2,1,0:T(8,128)(2,1)} %param.4) | copy-start | bytes 3145732
  20.3 2.3 %copy-start.3 = (bf16[1,128,4096]{2,1,0:T(8,128)(2,1)S(1)}, bf16[1,128,4096]{2,1,0:T(8,128)(2,1)}, u32[]{:S(2)}) copy-start(bf16[1,128,4096]{2,1,0:T(8,128)(2,1)} %param.6) | copy-start | bytes 3145732
  30.9 4.4 %collective-permute-start.6 = (bf16[128,1024]{1,0:T(8,128)(2,1)S(1)}, bf16[128,1024]{1,0:T(8,128)(2,1)S(1)}, u32[]{:S(2)}, u32[]{:S(2)}) collective-permute-start(bf16[128,1024]{1,0:T(8,128)(2,1)S(1)} %get-tuple-element.13), channel_id=1, source_target_pairs={{0,1},{1,0},{2,3},{3,2},{4,5},{5,4},{6,7},{7,6},{8,9},{9,8},{10,11... | collective-permute-start | bytes 786440 | tf_op jit(solution)/shard_map/ppermute | solution.py:29
  33.4 11.6 %collective-permute-start.5 = (bf16[128,1024]{1,0:T(8,128)(2,1)S(1)}, bf16[128,1024]{1,0:T(8,128)(2,1)S(1)}, u32[]{:S(2)}, u32[]{:S(2)}) collective-permute-start(bf16[128,1024]{1,0:T(8,128)(2,1)S(1)} %get-tuple-element.11), channel_id=1, source_target_pairs={{1,0},{3,2},{4,1},{5,4},{6,3},{7,6},{9,8},{11,10},{12,9},{13,12},{... | collective-permute-start | bytes 786440 | tf_op jit(solution)/shard_map/ppermute | solution.py:29
  35.4 2.0 %copy-start.5 = (bf16[1,128,1024]{2,1,0:T(8,128)(2,1)S(1)}, bf16[1,128,1024]{2,1,0:T(8,128)(2,1)}, u32[]{:S(2)}) copy-start(bf16[1,128,1024]{2,1,0:T(8,128)(2,1)} %param.5) | copy-start | bytes 786436
  35.5 15.0 %collective-permute-start.7 = (bf16[128,1024]{1,0:T(8,128)(2,1)S(1)}, bf16[128,1024]{1,0:T(8,128)(2,1)S(1)}, u32[]{:S(2)}, u32[]{:S(2)}) collective-permute-start(bf16[128,1024]{1,0:T(8,128)(2,1)S(1)} %add_convert_fusion.1), channel_id=1, source_target_pairs={{2,1},{3,0},{4,3},{5,2},{6,5},{7,4},{10,9},{11,8},{12,11},{13,10},... | collective-permute-start | bytes 786440 | tf_op jit(solution)/shard_map/ppermute | solution.py:29

commit v4 on v3

v4 whole, which is shorter than its diff:
```python
import functools
import math

import jax
import jax.numpy as jnp
from jax import lax
from jax.experimental import pallas as pl
from jax.experimental.pallas import tpu as pltpu
from jax.sharding import PartitionSpec as P


HQ = 32
HK = 4
HD = 128
REACH = 3
GROUP = HQ // HK
F32 = jnp.float32
BF16 = jnp.bfloat16
NT = (((1,), (1,)), ((), ()))
NN = (((1,), (0,)), ((), ()))
SCALE = 1.0 / math.sqrt(HD)
RATE = SCALE * math.log2(math.e)
PAIRS = HQ // 2
PER_GROUP = GROUP // 2
SLOTS = 4


def moved(value, target_of):
    count = lax.axis_size("ctx")
    pairs = [(i, target_of(i)) for i in range(count)]
    return lax.ppermute(value, "ctx", [(s, t) for s, t in pairs if 0 <= t < count])


def one_three(value):
    return moved(value, lambda i: i + 1 if i % 2 else i + 3)


def three_one(value):
    return moved(value, lambda i: i + 3 if i % 2 else i + 1)


def swapped(value):
    return moved(value, lambda i: i ^ 1)


def all_lengths(lengths):
    count = lax.axis_size("pipe")
    pieces, stride = [lengths], 1
    while stride < count:
        pieces.append(
            lax.ppermute(jnp.concatenate(pieces), "pipe", [(i, i ^ stride) for i in range(count)])
        )
        stride *= 2
    return pieces


def fill_bias(lens_refs, starts_scr, bias_scr, offsets, rows, base=None):
    here = lax.axis_index("ctx")
    pipe = lax.axis_index("pipe")
    t_pos = here * rows + lax.broadcasted_iota(jnp.int32, (1, rows), 1)
    per_pipe = lens_refs[0].shape[0]
    place = 0
    for ref in lens_refs:
        for k in range(ref.shape[0]):
            starts_scr[((place // per_pipe) ^ pipe) * per_pipe + place % per_pipe] = ref[k]
            place += 1

    def step(d, carry):
        start, doc_start = carry
        doc_start = jnp.where(t_pos >= start, start, doc_start)
        return start + starts_scr[d], doc_start

    _, doc_start = lax.fori_loop(0, place, step, (jnp.int32(0), jnp.zeros((1, rows), jnp.int32)))
    for b, offset in enumerate(offsets):
        u_pos = (here - offset) * rows + lax.broadcasted_iota(jnp.int32, (rows, rows), 0)
        kept = 0.0 if base is None else base
        bias_scr[at(b, rows)] = jnp.where(u_pos >= doc_start, kept, -1e30).astype(F32)


def offsets_of_moved():
    odd = lax.rem(lax.axis_index("ctx"), 2)
    return (1 + 2 * odd, 2, 3 - 2 * odd)


def at(i, width):
    return slice(i * width, (i + 1) * width)


def stacked(ref, first, count):
    return jnp.concatenate([ref[:, at(first + k, HD)] for k in range(count)], axis=0)


def tall(refs, column):
    return jnp.concatenate([ref[:, at(column, HD)] for ref in refs], axis=0)


def keys_of(refs, i):
    return tall(refs, i // PER_GROUP)


def values_of(refs, i):
    return tall(refs, HK + i // PER_GROUP)


def scores_of(refs, q_ref, bias_scr, i):
    s = lax.dot_general(keys_of(refs, i), stacked(q_ref, 2 * i, 2), NT, preferred_element_type=F32)
    bias = bias_scr[...]
    return s + jnp.concatenate([bias, bias], axis=1)


def dweights_of(refs, d_ref, i):
    return lax.dot_general(values_of(refs, i), stacked(d_ref, 2 * i, 2), NT, preferred_element_type=F32)


def pipelined(stages):
    for step in range(PAIRS + len(stages) - 1):
        for k, stage in enumerate(stages):
            if 0 <= step - k < PAIRS:
                stage(step - k)


def at_group_end(action):
    def stage(i):
        if i % PER_GROUP == PER_GROUP - 1:
            action(i // PER_GROUP)

    return stage


def exponentials_kernel(n_lens, n_blocks, offsets_of, *refs):
    lens_refs, refs = refs[:n_lens], refs[n_lens:]
    q_ref, d_ref = refs[:2]
    kv_refs, (stats_ref, p_ref, dp_ref) = refs[2:2 + n_blocks], refs[2 + n_blocks:5 + n_blocks]
    starts_scr, bias_scr, s_scr = refs[5 + n_blocks:]
    rows = q_ref.shape[0]
    fill_bias(lens_refs, starts_scr, bias_scr, offsets_of(), rows)

    def first(i):
        s_scr[i % SLOTS] = scores_of(kv_refs, q_ref, bias_scr, i)
        dp_ref[:, at(i, 2 * rows)] = dweights_of(kv_refs, d_ref, i)

    def second(i):
        column = at(i, 2 * rows)
        s = s_scr[i % SLOTS]
        top = jnp.max(s, axis=0, keepdims=True)
        p = jnp.exp2((s - top) * RATE)
        p_ref[:, column] = p
        stats_ref[0:1, column] = top
        stats_ref[1:2, column] = jnp.sum(p, axis=0, keepdims=True)
        stats_ref[2:3, column] = jnp.sum(p * dp_ref[:, column], axis=0, keepdims=True)

    pipelined([first, second])


def products_kernel(
    n_lens, q_hbm, d_hbm, kv_hbm, s_ref, dp_ref, q_ref, d_ref, kv_ref, sems, kv_sem
):
    rows = q_ref.shape[0]
    kv_copy = pltpu.make_async_copy(kv_hbm, kv_ref, kv_sem)
    kv_copy.start()
    copies = []
    for group in range(HK):
        part = at(group, GROUP * HD)
        for k, (source, target) in enumerate(((q_hbm, q_ref), (d_hbm, d_ref))):
            copies.append(
                pltpu.make_async_copy(source.at[:, part], target.at[:, part], sems.at[k, group])
            )
            copies[-1].start()
    kv_copy.wait()
    for i in range(PAIRS):
        if i % PER_GROUP == 0:
            for k in range(2):
                copies[2 * (i // PER_GROUP) + k].wait()
        column = at(i, 2 * rows)
        s_ref[:, column] = lax.dot_general(
            keys_of([kv_ref], i), stacked(q_ref, 2 * i, 2), NT, preferred_element_type=F32
        )
        dp_ref[:, column] = dweights_of([kv_ref], d_ref, i)


def causal_kernel(n_lens, causal_ref):
    u = lax.broadcasted_iota(jnp.int32, causal_ref.shape, 0)
    t = lax.broadcasted_iota(jnp.int32, causal_ref.shape, 1)
    causal_ref[...] = jnp.where(u <= t, 0.0, -1e30).astype(F32)


def own_kernel(n_lens, *refs):
    lens_refs, refs = refs[:n_lens], refs[n_lens:]
    s_ref, dp_ref, causal_ref, stats_ref, p_ref, starts_scr, bias_scr = refs
    rows = s_ref.shape[0]
    fill_bias(lens_refs, starts_scr, bias_scr, (0,), rows, causal_ref[...])
    for i in range(PAIRS):
        column = at(i, 2 * rows)
        s = s_ref[:, column] + jnp.concatenate([bias_scr[...]] * 2, axis=1)
        top = jnp.max(s, axis=0, keepdims=True)
        p = jnp.exp2((s - top) * RATE)
        p_ref[:, column] = p
        stats_ref[0:1, column] = top
        stats_ref[1:2, column] = jnp.sum(p, axis=0, keepdims=True)
        stats_ref[2:3, column] = jnp.sum(p * dp_ref[:, column], axis=0, keepdims=True)


def remote_kernel(n_lens, *refs):
    lens_refs, refs = refs[:n_lens], refs[n_lens:]
    q_ref, d_ref, kv_ref, own_ref, mid_ref, pm_ref, dpm_ref = refs[:7]
    final_ref, ds_ref, g1_ref, g2_ref, g3_ref = refs[7:12]
    starts_scr, bias_scr, s_scr, dp_scr, p_scr, row_scr, w_scr = refs[12:]
    rows = q_ref.shape[0]
    mid = pm_ref.shape[0]
    g_refs = (g1_ref, g2_ref, g3_ref)
    fill_bias(lens_refs, starts_scr, bias_scr, offsets_of_moved()[2:], rows)

    def first(i):
        s_scr[i % SLOTS] = scores_of([kv_ref], q_ref, bias_scr, i)
        dp_scr[i % SLOTS] = dweights_of([kv_ref], d_ref, i)

    def second(i):
        column = at(i, 2 * rows)
        s, dp = s_scr[i % SLOTS], dp_scr[i % SLOTS]
        own_top, mid_top = own_ref[0:1, column], mid_ref[0:1, column]
        top = jnp.maximum(jnp.max(s, axis=0, keepdims=True), jnp.maximum(own_top, mid_top))
        p = jnp.exp2((s - top) * RATE)
        p_scr[i % SLOTS] = p
        own = jnp.exp2((own_top - top) * RATE)
        other = jnp.exp2((mid_top - top) * RATE)
        total = own_ref[1:2, column] * own + mid_ref[1:2, column] * other
        dot = own_ref[2:3, column] * own + mid_ref[2:3, column] * other
        inv = 1.0 / (total + jnp.sum(p, axis=0, keepdims=True))
        delta = (dot + jnp.sum(p * dp, axis=0, keepdims=True)) * inv
        row_scr[i % SLOTS, 0:1] = other * inv
        row_scr[i % SLOTS, 1:2] = inv
        row_scr[i % SLOTS, 2:3] = delta
        final_ref[0:1, column] = own * inv
        final_ref[1:2, column] = delta

    def third(i):
        column = at(i, 2 * rows)
        half, part = i // PER_GROUP % 2, at(i % PER_GROUP, 2 * rows)
        delta = row_scr[i % SLOTS, 2:3]
        w = pm_ref[:, column] * row_scr[i % SLOTS, 0:1]
        ds_ref[:mid, column] = (w * (dpm_ref[:, column] - delta)).astype(BF16)
        w_scr[half, :mid, part] = w.astype(BF16)
        w = p_scr[i % SLOTS] * row_scr[i % SLOTS, 1:2]
        ds_ref[mid:, column] = (w * (dp_scr[i % SLOTS] - delta)).astype(BF16)
        w_scr[half, mid:, part] = w.astype(BF16)

    def key_grads(group):
        dk = SCALE * lax.dot_general(
            ds_ref[:, at(group, GROUP * rows)], stacked(q_ref, group * GROUP, GROUP), NN,
            preferred_element_type=F32,
        )
        for b, g_ref in enumerate(g_refs):
            g_ref[:, at(group, HD)] = dk[at(b, rows)].astype(BF16)

    def value_grads(group):
        dv = lax.dot_general(
            w_scr[group % 2], stacked(d_ref, group * GROUP, GROUP), NN, preferred_element_type=F32
        )
        for b, g_ref in enumerate(g_refs):
            g_ref[:, at(HK + group, HD)] = dv[at(b, rows)].astype(BF16)

    pipelined([first, second, third, at_group_end(key_grads), at_group_end(value_grads)])


def join_kernel(n_lens, a_ref, b_ref, c_ref, sum_ref):
    total = a_ref[...].astype(F32) + b_ref[...].astype(F32) + c_ref[...].astype(F32)
    sum_ref[...] = total.astype(BF16)


def query_kernel(n_lens, *refs):
    q_ref, d_ref, kv0_ref, kv1_ref, kv2_ref, kv3_ref = refs[:6]
    p_ref, dp_ref, final_ref, ds_ref, dq_ref, own_ref, kt_scr, ds_scr, w_scr = refs[6:]
    rows = q_ref.shape[0]
    kv_refs = [kv0_ref, kv1_ref, kv2_ref, kv3_ref]

    def first(i):
        group = i // PER_GROUP
        if i % PER_GROUP == 0:
            for b, ref in enumerate(kv_refs):
                kt_scr[group, :, at(b, rows)] = ref[:, at(group, HD)].T
        column = at(i, 2 * rows)
        half, part = group % 2, at(i % PER_GROUP, 2 * rows)
        w = p_ref[:, column] * final_ref[0:1, column]
        ds_scr[half, :, part] = (w * (dp_ref[:, column] - final_ref[1:2, column])).astype(BF16)
        w_scr[half, :, part] = w.astype(BF16)

    def second(i):
        half, part = i // PER_GROUP % 2, at(i % PER_GROUP, 2 * rows)
        ds = jnp.concatenate([ds_scr[half, :, part], ds_ref[:, at(i, 2 * rows)]], axis=0)
        dqt = lax.dot_general(kt_scr[i // PER_GROUP], ds, NN, preferred_element_type=F32)
        dq = (dqt * SCALE).astype(BF16).T
        dq_ref[:, at(2 * i, HD)] = dq[:rows]
        dq_ref[:, at(2 * i + 1, HD)] = dq[rows:]

    def own_grads(group):
        own_ref[:, at(group, HD)] = SCALE * lax.dot_general(
            ds_scr[group % 2], stacked(q_ref, group * GROUP, GROUP), NN, preferred_element_type=F32
        )
        own_ref[:, at(HK + group, HD)] = lax.dot_general(
            w_scr[group % 2], stacked(d_ref, group * GROUP, GROUP), NN, preferred_element_type=F32
        )

    pipelined([first, second, at_group_end(own_grads)])


def call(body, lens, args, outs, scratch, matmul_rows, grant, in_hbm=0):
    specs = [pl.BlockSpec(memory_space=pltpu.SMEM)] * len(lens)
    specs += [pl.BlockSpec(memory_space=pltpu.HBM)] * in_hbm
    specs += [pl.BlockSpec(memory_space=pltpu.VMEM)] * (len(args) - in_hbm)
    docs = sum(x.shape[0] for x in lens)
    return pl.pallas_call(
        functools.partial(body, len(lens)),
        in_specs=specs,
        out_specs=[pl.BlockSpec(memory_space=pltpu.VMEM)] * len(outs),
        out_shape=outs,
        scratch_shapes=([pltpu.SMEM((docs,), jnp.int32)] if lens else []) + scratch,
        cost_estimate=pl.CostEstimate(
            flops=2 * HQ * HD * HD * matmul_rows,
            bytes_accessed=sum(x.size * x.dtype.itemsize for x in list(args) + list(outs)),
            transcendentals=0,
        ),
        compiler_params=pltpu.CompilerParams(vmem_limit_bytes=grant << 20),
    )(*lens, *args)


def exponentials(lens, q, dout, kvs, offsets_of):
    rows = q.shape[0]
    tall_rows = len(kvs) * rows
    array = jax.ShapeDtypeStruct
    return call(
        lambda n_lens, *refs: exponentials_kernel(n_lens, len(kvs), offsets_of, *refs),
        lens, (q, dout) + tuple(kvs),
        [array((8, HQ * rows), F32)] + [array((tall_rows, HQ * rows), F32)] * 2,
        [pltpu.VMEM((tall_rows, rows), F32), pltpu.VMEM((SLOTS, tall_rows, 2 * rows), F32)],
        2 * tall_rows, 4,
    )


def on_device(queries, keys_values, out_grads, doc_lengths):
    kv, q, dout = keys_values[0], queries[0], out_grads[0]
    rows, wide = kv.shape
    array = jax.ShapeDtypeStruct
    blocks = REACH * rows
    keys = blocks + rows
    near = one_three(kv)
    far = three_one(kv)
    lens = all_lengths(doc_lengths)
    side = swapped(near)
    square = array((rows, HQ * rows), F32)
    (causal,) = call(causal_kernel, (), (), [array((rows, rows), F32)], [], keys, 1)
    s_own, dp_own, q, dout, kv = call(
        products_kernel, (),
        [pltpu.with_memory_space_constraint(x, pltpu.HBM) for x in (q, dout, kv)],
        [square, square] + [array(x.shape, BF16) for x in (q, dout, kv)],
        [pltpu.SemaphoreType.DMA((2, HK)), pltpu.SemaphoreType.DMA(())],
        2 * rows, 4, in_hbm=3,
    )
    own_stats, p_own = call(
        own_kernel, lens, (s_own, dp_own, causal),
        [array((8, HQ * rows), F32), square], [pltpu.VMEM((rows, rows), F32)], rows, 2,
    )
    mid_stats, p_mid, dp_mid = exponentials(
        lens, q, dout, (near, side), lambda: offsets_of_moved()[:2]
    )
    final, ds, g_near, g_side, g_far = call(
        remote_kernel, lens,
        (q, dout, far, own_stats, mid_stats, p_mid, dp_mid),
        [array((8, HQ * rows), F32), array((blocks, HQ * rows), BF16)]
        + [array((rows, wide), BF16)] * 3,
        [pltpu.VMEM((rows, rows), F32)]
        + [pltpu.VMEM((SLOTS, rows, 2 * rows), F32)] * 3
        + [pltpu.VMEM((SLOTS, 8, 2 * rows), F32)]
        + [pltpu.VMEM((2, blocks, GROUP * rows), BF16)],
        2 * rows + 2 * blocks, 8,
    )
    relayed = moved(g_far, lambda i: -1 if i % 2 else i - 2)
    side_back = swapped(g_side)
    chip_back = moved(g_far, lambda i: i - 1 if i % 2 else -1)
    joined = g_near.astype(F32) + side_back.astype(F32)
    odd_back = moved(joined.astype(BF16), lambda i: i - 3 if i % 2 else -1)
    dq, own = call(
        query_kernel, (),
        (q, dout, kv, near, side, far, p_own, dp_own, final, ds),
        [array(q.shape, BF16), array((rows, wide), F32)],
        [pltpu.VMEM((HK, HD, keys), BF16)]
        + [pltpu.VMEM((2, rows, GROUP * rows), BF16)] * 2,
        2 * rows + keys, 6,
    )
    (joined,) = call(
        join_kernel, (), (g_near, side_back, relayed),
        [array((rows, wide), BF16)], [], 1, 1,
    )
    even_back = moved(joined, lambda i: -1 if i % 2 else i - 1)
    total = own + chip_back.astype(F32) + odd_back.astype(F32) + even_back.astype(F32)
    return (dq[None], total.astype(BF16)[None])


def solution(mesh):
    spec = P("pipe", "ctx", None)
    return jax.shard_map(
        on_device,
        mesh=mesh,
        in_specs=(spec, spec, spec, P("pipe")),
        out_specs=(spec, spec),
        check_vma=False,
    )
```

time: 51.5 us -> 49 us (0.951)
  the two profiles are of different devices: /device:TPU:9 before, /device:TPU:1 now
where the time goes in v4:
time: 49 us; the launch traced here: 48.8 us
  starting transfers between devices  18.2 us (37%)
  waiting for transfers between devices  14.4 us (29%)
  Pallas kernels  14.3 us (29%)
  other arithmetic  1.01 us (2%)
  between operations  0.79 us (2%)
    ppermute x8, starting transfers between devices, moved(): lax.ppermute(value, 'ctx', [(s, t) for s, t in pairs if 0 <= t < count])  15.7 us
    pallas_call x7, Pallas kernels, call(): pl.pallas_call(functools.partial(body, len(lens)), in_specs=specs, out_sp...  14.3 us
    ppermute x8, waiting for transfers between devices, moved(): lax.ppermute(value, 'ctx', [(s, t) for s, t in pairs if 0 <= t < count])  13.2 us
    ppermute x2, starting transfers between devices, all_lengths(): lax.ppermute(jnp.concatenate(pieces), 'pipe', [(i, i ^ stride) for i in r...  2.52 us
    ppermute x2, waiting for transfers between devices, all_lengths(): lax.ppermute(jnp.concatenate(pieces), 'pipe', [(i, i ^ stride) for i in r...  1.18 us
  transfers between devices with their start and end apart: 10, of which 3 were waited for; matrix products, arithmetic and copies ran while one was open for 0% of the time, Pallas kernels for 20%

profile of v4, /device:TPU:1, one launch (start us, length us, event | category | flops | bytes accessed | tf_op | source)
XLA Modules:
  0.0 48.8 jit_solution(7039214051701211885)
XLA Ops:
  0.6 0.0 copy-start
  0.6 4.6 %collective-permute-start = (bf16[128,1024]{1,0:T(8,128)(2,1)}, bf16[128,1024]{1,0:T(8,128)(2,1)S(1)}, u32[]{:S(2)}, u32[]{:S(2)}) collective-permute-start(bf16[128,1024]{1,0:T(8,128)(2,1)} %bitcast.8), channel_id=1, source_target_pairs={{0,3},{1,2},{2,5},{3,4},{4,7},{5,6},{8,11},{9,10},{10,13},{11,12},... | collective-permute-start | bytes 786440 | tf_op jit(solution)/shard_map/ppermute | solution.py:31
  5.2 6.4 %collective-permute-done.refs_5_.refs_3_ = bf16[128,1024]{1,0:T(8,128)(2,1)S(1)} collective-permute-done((bf16[128,1024]{1,0:T(8,128)(2,1)}, bf16[128,1024]{1,0:T(8,128)(2,1)S(1)}, u32[]{:S(2)}, u32[]{:S(2)}) %collective-permute-start) | collective-permute-done | bytes 262176 | tf_op jit(solution)/shard_map/ppermute | solution.py:31
  11.6 0.4 collective-permute-start.1
  12.0 5.0 %collective-permute-start.2 = (bf16[128,1024]{1,0:T(8,128)(2,1)}, bf16[128,1024]{1,0:T(8,128)(2,1)S(1)}, u32[]{:S(2)}, u32[]{:S(2)}) collective-permute-start(bf16[128,1024]{1,0:T(8,128)(2,1)} %bitcast.9), channel_id=1, source_target_pairs={{0,1},{1,4},{2,3},{3,6},{4,5},{6,7},{8,9},{9,12},{10,11},{11,14},{... | collective-permute-start | bytes 786440 | tf_op jit(solution)/shard_map/ppermute | solution.py:31
  17.0 1.3 %collective-permute-start.3 = (s32[2]{0:T(128)}, s32[2]{0:T(128)S(1)}, u32[]{:S(2)}, u32[]{:S(2)}) collective-permute-start(s32[2]{0:T(128)} %refs_0_.5), channel_id=1, source_target_pairs={{0,8},{8,0},{16,24},{24,16},{1,9},{9,1},{17,25},{25,17},{2,10},{10... | collective-permute-start | bytes 32 | tf_op jit(solution)/shard_map/ppermute | solution.py:51
  18.3 2.8 %shard_map.59 = (f32[128,4096]{1,0:T(8,128)S(1)}, f32[128,4096]{1,0:T(8,128)S(1)}, bf16[128,4096]{1,0:T(8,128)(2,1)S(1)}, bf16[128,4096]{1,0:T(8,128)(2,1)S(1)}, bf16[128,1024]{1,0:T(8,128)(2,1)S(1)}) custom-call(bf16[128,4096]{1,0:T(8,128)(2,1)} %bitcast.6, bf16[128,4096]{1,0:T(8,128)(2,1)} %bitcast.7, bf16[128,1024]{1,0:T(8,128)(2,1)} %bitcast.10), custom_call_target="tpu_custom_call" | custom-call | flops 268435456 | bytes 8912896 | tf_op jit(solution)/shard_map/pallas_call | solution.py:311
  21.2 0.0 collective-permute-done.3.refs_1_
  21.2 0.0 copy-done
  21.2 0.1 pad_add_fusion
  21.3 1.2 %collective-permute-start.4 = (s32[4]{0:T(128)S(1)}, s32[4]{0:T(128)S(1)}, u32[]{:S(2)}, u32[]{:S(2)}) collective-permute-start(s32[4]{0:T(128)S(1)} %pad_add_fusion), channel_id=1, source_target_pairs={{0,16},{8,24},{16,0},{24,8},{1,17},{9,25},{17,1},{25,9},{2,18},{10... | collective-permute-start | bytes 56 | tf_op jit(solution)/shard_map/ppermute | solution.py:51
  22.5 1.2 %collective-permute-done.4.refs_2_ = s32[4]{0:T(128)S(1)} collective-permute-done((s32[4]{0:T(128)S(1)}, s32[4]{0:T(128)S(1)}, u32[]{:S(2)}, u32[]{:S(2)}) %collective-permute-start.4) | collective-permute-done | bytes 48 | tf_op jit(solution)/shard_map/ppermute | solution.py:51
  23.7 1.4 %shard_map.61 = (f32[8,4096]{1,0:T(8,128)S(1)}, f32[128,4096]{1,0:T(8,128)S(1)}) custom-call(s32[2]{0:T(128)S(1)} %copy-done, s32[2]{0:T(128)S(1)} %collective-permute-done.3.refs_1_, s32[4]{0:T(128)S(1)} %collective-permute-done.4.refs_2_, f32[128,4096]{1,0:T(8,128)S(1)} %get-tuple-element.22.refs_3_, f32[128,4096]{1,0:T(8,128)S(1)} %get-tuple-element.23.refs_4_.refs_7_, ...), custom_call_target="tpu_custom_call" | custom-call | flops 134217728 | bytes 6488064 | tf_op jit(solution)/shard_map/pallas_call | solution.py:311
  25.0 0.0 collective-permute-done.1.refs_6_.refs_4_
  25.1 3.1 %shard_map.62 = (f32[8,4096]{1,0:T(8,128)S(1)}, f32[256,4096]{1,0:T(8,128)S(1)}, f32[256,4096]{1,0:T(8,128)S(1)}) custom-call(s32[2]{0:T(128)S(1)} %copy-done, s32[2]{0:T(128)S(1)} %collective-permute-done.3.refs_1_, s32[4]{0:T(128)S(1)} %collective-permute-done.4.refs_2_, bf16[128,4096]{1,0:T(8,128)(2,1)S(1)} %get-tuple-element.19.refs_3_.refs_0_, ...), custom_call_target="tpu_custom_call" | custom-call | flops 536870912 | bytes 11141120 | tf_op jit(solution)/shard_map/pallas_call | solution.py:311
  28.1 0.0 collective-permute-done.2.refs_5_
  28.1 4.3 %shard_map.63 = (f32[8,4096]{1,0:T(8,128)S(1)}, bf16[384,4096]{1,0:T(8,128)(2,1)S(1)}, bf16[128,1024]{1,0:T(8,128)(2,1)S(1)}, bf16[128,1024]{1,0:T(8,128)(2,1)S(1)}, bf16[128,1024]{1,0:T(8,128)(2,1)S(1)}) custom-call(s32[2]{0:T(128)S(1)} %copy-done, s32[2]{0:T(128)S(1)} %collective-permute-done.3.refs_1_, s32[4]{0:T(128)S(1)} %collective-permute-done.4.refs_2_, ...), custom_call_target="tpu_custom_call" | custom-call | flops 1073741824 | bytes 15073280 | tf_op jit(solution)/shard_map/pallas_call | solution.py:311
  32.5 0.1 collective-permute-start.6
  32.5 0.7 %collective-permute-start.8 = (bf16[128,1024]{1,0:T(8,128)(2,1)S(1)}, bf16[128,1024]{1,0:T(8,128)(2,1)S(1)}, u32[]{:S(2)}, u32[]{:S(2)}) collective-permute-start(bf16[128,1024]{1,0:T(8,128)(2,1)S(1)} %get-tuple-element.33), channel_id=1, source_target_pairs={{2,0},{4,2},{6,4},{10,8},{12,10},{14,12},{18,16},{20,18},{22,20},{... | collective-permute-start | bytes 786440 | tf_op jit(solution)/shard_map/ppermute | solution.py:31
  33.2 3.0 %collective-permute-start.5 = (bf16[128,1024]{1,0:T(8,128)(2,1)S(1)}, bf16[128,1024]{1,0:T(8,128)(2,1)S(1)}, u32[]{:S(2)}, u32[]{:S(2)}) collective-permute-start(bf16[128,1024]{1,0:T(8,128)(2,1)S(1)} %get-tuple-element.33), channel_id=1, source_target_pairs={{1,0},{3,2},{5,4},{7,6},{9,8},{11,10},{13,12},{15,14},{17,16},{19,... | collective-permute-start | bytes 786440 | tf_op jit(solution)/shard_map/ppermute | solution.py:31
  36.3 0.0 collective-permute-done.6.b_ref
  36.3 0.1 add_convert_fusion.1
  36.3 0.7 %collective-permute-start.7 = (bf16[128,1024]{1,0:T(8,128)(2,1)S(1)}, bf16[128,1024]{1,0:T(8,128)(2,1)S(1)}, u32[]{:S(2)}, u32[]{:S(2)}) collective-permute-start(bf16[128,1024]{1,0:T(8,128)(2,1)S(1)} %add_convert_fusion.1), channel_id=1, source_target_pairs={{3,0},{5,2},{7,4},{11,8},{13,10},{15,12},{19,16},{21,18},{23,20},{... | collective-permute-start | bytes 786440 | tf_op jit(solution)/shard_map/ppermute | solution.py:31
  37.0 0.0 collective-permute-done.8.c_ref
  37.0 0.1 shard_map.65
  37.1 1.3 %collective-permute-start.9 = (bf16[128,1024]{1,0:T(8,128)(2,1)S(1)}, bf16[128,1024]{1,0:T(8,128)(2,1)S(1)}, u32[]{:S(2)}, u32[]{:S(2)}) collective-permute-start(bf16[128,1024]{1,0:T(8,128)(2,1)S(1)} %shard_map.65), channel_id=1, source_target_pairs={{2,1},{4,3},{6,5},{10,9},{12,11},{14,13},{18,17},{20,19},{22,21},{... | collective-permute-start | bytes 786440 | tf_op jit(solution)/shard_map/ppermute | solution.py:31
  38.4 2.6 %shard_map.64 = (bf16[128,4096]{1,0:T(8,128)(2,1)}, f32[128,1024]{1,0:T(8,128)S(1)}) custom-call(bf16[128,4096]{1,0:T(8,128)(2,1)S(1)} %get-tuple-element.19.refs_3_.refs_0_, bf16[128,4096]{1,0:T(8,128)(2,1)S(1)} %get-tuple-element.20.refs_4_.refs_1_, bf16[128,1024]{1,0:T(8,128)(2,1)S(1)} %get-tuple-element.21.refs_2_, ...), custom_call_target="tpu_custom_call" | custom-call | flops 805306368 | bytes 12189696 | tf_op jit(solution)/shard_map/pallas_call | solution.py:311
  41.1 0.0 collective-permute-done.5
  41.1 0.0 collective-permute-done.7
  41.1 6.8 %collective-permute-done.9 = bf16[128,1024]{1,0:T(8,128)(2,1)S(1)} collective-permute-done((bf16[128,1024]{1,0:T(8,128)(2,1)S(1)}, bf16[128,1024]{1,0:T(8,128)(2,1)S(1)}, u32[]{:S(2)}, u32[]{:S(2)}) %collective-permute-start.9) | collective-permute-done | bytes 262176 | tf_op jit(solution)/shard_map/ppermute | solution.py:31
  47.9 0.9 %fusion = bf16[1,128,1024]{2,1,0:T(8,128)(2,1)} fusion(bf16[128,1024]{1,0:T(8,128)(2,1)S(1)} %collective-permute-done.9, bf16[128,1024]{1,0:T(8,128)(2,1)S(1)} %collective-permute-done.7, f32[128,1024]{1,0:T(8,128)S(1)} %get-tuple-element.32, bf16[128,1024]{1,0:T(8,128)(2,1)S(1)} %collective-permute-done.5), kind=kLoop, calls=%fused_computation.2 | loop fusion | flops 917504 | bytes 1572864 | tf_op jit(solution)/shard_map/broadcast_in_dim | solution.py:395
  (1 shorter events, 0.0 us)
Async XLA Ops:
  0.6 20.5 %copy-start = (s32[2]{0:T(128)S(1)}, s32[2]{0:T(128)}, u32[]{:S(2)}) copy-start(s32[2]{0:T(128)} %refs_0_.5) | copy-start | bytes 28
  0.6 11.0 %collective-permute-start = (bf16[128,1024]{1,0:T(8,128)(2,1)}, bf16[128,1024]{1,0:T(8,128)(2,1)S(1)}, u32[]{:S(2)}, u32[]{:S(2)}) collective-permute-start(bf16[128,1024]{1,0:T(8,128)(2,1)} %bitcast.8), channel_id=1, source_target_pairs={{0,3},{1,2},{2,5},{3,4},{4,7},{5,6},{8,11},{9,10},{10,13},{11,12},... | collective-permute-start | bytes 786440 | tf_op jit(solution)/shard_map/ppermute | solution.py:31
  11.6 13.4 %collective-permute-start.1 = (bf16[128,1024]{1,0:T(8,128)(2,1)S(1)}, bf16[128,1024]{1,0:T(8,128)(2,1)S(1)}, u32[]{:S(2)}, u32[]{:S(2)}) collective-permute-start(bf16[128,1024]{1,0:T(8,128)(2,1)S(1)} %collective-permute-done.refs_5_.refs_3_), channel_id=1, source_target_pairs={{0,1},{1,0},{2,3},{3,2},{4,5},{5,4},{6,7},{7,6},{8,9},{9,8},{10,11... | collective-permute-start | bytes 786440 | tf_op jit(solution)/shard_map/ppermute | solution.py:31
  12.0 16.1 %collective-permute-start.2 = (bf16[128,1024]{1,0:T(8,128)(2,1)}, bf16[128,1024]{1,0:T(8,128)(2,1)S(1)}, u32[]{:S(2)}, u32[]{:S(2)}) collective-permute-start(bf16[128,1024]{1,0:T(8,128)(2,1)} %bitcast.9), channel_id=1, source_target_pairs={{0,1},{1,4},{2,3},{3,6},{4,5},{6,7},{8,9},{9,12},{10,11},{11,14},{... | collective-permute-start | bytes 786440 | tf_op jit(solution)/shard_map/ppermute | solution.py:31
  17.0 4.1 %collective-permute-start.3 = (s32[2]{0:T(128)}, s32[2]{0:T(128)S(1)}, u32[]{:S(2)}, u32[]{:S(2)}) collective-permute-start(s32[2]{0:T(128)} %refs_0_.5), channel_id=1, source_target_pairs={{0,8},{8,0},{16,24},{24,16},{1,9},{9,1},{17,25},{25,17},{2,10},{10... | collective-permute-start | bytes 32 | tf_op jit(solution)/shard_map/ppermute | solution.py:51
  21.3 2.4 %collective-permute-start.4 = (s32[4]{0:T(128)S(1)}, s32[4]{0:T(128)S(1)}, u32[]{:S(2)}, u32[]{:S(2)}) collective-permute-start(s32[4]{0:T(128)S(1)} %pad_add_fusion), channel_id=1, source_target_pairs={{0,16},{8,24},{16,0},{24,8},{1,17},{9,25},{17,1},{25,9},{2,18},{10... | collective-permute-start | bytes 56 | tf_op jit(solution)/shard_map/ppermute | solution.py:51
  32.5 3.8 %collective-permute-start.6 = (bf16[128,1024]{1,0:T(8,128)(2,1)S(1)}, bf16[128,1024]{1,0:T(8,128)(2,1)S(1)}, u32[]{:S(2)}, u32[]{:S(2)}) collective-permute-start(bf16[128,1024]{1,0:T(8,128)(2,1)S(1)} %get-tuple-element.35), channel_id=1, source_target_pairs={{0,1},{1,0},{2,3},{3,2},{4,5},{5,4},{6,7},{7,6},{8,9},{9,8},{10,11... | collective-permute-start | bytes 786440 | tf_op jit(solution)/shard_map/ppermute | solution.py:31
  32.5 4.5 %collective-permute-start.8 = (bf16[128,1024]{1,0:T(8,128)(2,1)S(1)}, bf16[128,1024]{1,0:T(8,128)(2,1)S(1)}, u32[]{:S(2)}, u32[]{:S(2)}) collective-permute-start(bf16[128,1024]{1,0:T(8,128)(2,1)S(1)} %get-tuple-element.33), channel_id=1, source_target_pairs={{2,0},{4,2},{6,4},{10,8},{12,10},{14,12},{18,16},{20,18},{22,20},{... | collective-permute-start | bytes 786440 | tf_op jit(solution)/shard_map/ppermute | solution.py:31
  33.2 7.9 %collective-permute-start.5 = (bf16[128,1024]{1,0:T(8,128)(2,1)S(1)}, bf16[128,1024]{1,0:T(8,128)(2,1)S(1)}, u32[]{:S(2)}, u32[]{:S(2)}) collective-permute-start(bf16[128,1024]{1,0:T(8,128)(2,1)S(1)} %get-tuple-element.33), channel_id=1, source_target_pairs={{1,0},{3,2},{5,4},{7,6},{9,8},{11,10},{13,12},{15,14},{17,16},{19,... | collective-permute-start | bytes 786440 | tf_op jit(solution)/shard_map/ppermute | solution.py:31
  36.3 4.7 %collective-permute-start.7 = (bf16[128,1024]{1,0:T(8,128)(2,1)S(1)}, bf16[128,1024]{1,0:T(8,128)(2,1)S(1)}, u32[]{:S(2)}, u32[]{:S(2)}) collective-permute-start(bf16[128,1024]{1,0:T(8,128)(2,1)S(1)} %add_convert_fusion.1), channel_id=1, source_target_pairs={{3,0},{5,2},{7,4},{11,8},{13,10},{15,12},{19,16},{21,18},{23,20},{... | collective-permute-start | bytes 786440 | tf_op jit(solution)/shard_map/ppermute | solution.py:31
  37.1 10.8 %collective-permute-start.9 = (bf16[128,1024]{1,0:T(8,128)(2,1)S(1)}, bf16[128,1024]{1,0:T(8,128)(2,1)S(1)}, u32[]{:S(2)}, u32[]{:S(2)}) collective-permute-start(bf16[128,1024]{1,0:T(8,128)(2,1)S(1)} %shard_map.65), channel_id=1, source_target_pairs={{2,1},{4,3},{6,5},{10,9},{12,11},{14,13},{18,17},{20,19},{22,21},{... | collective-permute-start | bytes 786440 | tf_op jit(solution)/shard_map/ppermute | solution.py:31

commit v5 on v4

--- a/solution.py
+++ b/solution.py
@@ -152,25 +152,9 @@
     pipelined([first, second])
 
 
-def products_kernel(
-    n_lens, q_hbm, d_hbm, kv_hbm, s_ref, dp_ref, q_ref, d_ref, kv_ref, sems, kv_sem
-):
+def products_kernel(n_lens, q_ref, d_ref, kv_ref, s_ref, dp_ref):
     rows = q_ref.shape[0]
-    kv_copy = pltpu.make_async_copy(kv_hbm, kv_ref, kv_sem)
-    kv_copy.start()
-    copies = []
-    for group in range(HK):
-        part = at(group, GROUP * HD)
-        for k, (source, target) in enumerate(((q_hbm, q_ref), (d_hbm, d_ref))):
-            copies.append(
-                pltpu.make_async_copy(source.at[:, part], target.at[:, part], sems.at[k, group])
-            )
-            copies[-1].start()
-    kv_copy.wait()
     for i in range(PAIRS):
-        if i % PER_GROUP == 0:
-            for k in range(2):
-                copies[2 * (i // PER_GROUP) + k].wait()
         column = at(i, 2 * rows)
         s_ref[:, column] = lax.dot_general(
             keys_of([kv_ref], i), stacked(q_ref, 2 * i, 2), NT, preferred_element_type=F32
@@ -200,14 +184,12 @@
         stats_ref[2:3, column] = jnp.sum(p * dp_ref[:, column], axis=0, keepdims=True)
 
 
-def remote_kernel(n_lens, *refs):
+def far_kernel(n_lens, *refs):
     lens_refs, refs = refs[:n_lens], refs[n_lens:]
-    q_ref, d_ref, kv_ref, own_ref, mid_ref, pm_ref, dpm_ref = refs[:7]
-    final_ref, ds_ref, g1_ref, g2_ref, g3_ref = refs[7:12]
-    starts_scr, bias_scr, s_scr, dp_scr, p_scr, row_scr, w_scr = refs[12:]
+    q_ref, d_ref, kv_ref, own_ref, mid_ref = refs[:5]
+    final_ref, ds_ref, g_ref = refs[5:8]
+    starts_scr, bias_scr, s_scr, dp_scr, p_scr, row_scr, w_scr = refs[8:]
     rows = q_ref.shape[0]
-    mid = pm_ref.shape[0]
-    g_refs = (g1_ref, g2_ref, g3_ref)
     fill_bias(lens_refs, starts_scr, bias_scr, offsets_of_moved()[2:], rows)
 
     def first(i):
@@ -227,49 +209,81 @@
         dot = own_ref[2:3, column] * own + mid_ref[2:3, column] * other
         inv = 1.0 / (total + jnp.sum(p, axis=0, keepdims=True))
         delta = (dot + jnp.sum(p * dp, axis=0, keepdims=True)) * inv
-        row_scr[i % SLOTS, 0:1] = other * inv
-        row_scr[i % SLOTS, 1:2] = inv
-        row_scr[i % SLOTS, 2:3] = delta
+        row_scr[i % SLOTS, 0:1] = inv
+        row_scr[i % SLOTS, 1:2] = delta
         final_ref[0:1, column] = own * inv
         final_ref[1:2, column] = delta
+        final_ref[2:3, column] = other * inv
 
     def third(i):
-        column = at(i, 2 * rows)
-        half, part = i // PER_GROUP % 2, at(i % PER_GROUP, 2 * rows)
-        delta = row_scr[i % SLOTS, 2:3]
-        w = pm_ref[:, column] * row_scr[i % SLOTS, 0:1]
-        ds_ref[:mid, column] = (w * (dpm_ref[:, column] - delta)).astype(BF16)
-        w_scr[half, :mid, part] = w.astype(BF16)
-        w = p_scr[i % SLOTS] * row_scr[i % SLOTS, 1:2]
-        ds_ref[mid:, column] = (w * (dp_scr[i % SLOTS] - delta)).astype(BF16)
-        w_scr[half, mid:, part] = w.astype(BF16)
-
-    def key_grads(group):
-        dk = SCALE * lax.dot_general(
+        w = p_scr[i % SLOTS] * row_scr[i % SLOTS, 0:1]
+        ds = (w * (dp_scr[i % SLOTS] - row_scr[i % SLOTS, 1:2])).astype(BF16)
+        ds_ref[:, at(i, 2 * rows)] = ds
+        w_scr[i // PER_GROUP % 2, :, at(i % PER_GROUP, 2 * rows)] = w.astype(BF16)
+
+    def gradients(group):
+        dk = lax.dot_general(
             ds_ref[:, at(group, GROUP * rows)], stacked(q_ref, group * GROUP, GROUP), NN,
             preferred_element_type=F32,
         )
-        for b, g_ref in enumerate(g_refs):
-            g_ref[:, at(group, HD)] = dk[at(b, rows)].astype(BF16)
+        g_ref[:, at(group, HD)] = (dk * SCALE).astype(BF16)
+        dv = lax.dot_general(
+            w_scr[group % 2], stacked(d_ref, group * GROUP, GROUP), NN, preferred_element_type=F32
+        )
+        g_ref[:, at(HK + group, HD)] = dv.astype(BF16)
+
+    pipelined([first, second, third, at_group_end(gradients)])
+
+
+def mid_kernel(n_lens, *refs):
+    q_ref, d_ref, p_ref, dp_ref, final_ref, far_ref, near_ref, pair_ref, ds_ref, w_scr = refs
+    rows = q_ref.shape[0]
+    pair_ref[rows:] = far_ref[...]
+
+    def first(i):
+        column = at(i, 2 * rows)
+        w = p_ref[:, column] * final_ref[2:3, column]
+        ds_ref[:, column] = (w * (dp_ref[:, column] - final_ref[1:2, column])).astype(BF16)
+        w_scr[i // PER_GROUP % 2, :, at(i % PER_GROUP, 2 * rows)] = w.astype(BF16)
+
+    def key_grads(group):
+        dk = lax.dot_general(
+            ds_ref[:, at(group, GROUP * rows)], stacked(q_ref, group * GROUP, GROUP), NN,
+            preferred_element_type=F32,
+        )
+        dk = (dk * SCALE).astype(BF16)
+        near_ref[:, at(group, HD)] = dk[:rows]
+        pair_ref[:rows, at(group, HD)] = dk[rows:]
 
     def value_grads(group):
         dv = lax.dot_general(
             w_scr[group % 2], stacked(d_ref, group * GROUP, GROUP), NN, preferred_element_type=F32
-        )
-        for b, g_ref in enumerate(g_refs):
-            g_ref[:, at(HK + group, HD)] = dv[at(b, rows)].astype(BF16)
-
-    pipelined([first, second, third, at_group_end(key_grads), at_group_end(value_grads)])
-
-
-def join_kernel(n_lens, a_ref, b_ref, c_ref, sum_ref):
-    total = a_ref[...].astype(F32) + b_ref[...].astype(F32) + c_ref[...].astype(F32)
-    sum_ref[...] = total.astype(BF16)
+        ).astype(BF16)
+        near_ref[:, at(HK + group, HD)] = dv[:rows]
+        pair_ref[:rows, at(HK + group, HD)] = dv[rows:]
+
+    pipelined([first, at_group_end(key_grads), at_group_end(value_grads)])
+
+
+def sum_kernel(n_lens, near_ref, pair_ref, *refs):
+    rows = near_ref.shape[0]
+    total = near_ref[...].astype(F32) + pair_ref[:rows].astype(F32)
+    for ref in refs[:-1]:
+        total = total + ref[...].astype(F32)
+    refs[-1][...] = total.astype(BF16)
+
+
+def finish_kernel(n_lens, own_ref, pair_ref, odd_ref, even_ref, total_ref):
+    rows = own_ref.shape[0]
+    even = lax.rem(lax.axis_index("ctx"), 2) == 0
+    chip = pair_ref[rows:].astype(F32) + odd_ref[...].astype(F32)
+    moved_in = jnp.where(even, chip, even_ref[...].astype(F32))
+    total_ref[...] = (own_ref[...] + moved_in).astype(BF16)
 
 
 def query_kernel(n_lens, *refs):
     q_ref, d_ref, kv0_ref, kv1_ref, kv2_ref, kv3_ref = refs[:6]
-    p_ref, dp_ref, final_ref, ds_ref, dq_ref, own_ref, kt_scr, ds_scr, w_scr = refs[6:]
+    p_ref, dp_ref, final_ref, mid_ref, far_ref, dq_ref, own_ref, kt_scr, ds_scr, w_scr = refs[6:]
     rows = q_ref.shape[0]
     kv_refs = [kv0_ref, kv1_ref, kv2_ref, kv3_ref]
 
@@ -286,7 +300,10 @@
 
     def second(i):
         half, part = i // PER_GROUP % 2, at(i % PER_GROUP, 2 * rows)
-        ds = jnp.concatenate([ds_scr[half, :, part], ds_ref[:, at(i, 2 * rows)]], axis=0)
+        column = at(i, 2 * rows)
+        ds = jnp.concatenate(
+            [ds_scr[half, :, part], mid_ref[:, column], far_ref[:, column]], axis=0
+        )
         dqt = lax.dot_general(kt_scr[i // PER_GROUP], ds, NN, preferred_element_type=F32)
         dq = (dqt * SCALE).astype(BF16).T
         dq_ref[:, at(2 * i, HD)] = dq[:rows]
@@ -303,10 +320,9 @@
     pipelined([first, second, at_group_end(own_grads)])
 
 
-def call(body, lens, args, outs, scratch, matmul_rows, grant, in_hbm=0):
+def call(body, lens, args, outs, scratch, matmul_rows, grant):
     specs = [pl.BlockSpec(memory_space=pltpu.SMEM)] * len(lens)
-    specs += [pl.BlockSpec(memory_space=pltpu.HBM)] * in_hbm
-    specs += [pl.BlockSpec(memory_space=pltpu.VMEM)] * (len(args) - in_hbm)
+    specs += [pl.BlockSpec(memory_space=pltpu.VMEM)] * len(args)
     docs = sum(x.shape[0] for x in lens)
     return pl.pallas_call(
         functools.partial(body, len(lens)),
@@ -347,14 +363,8 @@
     lens = all_lengths(doc_lengths)
     side = swapped(near)
     square = array((rows, HQ * rows), F32)
-    (causal,) = call(causal_kernel, (), (), [array((rows, rows), F32)], [], keys, 1)
-    s_own, dp_own, q, dout, kv = call(
-        products_kernel, (),
-        [pltpu.with_memory_space_constraint(x, pltpu.HBM) for x in (q, dout, kv)],
-        [square, square] + [array(x.shape, BF16) for x in (q, dout, kv)],
-        [pltpu.SemaphoreType.DMA((2, HK)), pltpu.SemaphoreType.DMA(())],
-        2 * rows, 4, in_hbm=3,
-    )
+    (causal,) = call(causal_kernel, (), (), [array((rows, rows), F32)], [], 100 * keys, 1)
+    s_own, dp_own = call(products_kernel, (), (q, dout, kv), [square, square], [], 2 * rows, 4)
     own_stats, p_own = call(
         own_kernel, lens, (s_own, dp_own, causal),
         [array((8, HQ * rows), F32), square], [pltpu.VMEM((rows, rows), F32)], rows, 2,
@@ -362,37 +372,41 @@
     mid_stats, p_mid, dp_mid = exponentials(
         lens, q, dout, (near, side), lambda: offsets_of_moved()[:2]
     )
-    final, ds, g_near, g_side, g_far = call(
-        remote_kernel, lens,
-        (q, dout, far, own_stats, mid_stats, p_mid, dp_mid),
-        [array((8, HQ * rows), F32), array((blocks, HQ * rows), BF16)]
-        + [array((rows, wide), BF16)] * 3,
+    final, ds_far, g_far = call(
+        far_kernel, lens, (q, dout, far, own_stats, mid_stats),
+        [array((8, HQ * rows), F32), array((rows, HQ * rows), BF16), array((rows, wide), BF16)],
         [pltpu.VMEM((rows, rows), F32)]
         + [pltpu.VMEM((SLOTS, rows, 2 * rows), F32)] * 3
         + [pltpu.VMEM((SLOTS, 8, 2 * rows), F32)]
-        + [pltpu.VMEM((2, blocks, GROUP * rows), BF16)],
-        2 * rows + 2 * blocks, 8,
+        + [pltpu.VMEM((2, rows, GROUP * rows), BF16)],
+        4 * rows, 6,
     )
     relayed = moved(g_far, lambda i: -1 if i % 2 else i - 2)
-    side_back = swapped(g_side)
-    chip_back = moved(g_far, lambda i: i - 1 if i % 2 else -1)
-    joined = g_near.astype(F32) + side_back.astype(F32)
-    odd_back = moved(joined.astype(BF16), lambda i: i - 3 if i % 2 else -1)
+    g_near, g_pair, ds_mid = call(
+        mid_kernel, (), (q, dout, p_mid, dp_mid, final, g_far),
+        [
+            array((rows, wide), BF16),
+            array((2 * rows, wide), BF16),
+            array((2 * rows, HQ * rows), BF16),
+        ],
+        [pltpu.VMEM((2, 2 * rows, GROUP * rows), BF16)], 4 * rows, 4,
+    )
+    pair_back = swapped(g_pair)
+    block = array((rows, wide), BF16)
+    (odd_sum,) = call(sum_kernel, (), (g_near, pair_back), [block], [], 1, 1)
+    odd_back = moved(odd_sum, lambda i: i - 3 if i % 2 else -1)
+    (joined,) = call(sum_kernel, (), (g_near, pair_back, relayed), [block], [], 1, 1)
+    even_back = moved(joined, lambda i: -1 if i % 2 else i - 1)
     dq, own = call(
         query_kernel, (),
-        (q, dout, kv, near, side, far, p_own, dp_own, final, ds),
+        (q, dout, kv, near, side, far, p_own, dp_own, final, ds_mid, ds_far),
         [array(q.shape, BF16), array((rows, wide), F32)],
         [pltpu.VMEM((HK, HD, keys), BF16)]
         + [pltpu.VMEM((2, rows, GROUP * rows), BF16)] * 2,
         2 * rows + keys, 6,
     )
-    (joined,) = call(
-        join_kernel, (), (g_near, side_back, relayed),
-        [array((rows, wide), BF16)], [], 1, 1,
-    )
-    even_back = moved(joined, lambda i: -1 if i % 2 else i - 1)
-    total = own + chip_back.astype(F32) + odd_back.astype(F32) + even_back.astype(F32)
-    return (dq[None], total.astype(BF16)[None])
+    (total,) = call(finish_kernel, (), (own, pair_back, odd_back, even_back), [block], [], 1, 3)
+    return (dq[None], total[None])
 
 
 def solution(mesh):

time: 49 us -> 46.4 us (0.947)
  waiting for transfers between devices: 14.4 us -> 17.1 us
  starting transfers between devices: 18.2 us -> 15.5 us
  Pallas kernels: 14.3 us -> 12.7 us
  other arithmetic: 1.01 us -> 0.08 us
    ppermute x8 -> x7, starting transfers between devices: 15.7 us -> 13 us  [moved(): lax.ppermute(value, 'ctx', [(s, t) for s, t in pairs if 0 <= t < count])]
    ppermute x8 -> x7, waiting for transfers between devices: 13.2 us -> 15.9 us  [moved(): lax.ppermute(value, 'ctx', [(s, t) for s, t in pairs if 0 <= t < count])]
    pallas_call x7 -> x10, Pallas kernels: 14.3 us -> 12.7 us  [call(): pl.pallas_call(functools.partial(body, len(lens)), in_specs=specs, out_sp...]
    broadcast_in_dim x1 -> x0, other arithmetic: 0.86 us -> none  [on_device(): return (dq[None], total.astype(BF16)[None])]
  transfers between devices with their start and end apart: 10 -> 9, of which waited for: 3 -> 4; matrix products, arithmetic and copies ran while one was open for 0% -> 0% of each run, Pallas kernels for 20% -> 16%
where the time goes in v5:
time: 46.4 us; the launch traced here: 46.2 us
  waiting for transfers between devices  17.1 us (37%)
  starting transfers between devices  15.5 us (33%)
  Pallas kernels  12.7 us (27%)
  between operations  0.81 us (2%)
    ppermute x7, waiting for transfers between devices, moved(): lax.ppermute(value, 'ctx', [(s, t) for s, t in pairs if 0 <= t < count])  15.9 us
    ppermute x7, starting transfers between devices, moved(): lax.ppermute(value, 'ctx', [(s, t) for s, t in pairs if 0 <= t < count])  13 us
    pallas_call x10, Pallas kernels, call(): pl.pallas_call(functools.partial(body, len(lens)), in_specs=specs, out_sp...  12.7 us
    ppermute x2, starting transfers between devices, all_lengths(): lax.ppermute(jnp.concatenate(pieces), 'pipe', [(i, i ^ stride) for i in r...  2.52 us
    ppermute x2, waiting for transfers between devices, all_lengths(): lax.ppermute(jnp.concatenate(pieces), 'pipe', [(i, i ^ stride) for i in r...  1.18 us
  transfers between devices with their start and end apart: 9, of which 4 were waited for; matrix products, arithmetic and copies ran while one was open for 0% of the time, Pallas kernels for 16%

profile of v5, /device:TPU:1, one launch (start us, length us, event | category | flops | bytes accessed | tf_op | source)
XLA Modules:
  0.0 46.2 jit_solution(7481576790416463540)
XLA Ops:
  0.6 0.0 copy-start
  0.6 0.0 copy-start.1
  0.6 0.0 copy-start.2
  0.7 4.7 %collective-permute-start = (bf16[128,1024]{1,0:T(8,128)(2,1)}, bf16[128,1024]{1,0:T(8,128)(2,1)S(1)}, u32[]{:S(2)}, u32[]{:S(2)}) collective-permute-start(bf16[128,1024]{1,0:T(8,128)(2,1)} %bitcast.15), channel_id=1, source_target_pairs={{0,3},{1,2},{2,5},{3,4},{4,7},{5,6},{8,11},{9,10},{10,13},{11,12},... | collective-permute-start | bytes 786440 | tf_op jit(solution)/shard_map/ppermute | solution.py:31
  5.4 3.9 %collective-permute-start.2 = (bf16[128,1024]{1,0:T(8,128)(2,1)}, bf16[128,1024]{1,0:T(8,128)(2,1)S(1)}, u32[]{:S(2)}, u32[]{:S(2)}) collective-permute-start(bf16[128,1024]{1,0:T(8,128)(2,1)} %bitcast.16), channel_id=1, source_target_pairs={{0,1},{1,4},{2,3},{3,6},{4,5},{6,7},{8,9},{9,12},{10,11},{11,14},{... | collective-permute-start | bytes 786440 | tf_op jit(solution)/shard_map/ppermute | solution.py:31
  9.3 1.3 %collective-permute-start.3 = (s32[2]{0:T(128)}, s32[2]{0:T(128)S(1)}, u32[]{:S(2)}, u32[]{:S(2)}) collective-permute-start(s32[2]{0:T(128)} %refs_0_.5), channel_id=1, source_target_pairs={{0,8},{8,0},{16,24},{24,16},{1,9},{9,1},{17,25},{25,17},{2,10},{10... | collective-permute-start | bytes 32 | tf_op jit(solution)/shard_map/ppermute | solution.py:51
  10.6 1.2 %collective-permute-done.refs_5_.refs_3_ = bf16[128,1024]{1,0:T(8,128)(2,1)S(1)} collective-permute-done((bf16[128,1024]{1,0:T(8,128)(2,1)}, bf16[128,1024]{1,0:T(8,128)(2,1)S(1)}, u32[]{:S(2)}, u32[]{:S(2)}) %collective-permute-start) | collective-permute-done | bytes 262176 | tf_op jit(solution)/shard_map/ppermute | solution.py:31
  11.8 0.4 collective-permute-start.1
  12.2 0.0 copy-start.3
  12.2 0.0 copy-done
  12.2 0.0 copy-done.1
  12.3 0.0 copy-done.2
  12.3 0.7 %shard_map.59 = (f32[128,4096]{1,0:T(8,128)S(1)}, f32[128,4096]{1,0:T(8,128)S(1)}) custom-call(bf16[128,4096]{1,0:T(8,128)(2,1)S(1)} %bitcast.5, bf16[128,4096]{1,0:T(8,128)(2,1)S(1)} %bitcast.10, bf16[128,1024]{1,0:T(8,128)(2,1)S(1)} %bitcast.17), custom_call_target="tpu_custom_call" | custom-call | flops 268435456 | bytes 6553600 | tf_op jit(solution)/shard_map/pallas_call | solution.py:327
  13.0 0.0 collective-permute-done.3.refs_1_
  13.0 0.0 copy-done.3
  13.0 0.1 pad_add_fusion
  13.1 1.2 %collective-permute-start.4 = (s32[4]{0:T(128)S(1)}, s32[4]{0:T(128)S(1)}, u32[]{:S(2)}, u32[]{:S(2)}) collective-permute-start(s32[4]{0:T(128)S(1)} %pad_add_fusion), channel_id=1, source_target_pairs={{0,16},{8,24},{16,0},{24,8},{1,17},{9,25},{17,1},{25,9},{2,18},{10... | collective-permute-start | bytes 56 | tf_op jit(solution)/shard_map/ppermute | solution.py:51
  14.3 1.2 %collective-permute-done.4.refs_2_ = s32[4]{0:T(128)S(1)} collective-permute-done((s32[4]{0:T(128)S(1)}, s32[4]{0:T(128)S(1)}, u32[]{:S(2)}, u32[]{:S(2)}) %collective-permute-start.4) | collective-permute-done | bytes 48 | tf_op jit(solution)/shard_map/ppermute | solution.py:51
  15.5 1.3 %shard_map.61 = (f32[8,4096]{1,0:T(8,128)S(1)}, f32[128,4096]{1,0:T(8,128)S(1)}) custom-call(s32[2]{0:T(128)S(1)} %copy-done.3, s32[2]{0:T(128)S(1)} %collective-permute-done.3.refs_1_, s32[4]{0:T(128)S(1)} %collective-permute-done.4.refs_2_, f32[128,4096]{1,0:T(8,128)S(1)} %get-tuple-element.17.refs_3_, f32[128,4096]{1,0:T(8,128)S(1)} %get-tuple-element.18.refs_4_.refs_7_, ...), custom_call_target="tpu_custom_call" | custom-call | flops 134217728 | bytes 6488064 | tf_op jit(solution)/shard_map/pallas_call | solution.py:327
  16.8 0.0 collective-permute-done.1.refs_6_.refs_4_
  16.8 2.9 %shard_map.62 = (f32[8,4096]{1,0:T(8,128)S(1)}, f32[256,4096]{1,0:T(8,128)S(1)}, f32[256,4096]{1,0:T(8,128)S(1)}) custom-call(s32[2]{0:T(128)S(1)} %copy-done.3, s32[2]{0:T(128)S(1)} %collective-permute-done.3.refs_1_, s32[4]{0:T(128)S(1)} %collective-permute-done.4.refs_2_, bf16[128,4096]{1,0:T(8,128)(2,1)S(1)} %bitcast.6, bf16[128,4096]{1,0:T(8,128)(2,1)S(1)} %bitcast.11, ...), custom_call_target="tpu_custom_call" | custom-call | flops 536870912 | bytes 11141120 | tf_op jit(solution)/shard_map/pallas_call | solution.py:327
  19.7 0.0 collective-permute-done.2.refs_5_
  19.7 2.7 %shard_map.63 = (f32[8,4096]{1,0:T(8,128)S(1)}, bf16[128,4096]{1,0:T(8,128)(2,1)S(1)}, bf16[128,1024]{1,0:T(8,128)(2,1)S(1)}) custom-call(s32[2]{0:T(128)S(1)} %copy-done.3, s32[2]{0:T(128)S(1)} %collective-permute-done.3.refs_1_, s32[4]{0:T(128)S(1)} %collective-permute-done.4.refs_2_, bf16[128,4096]{1,0:T(8,128)(2,1)S(1)} %bitcast.7, ...), custom_call_target="tpu_custom_call" | custom-call | flops 536870912 | bytes 4063232 | tf_op jit(solution)/shard_map/pallas_call | solution.py:327
  22.4 1.6 %shard_map.64 = (bf16[128,1024]{1,0:T(8,128)(2,1)S(1)}, bf16[256,1024]{1,0:T(8,128)(2,1)S(1)}, bf16[256,4096]{1,0:T(8,128)(2,1)S(1)}) custom-call(bf16[128,4096]{1,0:T(8,128)(2,1)S(1)} %bitcast.8, bf16[128,4096]{1,0:T(8,128)(2,1)S(1)} %bitcast.13, f32[256,4096]{1,0:T(8,128)S(1)} %get-tuple-element.23.refs_2_, f32[256,4096]{1,0:T(8,128)S(1)} %get-tuple-element.24.refs_3_, ...), custom_call_target="tpu_custom_call" | custom-call | flops 536870912 | bytes 13762560 | tf_op jit(solution)/shard_map/pallas_call | solution.py:327
  24.1 1.3 %collective-permute-start.5 = (bf16[256,1024]{1,0:T(8,128)(2,1)S(1)}, bf16[256,1024]{1,0:T(8,128)(2,1)S(1)}, u32[]{:S(2)}, u32[]{:S(2)}) collective-permute-start(bf16[256,1024]{1,0:T(8,128)(2,1)S(1)} %get-tuple-element.30), channel_id=1, source_target_pairs={{0,1},{1,0},{2,3},{3,2},{4,5},{5,4},{6,7},{7,6},{8,9},{9,8},{10,11... | collective-permute-start | bytes 1572872 | tf_op jit(solution)/shard_map/ppermute | solution.py:31
  25.3 0.7 %collective-permute-start.7 = (bf16[128,1024]{1,0:T(8,128)(2,1)S(1)}, bf16[128,1024]{1,0:T(8,128)(2,1)S(1)}, u32[]{:S(2)}, u32[]{:S(2)}) collective-permute-start(bf16[128,1024]{1,0:T(8,128)(2,1)S(1)} %get-tuple-element.25.refs_5_), channel_id=1, source_target_pairs={{2,0},{4,2},{6,4},{10,8},{12,10},{14,12},{18,16},{20,18},{22,20},{... | collective-permute-start | bytes 786440 | tf_op jit(solution)/shard_map/ppermute | solution.py:31
  26.0 0.9 %collective-permute-done.5.pair_ref = bf16[256,1024]{1,0:T(8,128)(2,1)S(1)} collective-permute-done((bf16[256,1024]{1,0:T(8,128)(2,1)S(1)}, bf16[256,1024]{1,0:T(8,128)(2,1)S(1)}, u32[]{:S(2)}, u32[]{:S(2)}) %collective-permute-start.5) | collective-permute-done | bytes 524320 | tf_op jit(solution)/shard_map/ppermute | solution.py:31
  26.9 0.1 shard_map.66
  27.0 0.7 %collective-permute-start.6 = (bf16[128,1024]{1,0:T(8,128)(2,1)S(1)}, bf16[128,1024]{1,0:T(8,128)(2,1)S(1)}, u32[]{:S(2)}, u32[]{:S(2)}) collective-permute-start(bf16[128,1024]{1,0:T(8,128)(2,1)S(1)} %shard_map.66), channel_id=1, source_target_pairs={{3,0},{5,2},{7,4},{11,8},{13,10},{15,12},{19,16},{21,18},{23,20},{... | collective-permute-start | bytes 786440 | tf_op jit(solution)/shard_map/ppermute | solution.py:31
  27.6 0.0 collective-permute-done.7.refs_0_
  27.6 0.1 shard_map.67
  27.8 1.3 %collective-permute-start.8 = (bf16[128,1024]{1,0:T(8,128)(2,1)S(1)}, bf16[128,1024]{1,0:T(8,128)(2,1)S(1)}, u32[]{:S(2)}, u32[]{:S(2)}) collective-permute-start(bf16[128,1024]{1,0:T(8,128)(2,1)S(1)} %shard_map.67), channel_id=1, source_target_pairs={{2,1},{4,3},{6,5},{10,9},{12,11},{14,13},{18,17},{20,19},{22,21},{... | collective-permute-start | bytes 786440 | tf_op jit(solution)/shard_map/ppermute | solution.py:31
  29.1 2.5 %shard_map.65 = (bf16[128,4096]{1,0:T(8,128)(2,1)}, f32[128,1024]{1,0:T(8,128)S(1)}) custom-call(bf16[128,4096]{1,0:T(8,128)(2,1)S(1)} %bitcast.9, bf16[128,4096]{1,0:T(8,128)(2,1)S(1)} %bitcast.14, bf16[128,1024]{1,0:T(8,128)(2,1)S(1)} %bitcast.18, bf16[128,1024]{1,0:T(8,128)(2,1)S(1)} %collective-permute-done.refs_5_.refs_3_, ...), custom_call_target="tpu_custom_call" | custom-call | flops 805306368 | bytes 12189696 | tf_op jit(solution)/shard_map/pallas_call | solution.py:327
  31.5 0.0 collective-permute-done.6.odd_ref
  31.5 13.9 %collective-permute-done.8.even_ref = bf16[128,1024]{1,0:T(8,128)(2,1)S(1)} collective-permute-done((bf16[128,1024]{1,0:T(8,128)(2,1)S(1)}, bf16[128,1024]{1,0:T(8,128)(2,1)S(1)}, u32[]{:S(2)}, u32[]{:S(2)}) %collective-permute-start.8) | collective-permute-done | bytes 262176 | tf_op jit(solution)/shard_map/ppermute | solution.py:31
  45.4 0.8 %shard_map.68 = bf16[128,1024]{1,0:T(8,128)(2,1)} custom-call(f32[128,1024]{1,0:T(8,128)S(1)} %get-tuple-element.29.own_ref, bf16[256,1024]{1,0:T(8,128)(2,1)S(1)} %collective-permute-done.5.pair_ref, bf16[128,1024]{1,0:T(8,128)(2,1)S(1)} %collective-permute-done.6.odd_ref, bf16[128,1024]{1,0:T(8,128)(2,1)S(1)} %collective-permute-done.8.even_ref), custom_call_target="tpu_custom_call" | custom-call | flops 1048576 | bytes 1835008 | tf_op jit(solution)/shard_map/pallas_call | solution.py:327
  (1 shorter events, 0.0 us)
Async XLA Ops:
  0.6 11.6 %copy-start = (bf16[1,128,4096]{2,1,0:T(8,128)(2,1)S(1)}, bf16[1,128,4096]{2,1,0:T(8,128)(2,1)}, u32[]{:S(2)}) copy-start(bf16[1,128,4096]{2,1,0:T(8,128)(2,1)} %param.4) | copy-start | bytes 3145732
  0.6 11.6 %copy-start.1 = (bf16[1,128,4096]{2,1,0:T(8,128)(2,1)S(1)}, bf16[1,128,4096]{2,1,0:T(8,128)(2,1)}, u32[]{:S(2)}) copy-start(bf16[1,128,4096]{2,1,0:T(8,128)(2,1)} %param.6) | copy-start | bytes 3145732
  0.6 11.6 %copy-start.2 = (bf16[1,128,1024]{2,1,0:T(8,128)(2,1)S(1)}, bf16[1,128,1024]{2,1,0:T(8,128)(2,1)}, u32[]{:S(2)}) copy-start(bf16[1,128,1024]{2,1,0:T(8,128)(2,1)} %param.5) | copy-start | bytes 786436
  0.7 11.1 %collective-permute-start = (bf16[128,1024]{1,0:T(8,128)(2,1)}, bf16[128,1024]{1,0:T(8,128)(2,1)S(1)}, u32[]{:S(2)}, u32[]{:S(2)}) collective-permute-start(bf16[128,1024]{1,0:T(8,128)(2,1)} %bitcast.15), channel_id=1, source_target_pairs={{0,3},{1,2},{2,5},{3,4},{4,7},{5,6},{8,11},{9,10},{10,13},{11,12},... | collective-permute-start | bytes 786440 | tf_op jit(solution)/shard_map/ppermute | solution.py:31
  5.4 14.3 %collective-permute-start.2 = (bf16[128,1024]{1,0:T(8,128)(2,1)}, bf16[128,1024]{1,0:T(8,128)(2,1)S(1)}, u32[]{:S(2)}, u32[]{:S(2)}) collective-permute-start(bf16[128,1024]{1,0:T(8,128)(2,1)} %bitcast.16), channel_id=1, source_target_pairs={{0,1},{1,4},{2,3},{3,6},{4,5},{6,7},{8,9},{9,12},{10,11},{11,14},{... | collective-permute-start | bytes 786440 | tf_op jit(solution)/shard_map/ppermute | solution.py:31
  9.3 3.7 %collective-permute-start.3 = (s32[2]{0:T(128)}, s32[2]{0:T(128)S(1)}, u32[]{:S(2)}, u32[]{:S(2)}) collective-permute-start(s32[2]{0:T(128)} %refs_0_.5), channel_id=1, source_target_pairs={{0,8},{8,0},{16,24},{24,16},{1,9},{9,1},{17,25},{25,17},{2,10},{10... | collective-permute-start | bytes 32 | tf_op jit(solution)/shard_map/ppermute | solution.py:51
  11.8 5.0 %collective-permute-start.1 = (bf16[128,1024]{1,0:T(8,128)(2,1)S(1)}, bf16[128,1024]{1,0:T(8,128)(2,1)S(1)}, u32[]{:S(2)}, u32[]{:S(2)}) collective-permute-start(bf16[128,1024]{1,0:T(8,128)(2,1)S(1)} %collective-permute-done.refs_5_.refs_3_), channel_id=1, source_target_pairs={{0,1},{1,0},{2,3},{3,2},{4,5},{5,4},{6,7},{7,6},{8,9},{9,8},{10,11... | collective-permute-start | bytes 786440 | tf_op jit(solution)/shard_map/ppermute | solution.py:31
  12.2 0.8 %copy-start.3 = (s32[2]{0:T(128)S(1)}, s32[2]{0:T(128)}, u32[]{:S(2)}) copy-start(s32[2]{0:T(128)} %refs_0_.5) | copy-start | bytes 28
  13.1 2.4 %collective-permute-start.4 = (s32[4]{0:T(128)S(1)}, s32[4]{0:T(128)S(1)}, u32[]{:S(2)}, u32[]{:S(2)}) collective-permute-start(s32[4]{0:T(128)S(1)} %pad_add_fusion), channel_id=1, source_target_pairs={{0,16},{8,24},{16,0},{24,8},{1,17},{9,25},{17,1},{25,9},{2,18},{10... | collective-permute-start | bytes 56 | tf_op jit(solution)/shard_map/ppermute | solution.py:51
  24.1 2.8 %collective-permute-start.5 = (bf16[256,1024]{1,0:T(8,128)(2,1)S(1)}, bf16[256,1024]{1,0:T(8,128)(2,1)S(1)}, u32[]{:S(2)}, u32[]{:S(2)}) collective-permute-start(bf16[256,1024]{1,0:T(8,128)(2,1)S(1)} %get-tuple-element.30), channel_id=1, source_target_pairs={{0,1},{1,0},{2,3},{3,2},{4,5},{5,4},{6,7},{7,6},{8,9},{9,8},{10,11... | collective-permute-start | bytes 1572872 | tf_op jit(solution)/shard_map/ppermute | solution.py:31
  25.3 2.3 %collective-permute-start.7 = (bf16[128,1024]{1,0:T(8,128)(2,1)S(1)}, bf16[128,1024]{1,0:T(8,128)(2,1)S(1)}, u32[]{:S(2)}, u32[]{:S(2)}) collective-permute-start(bf16[128,1024]{1,0:T(8,128)(2,1)S(1)} %get-tuple-element.25.refs_5_), channel_id=1, source_target_pairs={{2,0},{4,2},{6,4},{10,8},{12,10},{14,12},{18,16},{20,18},{22,20},{... | collective-permute-start | bytes 786440 | tf_op jit(solution)/shard_map/ppermute | solution.py:31
  27.0 4.6 %collective-permute-start.6 = (bf16[128,1024]{1,0:T(8,128)(2,1)S(1)}, bf16[128,1024]{1,0:T(8,128)(2,1)S(1)}, u32[]{:S(2)}, u32[]{:S(2)}) collective-permute-start(bf16[128,1024]{1,0:T(8,128)(2,1)S(1)} %shard_map.66), channel_id=1, source_target_pairs={{3,0},{5,2},{7,4},{11,8},{13,10},{15,12},{19,16},{21,18},{23,20},{... | collective-permute-start | bytes 786440 | tf_op jit(solution)/shard_map/ppermute | solution.py:31
  27.8 17.6 %collective-permute-start.8 = (bf16[128,1024]{1,0:T(8,128)(2,1)S(1)}, bf16[128,1024]{1,0:T(8,128)(2,1)S(1)}, u32[]{:S(2)}, u32[]{:S(2)}) collective-permute-start(bf16[128,1024]{1,0:T(8,128)(2,1)S(1)} %shard_map.67), channel_id=1, source_target_pairs={{2,1},{4,3},{6,5},{10,9},{12,11},{14,13},{18,17},{20,19},{22,21},{... | collective-permute-start | bytes 786440 | tf_op jit(solution)/shard_map/ppermute | solution.py:31

commit v6 on v5

--- a/solution.py
+++ b/solution.py
@@ -54,32 +54,35 @@
     return pieces
 
 
-def fill_bias(lens_refs, starts_scr, bias_scr, offsets, rows, base=None):
-    here = lax.axis_index("ctx")
+def positions(rows):
+    return lax.axis_index("ctx") * rows + lax.broadcasted_iota(jnp.int32, (1, rows), 1)
+
+
+def find_doc_starts(lens_refs, starts_scr, rows):
     pipe = lax.axis_index("pipe")
-    t_pos = here * rows + lax.broadcasted_iota(jnp.int32, (1, rows), 1)
+    t_pos = positions(rows)
     per_pipe = lens_refs[0].shape[0]
     place = 0
     for ref in lens_refs:
         for k in range(ref.shape[0]):
             starts_scr[((place // per_pipe) ^ pipe) * per_pipe + place % per_pipe] = ref[k]
             place += 1
-
-    def step(d, carry):
-        start, doc_start = carry
+    start, doc_start = jnp.int32(0), jnp.zeros((1, rows), jnp.int32)
+    for d in range(place):
         doc_start = jnp.where(t_pos >= start, start, doc_start)
-        return start + starts_scr[d], doc_start
-
-    _, doc_start = lax.fori_loop(0, place, step, (jnp.int32(0), jnp.zeros((1, rows), jnp.int32)))
-    for b, offset in enumerate(offsets):
-        u_pos = (here - offset) * rows + lax.broadcasted_iota(jnp.int32, (rows, rows), 0)
-        kept = 0.0 if base is None else base
-        bias_scr[at(b, rows)] = jnp.where(u_pos >= doc_start, kept, -1e30).astype(F32)
-
-
-def offsets_of_moved():
-    odd = lax.rem(lax.axis_index("ctx"), 2)
-    return (1 + 2 * odd, 2, 3 - 2 * odd)
+        start = start + starts_scr[d]
+    return doc_start
+
+
+def bias_of(doc_start, offset, base):
+    rows = doc_start.shape[1]
+    u_pos = (lax.axis_index("ctx") - offset) * rows
+    u_pos = u_pos + lax.broadcasted_iota(jnp.int32, (rows, rows), 0)
+    return jnp.where(u_pos >= doc_start, base, -1e30).astype(F32)
+
+
+def is_odd():
+    return lax.rem(lax.axis_index("ctx"), 2)
 
 
 def at(i, width):
@@ -90,26 +93,21 @@
     return jnp.concatenate([ref[:, at(first + k, HD)] for k in range(count)], axis=0)
 
 
-def tall(refs, column):
-    return jnp.concatenate([ref[:, at(column, HD)] for ref in refs], axis=0)
-
-
-def keys_of(refs, i):
-    return tall(refs, i // PER_GROUP)
-
-
-def values_of(refs, i):
-    return tall(refs, HK + i // PER_GROUP)
-
-
-def scores_of(refs, q_ref, bias_scr, i):
-    s = lax.dot_general(keys_of(refs, i), stacked(q_ref, 2 * i, 2), NT, preferred_element_type=F32)
-    bias = bias_scr[...]
-    return s + jnp.concatenate([bias, bias], axis=1)
-
-
-def dweights_of(refs, d_ref, i):
-    return lax.dot_general(values_of(refs, i), stacked(d_ref, 2 * i, 2), NT, preferred_element_type=F32)
+def scores_of(kv_ref, q_ref, i):
+    return lax.dot_general(
+        kv_ref[:, at(i // PER_GROUP, HD)], stacked(q_ref, 2 * i, 2), NT, preferred_element_type=F32
+    )
+
+
+def dweights_of(kv_ref, d_ref, i):
+    return lax.dot_general(
+        kv_ref[:, at(HK + i // PER_GROUP, HD)], stacked(d_ref, 2 * i, 2), NT,
+        preferred_element_type=F32,
+    )
+
+
+def twice(value):
+    return jnp.concatenate([value, value], axis=1)
 
 
 def pipelined(stages):
@@ -127,39 +125,11 @@
     return stage
 
 
-def exponentials_kernel(n_lens, n_blocks, offsets_of, *refs):
-    lens_refs, refs = refs[:n_lens], refs[n_lens:]
-    q_ref, d_ref = refs[:2]
-    kv_refs, (stats_ref, p_ref, dp_ref) = refs[2:2 + n_blocks], refs[2 + n_blocks:5 + n_blocks]
-    starts_scr, bias_scr, s_scr = refs[5 + n_blocks:]
-    rows = q_ref.shape[0]
-    fill_bias(lens_refs, starts_scr, bias_scr, offsets_of(), rows)
-
-    def first(i):
-        s_scr[i % SLOTS] = scores_of(kv_refs, q_ref, bias_scr, i)
-        dp_ref[:, at(i, 2 * rows)] = dweights_of(kv_refs, d_ref, i)
-
-    def second(i):
-        column = at(i, 2 * rows)
-        s = s_scr[i % SLOTS]
-        top = jnp.max(s, axis=0, keepdims=True)
-        p = jnp.exp2((s - top) * RATE)
-        p_ref[:, column] = p
-        stats_ref[0:1, column] = top
-        stats_ref[1:2, column] = jnp.sum(p, axis=0, keepdims=True)
-        stats_ref[2:3, column] = jnp.sum(p * dp_ref[:, column], axis=0, keepdims=True)
-
-    pipelined([first, second])
-
-
 def products_kernel(n_lens, q_ref, d_ref, kv_ref, s_ref, dp_ref):
     rows = q_ref.shape[0]
     for i in range(PAIRS):
-        column = at(i, 2 * rows)
-        s_ref[:, column] = lax.dot_general(
-            keys_of([kv_ref], i), stacked(q_ref, 2 * i, 2), NT, preferred_element_type=F32
-        )
-        dp_ref[:, column] = dweights_of([kv_ref], d_ref, i)
+        s_ref[:, at(i, 2 * rows)] = scores_of(kv_ref, q_ref, i)
+        dp_ref[:, at(i, 2 * rows)] = dweights_of(kv_ref, d_ref, i)
 
 
 def causal_kernel(n_lens, causal_ref):
@@ -168,52 +138,76 @@
     causal_ref[...] = jnp.where(u <= t, 0.0, -1e30).astype(F32)
 
 
+def keep_exponentials(s, dp, column, stats_ref, p_ref):
+    top = jnp.max(s, axis=0, keepdims=True)
+    p = jnp.exp2((s - top) * RATE)
+    p_ref[:, column] = p
+    stats_ref[0:1, column] = top
+    stats_ref[1:2, column] = jnp.sum(p, axis=0, keepdims=True)
+    stats_ref[2:3, column] = jnp.sum(p * dp, axis=0, keepdims=True)
+
+
 def own_kernel(n_lens, *refs):
     lens_refs, refs = refs[:n_lens], refs[n_lens:]
-    s_ref, dp_ref, causal_ref, stats_ref, p_ref, starts_scr, bias_scr = refs
+    s_ref, dp_ref, causal_ref, stats_ref, p_ref, docs_ref, starts_scr, bias_scr = refs
     rows = s_ref.shape[0]
-    fill_bias(lens_refs, starts_scr, bias_scr, (0,), rows, causal_ref[...])
+    doc_start = find_doc_starts(lens_refs, starts_scr, rows)
+    docs_ref[0:1] = doc_start
+    bias_scr[...] = bias_of(doc_start, 0, causal_ref[...])
     for i in range(PAIRS):
         column = at(i, 2 * rows)
-        s = s_ref[:, column] + jnp.concatenate([bias_scr[...]] * 2, axis=1)
-        top = jnp.max(s, axis=0, keepdims=True)
-        p = jnp.exp2((s - top) * RATE)
-        p_ref[:, column] = p
-        stats_ref[0:1, column] = top
-        stats_ref[1:2, column] = jnp.sum(p, axis=0, keepdims=True)
-        stats_ref[2:3, column] = jnp.sum(p * dp_ref[:, column], axis=0, keepdims=True)
+        s = s_ref[:, column] + twice(bias_scr[...])
+        keep_exponentials(s, dp_ref[:, column], column, stats_ref, p_ref)
+
+
+def block_kernel(offset_of, n_lens, *refs):
+    docs_ref, q_ref, d_ref, kv_ref, stats_ref, p_ref, dp_ref, bias_scr, s_scr = refs
+    rows = q_ref.shape[0]
+    bias_scr[...] = bias_of(docs_ref[0:1], offset_of(), 0.0)
+
+    def first(i):
+        s_scr[i % SLOTS] = scores_of(kv_ref, q_ref, i) + twice(bias_scr[...])
+        dp_ref[:, at(i, 2 * rows)] = dweights_of(kv_ref, d_ref, i)
+
+    def second(i):
+        column = at(i, 2 * rows)
+        keep_exponentials(s_scr[i % SLOTS], dp_ref[:, column], column, stats_ref, p_ref)
+
+    pipelined([first, second])
 
 
 def far_kernel(n_lens, *refs):
-    lens_refs, refs = refs[:n_lens], refs[n_lens:]
-    q_ref, d_ref, kv_ref, own_ref, mid_ref = refs[:5]
-    final_ref, ds_ref, g_ref = refs[5:8]
-    starts_scr, bias_scr, s_scr, dp_scr, p_scr, row_scr, w_scr = refs[8:]
+    docs_ref, q_ref, d_ref, kv_ref = refs[:4]
+    stats_refs = refs[4:7]
+    final_ref, ds_ref, g_ref = refs[7:10]
+    bias_scr, s_scr, dp_scr, p_scr, row_scr, w_scr = refs[10:]
     rows = q_ref.shape[0]
-    fill_bias(lens_refs, starts_scr, bias_scr, offsets_of_moved()[2:], rows)
+    bias_scr[...] = bias_of(docs_ref[0:1], 3 - 2 * is_odd(), 0.0)
 
     def first(i):
-        s_scr[i % SLOTS] = scores_of([kv_ref], q_ref, bias_scr, i)
-        dp_scr[i % SLOTS] = dweights_of([kv_ref], d_ref, i)
+        s_scr[i % SLOTS] = scores_of(kv_ref, q_ref, i) + twice(bias_scr[...])
+        dp_scr[i % SLOTS] = dweights_of(kv_ref, d_ref, i)
 
     def second(i):
         column = at(i, 2 * rows)
-        s, dp = s_scr[i % SLOTS], dp_scr[i % SLOTS]
-        own_top, mid_top = own_ref[0:1, column], mid_ref[0:1, column]
-        top = jnp.maximum(jnp.max(s, axis=0, keepdims=True), jnp.maximum(own_top, mid_top))
+        s = s_scr[i % SLOTS]
+        tops = [ref[0:1, column] for ref in stats_refs]
+        top = functools.reduce(jnp.maximum, tops, jnp.max(s, axis=0, keepdims=True))
         p = jnp.exp2((s - top) * RATE)
         p_scr[i % SLOTS] = p
-        own = jnp.exp2((own_top - top) * RATE)
-        other = jnp.exp2((mid_top - top) * RATE)
-        total = own_ref[1:2, column] * own + mid_ref[1:2, column] * other
-        dot = own_ref[2:3, column] * own + mid_ref[2:3, column] * other
-        inv = 1.0 / (total + jnp.sum(p, axis=0, keepdims=True))
-        delta = (dot + jnp.sum(p * dp, axis=0, keepdims=True)) * inv
+        total = jnp.sum(p, axis=0, keepdims=True)
+        dot = jnp.sum(p * dp_scr[i % SLOTS], axis=0, keepdims=True)
+        shares = [jnp.exp2((block_top - top) * RATE) for block_top in tops]
+        for ref, share in zip(stats_refs, shares):
+            total = total + ref[1:2, column] * share
+            dot = dot + ref[2:3, column] * share
+        inv = 1.0 / total
+        delta = dot * inv
         row_scr[i % SLOTS, 0:1] = inv
         row_scr[i % SLOTS, 1:2] = delta
-        final_ref[0:1, column] = own * inv
-        final_ref[1:2, column] = delta
-        final_ref[2:3, column] = other * inv
+        final_ref[0:1, column] = delta
+        for k, share in enumerate(shares):
+            final_ref[k + 1:k + 2, column] = share * inv
 
     def third(i):
         w = p_scr[i % SLOTS] * row_scr[i % SLOTS, 0:1]
@@ -236,15 +230,18 @@
 
 
 def mid_kernel(n_lens, *refs):
-    q_ref, d_ref, p_ref, dp_ref, final_ref, far_ref, near_ref, pair_ref, ds_ref, w_scr = refs
+    q_ref, d_ref, p1_ref, dp1_ref, p2_ref, dp2_ref, final_ref, far_ref = refs[:8]
+    near_ref, pair_ref, ds_ref, w_scr = refs[8:]
     rows = q_ref.shape[0]
     pair_ref[rows:] = far_ref[...]
 
     def first(i):
         column = at(i, 2 * rows)
-        w = p_ref[:, column] * final_ref[2:3, column]
-        ds_ref[:, column] = (w * (dp_ref[:, column] - final_ref[1:2, column])).astype(BF16)
-        w_scr[i // PER_GROUP % 2, :, at(i % PER_GROUP, 2 * rows)] = w.astype(BF16)
+        for b, (p_ref, dp_ref) in enumerate(((p1_ref, dp1_ref), (p2_ref, dp2_ref))):
+            w = p_ref[:, column] * final_ref[b + 2:b + 3, column]
+            ds = (w * (dp_ref[:, column] - final_ref[0:1, column])).astype(BF16)
+            ds_ref[at(b, rows), column] = ds
+            w_scr[i // PER_GROUP % 2, at(b, rows), at(i % PER_GROUP, 2 * rows)] = w.astype(BF16)
 
     def key_grads(group):
         dk = lax.dot_general(
@@ -294,8 +291,8 @@
                 kt_scr[group, :, at(b, rows)] = ref[:, at(group, HD)].T
         column = at(i, 2 * rows)
         half, part = group % 2, at(i % PER_GROUP, 2 * rows)
-        w = p_ref[:, column] * final_ref[0:1, column]
-        ds_scr[half, :, part] = (w * (dp_ref[:, column] - final_ref[1:2, column])).astype(BF16)
+        w = p_ref[:, column] * final_ref[1:2, column]
+        ds_scr[half, :, part] = (w * (dp_ref[:, column] - final_ref[0:1, column])).astype(BF16)
         w_scr[half, :, part] = w.astype(BF16)
 
     def second(i):
@@ -339,42 +336,40 @@
     )(*lens, *args)
 
 
-def exponentials(lens, q, dout, kvs, offsets_of):
-    rows = q.shape[0]
-    tall_rows = len(kvs) * rows
-    array = jax.ShapeDtypeStruct
-    return call(
-        lambda n_lens, *refs: exponentials_kernel(n_lens, len(kvs), offsets_of, *refs),
-        lens, (q, dout) + tuple(kvs),
-        [array((8, HQ * rows), F32)] + [array((tall_rows, HQ * rows), F32)] * 2,
-        [pltpu.VMEM((tall_rows, rows), F32), pltpu.VMEM((SLOTS, tall_rows, 2 * rows), F32)],
-        2 * tall_rows, 4,
-    )
-
-
 def on_device(queries, keys_values, out_grads, doc_lengths):
     kv, q, dout = keys_values[0], queries[0], out_grads[0]
     rows, wide = kv.shape
+    keys = (REACH + 1) * rows
     array = jax.ShapeDtypeStruct
-    blocks = REACH * rows
-    keys = blocks + rows
+    block = array((rows, wide), BF16)
+    square = array((rows, HQ * rows), F32)
+    stat = array((8, HQ * rows), F32)
+
+    def exponentials(block_kv, offset_of):
+        return call(
+            functools.partial(block_kernel, offset_of), (), (docs, q, dout, block_kv),
+            [stat, square, square],
+            [pltpu.VMEM((rows, rows), F32), pltpu.VMEM((SLOTS, rows, 2 * rows), F32)],
+            2 * rows, 4,
+        )
+
     near = one_three(kv)
     far = three_one(kv)
     lens = all_lengths(doc_lengths)
-    side = swapped(near)
-    square = array((rows, HQ * rows), F32)
     (causal,) = call(causal_kernel, (), (), [array((rows, rows), F32)], [], 100 * keys, 1)
     s_own, dp_own = call(products_kernel, (), (q, dout, kv), [square, square], [], 2 * rows, 4)
-    own_stats, p_own = call(
+    own_stats, p_own, docs = call(
         own_kernel, lens, (s_own, dp_own, causal),
-        [array((8, HQ * rows), F32), square], [pltpu.VMEM((rows, rows), F32)], rows, 2,
-    )
-    mid_stats, p_mid, dp_mid = exponentials(
-        lens, q, dout, (near, side), lambda: offsets_of_moved()[:2]
-    )
+        [stat, square, array((8, rows), jnp.int32)], [pltpu.VMEM((rows, rows), F32)],
+        rows, 2,
+    )
+    side = swapped(near)
+    near_stats, p_near, dp_near = exponentials(near, lambda: 1 + 2 * is_odd())
+    side_stats, p_side, dp_side = exponentials(side, lambda: 2)
     final, ds_far, g_far = call(
-        far_kernel, lens, (q, dout, far, own_stats, mid_stats),
-        [array((8, HQ * rows), F32), array((rows, HQ * rows), BF16), array((rows, wide), BF16)],
+        far_kernel, (),
+        (docs, q, dout, far, own_stats, near_stats, side_stats),
+        [stat, array((rows, HQ * rows), BF16), block],
         [pltpu.VMEM((rows, rows), F32)]
         + [pltpu.VMEM((SLOTS, rows, 2 * rows), F32)] * 3
         + [pltpu.VMEM((SLOTS, 8, 2 * rows), F32)]
@@ -383,16 +378,16 @@
     )
     relayed = moved(g_far, lambda i: -1 if i % 2 else i - 2)
     g_near, g_pair, ds_mid = call(
-        mid_kernel, (), (q, dout, p_mid, dp_mid, final, g_far),
+        mid_kernel, (),
+        (q, dout, p_near, dp_near, p_side, dp_side, final, g_far),
         [
-            array((rows, wide), BF16),
+            block,
             array((2 * rows, wide), BF16),
             array((2 * rows, HQ * rows), BF16),
         ],
         [pltpu.VMEM((2, 2 * rows, GROUP * rows), BF16)], 4 * rows, 4,
     )
     pair_back = swapped(g_pair)
-    block = array((rows, wide), BF16)
     (odd_sum,) = call(sum_kernel, (), (g_near, pair_back), [block], [], 1, 1)
     odd_back = moved(odd_sum, lambda i: i - 3 if i % 2 else -1)
     (joined,) = call(sum_kernel, (), (g_near, pair_back, relayed), [block], [], 1, 1)

time: 46.4 us -> 45.4 us (0.978)
  Pallas kernels: 12.7 us -> 11.7 us
    pallas_call x10 -> x11, Pallas kernels: 12.7 us -> 11.7 us  [call(): pl.pallas_call(functools.partial(body, len(lens)), in_specs=specs, out_sp...]
where the time goes in v6:
time: 45.4 us; the launch traced here: 45.2 us
  waiting for transfers between devices  17.1 us (38%)
  starting transfers between devices  15.5 us (34%)
  Pallas kernels  11.7 us (26%)
  between operations  0.81 us (2%)
    ppermute x7, waiting for transfers between devices, moved(): lax.ppermute(value, 'ctx', [(s, t) for s, t in pairs if 0 <= t < count])  15.9 us
    ppermute x7, starting transfers between devices, moved(): lax.ppermute(value, 'ctx', [(s, t) for s, t in pairs if 0 <= t < count])  13 us
    pallas_call x11, Pallas kernels, call(): pl.pallas_call(functools.partial(body, len(lens)), in_specs=specs, out_sp...  11.7 us
    ppermute x2, starting transfers between devices, all_lengths(): lax.ppermute(jnp.concatenate(pieces), 'pipe', [(i, i ^ stride) for i in r...  2.52 us
    ppermute x2, waiting for transfers between devices, all_lengths(): lax.ppermute(jnp.concatenate(pieces), 'pipe', [(i, i ^ stride) for i in r...  1.18 us
  transfers between devices with their start and end apart: 9, of which 4 were waited for; matrix products, arithmetic and copies ran while one was open for 0% of the time, Pallas kernels for 16%

profile of v6, /device:TPU:1, one launch (start us, length us, event | category | flops | bytes accessed | tf_op | source)
XLA Modules:
  0.0 45.2 jit_solution(15186487568151578761)
XLA Ops:
  0.6 0.0 copy-start
  0.6 0.0 copy-start.1
  0.6 0.0 copy-start.2
  0.7 4.7 %collective-permute-start = (bf16[128,1024]{1,0:T(8,128)(2,1)}, bf16[128,1024]{1,0:T(8,128)(2,1)S(1)}, u32[]{:S(2)}, u32[]{:S(2)}) collective-permute-start(bf16[128,1024]{1,0:T(8,128)(2,1)} %bitcast.17), channel_id=1, source_target_pairs={{0,3},{1,2},{2,5},{3,4},{4,7},{5,6},{8,11},{9,10},{10,13},{11,12},... | collective-permute-start | bytes 786440 | tf_op jit(solution)/shard_map/ppermute | solution.py:31
  5.4 3.9 %collective-permute-start.2 = (bf16[128,1024]{1,0:T(8,128)(2,1)}, bf16[128,1024]{1,0:T(8,128)(2,1)S(1)}, u32[]{:S(2)}, u32[]{:S(2)}) collective-permute-start(bf16[128,1024]{1,0:T(8,128)(2,1)} %bitcast.18), channel_id=1, source_target_pairs={{0,1},{1,4},{2,3},{3,6},{4,5},{6,7},{8,9},{9,12},{10,11},{11,14},{... | collective-permute-start | bytes 786440 | tf_op jit(solution)/shard_map/ppermute | solution.py:31
  9.3 1.3 %collective-permute-start.3 = (s32[2]{0:T(128)}, s32[2]{0:T(128)S(1)}, u32[]{:S(2)}, u32[]{:S(2)}) collective-permute-start(s32[2]{0:T(128)} %refs_0_.1), channel_id=1, source_target_pairs={{0,8},{8,0},{16,24},{24,16},{1,9},{9,1},{17,25},{25,17},{2,10},{10... | collective-permute-start | bytes 32 | tf_op jit(solution)/shard_map/ppermute | solution.py:51
  10.6 1.2 %collective-permute-done.refs_3_ = bf16[128,1024]{1,0:T(8,128)(2,1)S(1)} collective-permute-done((bf16[128,1024]{1,0:T(8,128)(2,1)}, bf16[128,1024]{1,0:T(8,128)(2,1)S(1)}, u32[]{:S(2)}, u32[]{:S(2)}) %collective-permute-start) | collective-permute-done | bytes 262176 | tf_op jit(solution)/shard_map/ppermute | solution.py:31
  11.8 0.4 collective-permute-start.1
  12.2 0.0 copy-start.3
  12.2 0.0 copy-done
  12.2 0.0 copy-done.1
  12.3 0.0 copy-done.2
  12.3 0.7 %shard_map.59 = (f32[128,4096]{1,0:T(8,128)S(1)}, f32[128,4096]{1,0:T(8,128)S(1)}) custom-call(bf16[128,4096]{1,0:T(8,128)(2,1)S(1)} %bitcast.5, bf16[128,4096]{1,0:T(8,128)(2,1)S(1)} %bitcast.11, bf16[128,1024]{1,0:T(8,128)(2,1)S(1)} %bitcast.19), custom_call_target="tpu_custom_call" | custom-call | flops 268435456 | bytes 6553600 | tf_op jit(solution)/shard_map/pallas_call | solution.py:324
  13.0 0.0 collective-permute-done.3.refs_1_
  13.0 0.0 copy-done.3
  13.0 0.1 pad_add_fusion
  13.1 1.2 %collective-permute-start.4 = (s32[4]{0:T(128)S(1)}, s32[4]{0:T(128)S(1)}, u32[]{:S(2)}, u32[]{:S(2)}) collective-permute-start(s32[4]{0:T(128)S(1)} %pad_add_fusion), channel_id=1, source_target_pairs={{0,16},{8,24},{16,0},{24,8},{1,17},{9,25},{17,1},{25,9},{2,18},{10... | collective-permute-start | bytes 56 | tf_op jit(solution)/shard_map/ppermute | solution.py:51
  14.3 1.2 %collective-permute-done.4.refs_2_ = s32[4]{0:T(128)S(1)} collective-permute-done((s32[4]{0:T(128)S(1)}, s32[4]{0:T(128)S(1)}, u32[]{:S(2)}, u32[]{:S(2)}) %collective-permute-start.4) | collective-permute-done | bytes 48 | tf_op jit(solution)/shard_map/ppermute | solution.py:51
  15.5 1.3 %shard_map.61 = (f32[8,4096]{1,0:T(8,128)S(1)}, f32[128,4096]{1,0:T(8,128)S(1)}, s32[8,128]{1,0:T(8,128)S(1)}) custom-call(s32[2]{0:T(128)S(1)} %copy-done.3, s32[2]{0:T(128)S(1)} %collective-permute-done.3.refs_1_, s32[4]{0:T(128)S(1)} %collective-permute-done.4.refs_2_, f32[128,4096]{1,0:T(8,128)S(1)} %get-tuple-element.21.refs_3_, ...), custom_call_target="tpu_custom_call" | custom-call | flops 134217728 | bytes 6492160 | tf_op jit(solution)/shard_map/pallas_call | solution.py:324
  16.8 1.2 %shard_map.62 = (f32[8,4096]{1,0:T(8,128)S(1)}, f32[128,4096]{1,0:T(8,128)S(1)}, f32[128,4096]{1,0:T(8,128)S(1)}) custom-call(s32[8,128]{1,0:T(8,128)S(1)} %get-tuple-element.24.refs_0_, bf16[128,4096]{1,0:T(8,128)(2,1)S(1)} %bitcast.6, bf16[128,4096]{1,0:T(8,128)(2,1)S(1)} %bitcast.12, bf16[128,1024]{1,0:T(8,128)(2,1)S(1)} %collective-permute-done.refs_3_), custom_call_target="tpu_custom_call" | custom-call | flops 268435456 | bytes 6688768 | tf_op jit(solution)/shard_map/pallas_call | solution.py:324
  18.0 0.0 collective-permute-done.1.refs_3_.refs_4_
  18.0 1.2 %shard_map.63 = (f32[8,4096]{1,0:T(8,128)S(1)}, f32[128,4096]{1,0:T(8,128)S(1)}, f32[128,4096]{1,0:T(8,128)S(1)}) custom-call(s32[8,128]{1,0:T(8,128)S(1)} %get-tuple-element.24.refs_0_, bf16[128,4096]{1,0:T(8,128)(2,1)S(1)} %bitcast.7, bf16[128,4096]{1,0:T(8,128)(2,1)S(1)} %bitcast.13, bf16[128,1024]{1,0:T(8,128)(2,1)S(1)} %collective-permute-done.1.refs_3_.refs_4_), custom_call_target="tpu_custom_call" | custom-call | flops 268435456 | bytes 6688768 | tf_op jit(solution)/shard_map/pallas_call | solution.py:324
  19.2 0.0 collective-permute-done.2.refs_3_.refs_5_
  19.2 2.1 %shard_map.64 = (f32[8,4096]{1,0:T(8,128)S(1)}, bf16[128,4096]{1,0:T(8,128)(2,1)S(1)}, bf16[128,1024]{1,0:T(8,128)(2,1)S(1)}) custom-call(s32[8,128]{1,0:T(8,128)S(1)} %get-tuple-element.24.refs_0_, bf16[128,4096]{1,0:T(8,128)(2,1)S(1)} %bitcast.8, bf16[128,4096]{1,0:T(8,128)(2,1)S(1)} %bitcast.14, ...), custom_call_target="tpu_custom_call" | custom-call | flops 536870912 | bytes 4198400 | tf_op jit(solution)/shard_map/pallas_call | solution.py:324
  21.4 1.6 %shard_map.65 = (bf16[128,1024]{1,0:T(8,128)(2,1)S(1)}, bf16[256,1024]{1,0:T(8,128)(2,1)S(1)}, bf16[256,4096]{1,0:T(8,128)(2,1)S(1)}) custom-call(bf16[128,4096]{1,0:T(8,128)(2,1)S(1)} %bitcast.9, bf16[128,4096]{1,0:T(8,128)(2,1)S(1)} %bitcast.15, f32[128,4096]{1,0:T(8,128)S(1)} %get-tuple-element.29.refs_2_, f32[128,4096]{1,0:T(8,128)S(1)} %get-tuple-element.30.refs_3_, ...), custom_call_target="tpu_custom_call" | custom-call | flops 536870912 | bytes 13762560 | tf_op jit(solution)/shard_map/pallas_call | solution.py:324
  23.0 1.3 %collective-permute-start.5 = (bf16[256,1024]{1,0:T(8,128)(2,1)S(1)}, bf16[256,1024]{1,0:T(8,128)(2,1)S(1)}, u32[]{:S(2)}, u32[]{:S(2)}) collective-permute-start(bf16[256,1024]{1,0:T(8,128)(2,1)S(1)} %get-tuple-element.38), channel_id=1, source_target_pairs={{0,1},{1,0},{2,3},{3,2},{4,5},{5,4},{6,7},{7,6},{8,9},{9,8},{10,11... | collective-permute-start | bytes 1572872 | tf_op jit(solution)/shard_map/ppermute | solution.py:31
  24.3 0.7 %collective-permute-start.7 = (bf16[128,1024]{1,0:T(8,128)(2,1)S(1)}, bf16[128,1024]{1,0:T(8,128)(2,1)S(1)}, u32[]{:S(2)}, u32[]{:S(2)}) collective-permute-start(bf16[128,1024]{1,0:T(8,128)(2,1)S(1)} %get-tuple-element.33.refs_7_), channel_id=1, source_target_pairs={{2,0},{4,2},{6,4},{10,8},{12,10},{14,12},{18,16},{20,18},{22,20},{... | collective-permute-start | bytes 786440 | tf_op jit(solution)/shard_map/ppermute | solution.py:31
  25.0 0.9 %collective-permute-done.5.pair_ref = bf16[256,1024]{1,0:T(8,128)(2,1)S(1)} collective-permute-done((bf16[256,1024]{1,0:T(8,128)(2,1)S(1)}, bf16[256,1024]{1,0:T(8,128)(2,1)S(1)}, u32[]{:S(2)}, u32[]{:S(2)}) %collective-permute-start.5) | collective-permute-done | bytes 524320 | tf_op jit(solution)/shard_map/ppermute | solution.py:31
  25.8 0.1 shard_map.67
  25.9 0.7 %collective-permute-start.6 = (bf16[128,1024]{1,0:T(8,128)(2,1)S(1)}, bf16[128,1024]{1,0:T(8,128)(2,1)S(1)}, u32[]{:S(2)}, u32[]{:S(2)}) collective-permute-start(bf16[128,1024]{1,0:T(8,128)(2,1)S(1)} %shard_map.67), channel_id=1, source_target_pairs={{3,0},{5,2},{7,4},{11,8},{13,10},{15,12},{19,16},{21,18},{23,20},{... | collective-permute-start | bytes 786440 | tf_op jit(solution)/shard_map/ppermute | solution.py:31
  26.6 0.0 collective-permute-done.7.refs_0_
  26.6 0.1 shard_map.68
  26.7 1.3 %collective-permute-start.8 = (bf16[128,1024]{1,0:T(8,128)(2,1)S(1)}, bf16[128,1024]{1,0:T(8,128)(2,1)S(1)}, u32[]{:S(2)}, u32[]{:S(2)}) collective-permute-start(bf16[128,1024]{1,0:T(8,128)(2,1)S(1)} %shard_map.68), channel_id=1, source_target_pairs={{2,1},{4,3},{6,5},{10,9},{12,11},{14,13},{18,17},{20,19},{22,21},{... | collective-permute-start | bytes 786440 | tf_op jit(solution)/shard_map/ppermute | solution.py:31
  28.0 2.5 %shard_map.66 = (bf16[128,4096]{1,0:T(8,128)(2,1)}, f32[128,1024]{1,0:T(8,128)S(1)}) custom-call(bf16[128,4096]{1,0:T(8,128)(2,1)S(1)} %bitcast.10, bf16[128,4096]{1,0:T(8,128)(2,1)S(1)} %bitcast.16, bf16[128,1024]{1,0:T(8,128)(2,1)S(1)} %bitcast.20, bf16[128,1024]{1,0:T(8,128)(2,1)S(1)} %collective-permute-done.refs_3_, ...), custom_call_target="tpu_custom_call" | custom-call | flops 805306368 | bytes 12189696 | tf_op jit(solution)/shard_map/pallas_call | solution.py:324
  30.5 0.0 collective-permute-done.6.odd_ref
  30.5 13.8 %collective-permute-done.8.even_ref = bf16[128,1024]{1,0:T(8,128)(2,1)S(1)} collective-permute-done((bf16[128,1024]{1,0:T(8,128)(2,1)S(1)}, bf16[128,1024]{1,0:T(8,128)(2,1)S(1)}, u32[]{:S(2)}, u32[]{:S(2)}) %collective-permute-start.8) | collective-permute-done | bytes 262176 | tf_op jit(solution)/shard_map/ppermute | solution.py:31
  44.3 0.8 %shard_map.69 = bf16[128,1024]{1,0:T(8,128)(2,1)} custom-call(f32[128,1024]{1,0:T(8,128)S(1)} %get-tuple-element.37.own_ref, bf16[256,1024]{1,0:T(8,128)(2,1)S(1)} %collective-permute-done.5.pair_ref, bf16[128,1024]{1,0:T(8,128)(2,1)S(1)} %collective-permute-done.6.odd_ref, bf16[128,1024]{1,0:T(8,128)(2,1)S(1)} %collective-permute-done.8.even_ref), custom_call_target="tpu_custom_call" | custom-call | flops 1048576 | bytes 1835008 | tf_op jit(solution)/shard_map/pallas_call | solution.py:324
  (1 shorter events, 0.0 us)
Async XLA Ops:
  0.6 11.6 %copy-start = (bf16[1,128,4096]{2,1,0:T(8,128)(2,1)S(1)}, bf16[1,128,4096]{2,1,0:T(8,128)(2,1)}, u32[]{:S(2)}) copy-start(bf16[1,128,4096]{2,1,0:T(8,128)(2,1)} %param.4) | copy-start | bytes 3145732
  0.6 11.6 %copy-start.1 = (bf16[1,128,4096]{2,1,0:T(8,128)(2,1)S(1)}, bf16[1,128,4096]{2,1,0:T(8,128)(2,1)}, u32[]{:S(2)}) copy-start(bf16[1,128,4096]{2,1,0:T(8,128)(2,1)} %param.6) | copy-start | bytes 3145732
  0.6 11.6 %copy-start.2 = (bf16[1,128,1024]{2,1,0:T(8,128)(2,1)S(1)}, bf16[1,128,1024]{2,1,0:T(8,128)(2,1)}, u32[]{:S(2)}) copy-start(bf16[1,128,1024]{2,1,0:T(8,128)(2,1)} %param.5) | copy-start | bytes 786436
  0.7 11.1 %collective-permute-start = (bf16[128,1024]{1,0:T(8,128)(2,1)}, bf16[128,1024]{1,0:T(8,128)(2,1)S(1)}, u32[]{:S(2)}, u32[]{:S(2)}) collective-permute-start(bf16[128,1024]{1,0:T(8,128)(2,1)} %bitcast.17), channel_id=1, source_target_pairs={{0,3},{1,2},{2,5},{3,4},{4,7},{5,6},{8,11},{9,10},{10,13},{11,12},... | collective-permute-start | bytes 786440 | tf_op jit(solution)/shard_map/ppermute | solution.py:31
  5.4 13.8 %collective-permute-start.2 = (bf16[128,1024]{1,0:T(8,128)(2,1)}, bf16[128,1024]{1,0:T(8,128)(2,1)S(1)}, u32[]{:S(2)}, u32[]{:S(2)}) collective-permute-start(bf16[128,1024]{1,0:T(8,128)(2,1)} %bitcast.18), channel_id=1, source_target_pairs={{0,1},{1,4},{2,3},{3,6},{4,5},{6,7},{8,9},{9,12},{10,11},{11,14},{... | collective-permute-start | bytes 786440 | tf_op jit(solution)/shard_map/ppermute | solution.py:31
  9.3 3.7 %collective-permute-start.3 = (s32[2]{0:T(128)}, s32[2]{0:T(128)S(1)}, u32[]{:S(2)}, u32[]{:S(2)}) collective-permute-start(s32[2]{0:T(128)} %refs_0_.1), channel_id=1, source_target_pairs={{0,8},{8,0},{16,24},{24,16},{1,9},{9,1},{17,25},{25,17},{2,10},{10... | collective-permute-start | bytes 32 | tf_op jit(solution)/shard_map/ppermute | solution.py:51
  11.8 6.2 %collective-permute-start.1 = (bf16[128,1024]{1,0:T(8,128)(2,1)S(1)}, bf16[128,1024]{1,0:T(8,128)(2,1)S(1)}, u32[]{:S(2)}, u32[]{:S(2)}) collective-permute-start(bf16[128,1024]{1,0:T(8,128)(2,1)S(1)} %collective-permute-done.refs_3_), channel_id=1, source_target_pairs={{0,1},{1,0},{2,3},{3,2},{4,5},{5,4},{6,7},{7,6},{8,9},{9,8},{10,11... | collective-permute-start | bytes 786440 | tf_op jit(solution)/shard_map/ppermute | solution.py:31
  12.2 0.8 %copy-start.3 = (s32[2]{0:T(128)S(1)}, s32[2]{0:T(128)}, u32[]{:S(2)}) copy-start(s32[2]{0:T(128)} %refs_0_.1) | copy-start | bytes 28
  13.1 2.4 %collective-permute-start.4 = (s32[4]{0:T(128)S(1)}, s32[4]{0:T(128)S(1)}, u32[]{:S(2)}, u32[]{:S(2)}) collective-permute-start(s32[4]{0:T(128)S(1)} %pad_add_fusion), channel_id=1, source_target_pairs={{0,16},{8,24},{16,0},{24,8},{1,17},{9,25},{17,1},{25,9},{2,18},{10... | collective-permute-start | bytes 56 | tf_op jit(solution)/shard_map/ppermute | solution.py:51
  23.0 2.8 %collective-permute-start.5 = (bf16[256,1024]{1,0:T(8,128)(2,1)S(1)}, bf16[256,1024]{1,0:T(8,128)(2,1)S(1)}, u32[]{:S(2)}, u32[]{:S(2)}) collective-permute-start(bf16[256,1024]{1,0:T(8,128)(2,1)S(1)} %get-tuple-element.38), channel_id=1, source_target_pairs={{0,1},{1,0},{2,3},{3,2},{4,5},{5,4},{6,7},{7,6},{8,9},{9,8},{10,11... | collective-permute-start | bytes 1572872 | tf_op jit(solution)/shard_map/ppermute | solution.py:31
  24.3 2.3 %collective-permute-start.7 = (bf16[128,1024]{1,0:T(8,128)(2,1)S(1)}, bf16[128,1024]{1,0:T(8,128)(2,1)S(1)}, u32[]{:S(2)}, u32[]{:S(2)}) collective-permute-start(bf16[128,1024]{1,0:T(8,128)(2,1)S(1)} %get-tuple-element.33.refs_7_), channel_id=1, source_target_pairs={{2,0},{4,2},{6,4},{10,8},{12,10},{14,12},{18,16},{20,18},{22,20},{... | collective-permute-start | bytes 786440 | tf_op jit(solution)/shard_map/ppermute | solution.py:31
  25.9 4.6 %collective-permute-start.6 = (bf16[128,1024]{1,0:T(8,128)(2,1)S(1)}, bf16[128,1024]{1,0:T(8,128)(2,1)S(1)}, u32[]{:S(2)}, u32[]{:S(2)}) collective-permute-start(bf16[128,1024]{1,0:T(8,128)(2,1)S(1)} %shard_map.67), channel_id=1, source_target_pairs={{3,0},{5,2},{7,4},{11,8},{13,10},{15,12},{19,16},{21,18},{23,20},{... | collective-permute-start | bytes 786440 | tf_op jit(solution)/shard_map/ppermute | solution.py:31
  26.7 17.6 %collective-permute-start.8 = (bf16[128,1024]{1,0:T(8,128)(2,1)S(1)}, bf16[128,1024]{1,0:T(8,128)(2,1)S(1)}, u32[]{:S(2)}, u32[]{:S(2)}) collective-permute-start(bf16[128,1024]{1,0:T(8,128)(2,1)S(1)} %shard_map.68), channel_id=1, source_target_pairs={{2,1},{4,3},{6,5},{10,9},{12,11},{14,13},{18,17},{20,19},{22,21},{... | collective-permute-start | bytes 786440 | tf_op jit(solution)/shard_map/ppermute | solution.py:31

commit v7 on v6

--- a/solution.py
+++ b/solution.py
@@ -81,6 +81,11 @@
     return jnp.where(u_pos >= doc_start, base, -1e30).astype(F32)
 
 
+def reaches(docs_ref, offset):
+    rows = docs_ref.shape[1]
+    return docs_ref[0:1, 0:1][0, 0] < (lax.axis_index("ctx") - offset + 1) * rows
+
+
 def is_odd():
     return lax.rem(lax.axis_index("ctx"), 2)
 
@@ -163,7 +168,7 @@
 def block_kernel(offset_of, n_lens, *refs):
     docs_ref, q_ref, d_ref, kv_ref, stats_ref, p_ref, dp_ref, bias_scr, s_scr = refs
     rows = q_ref.shape[0]
-    bias_scr[...] = bias_of(docs_ref[0:1], offset_of(), 0.0)
+    needed = reaches(docs_ref, offset_of())
 
     def first(i):
         s_scr[i % SLOTS] = scores_of(kv_ref, q_ref, i) + twice(bias_scr[...])
@@ -173,7 +178,17 @@
         column = at(i, 2 * rows)
         keep_exponentials(s_scr[i % SLOTS], dp_ref[:, column], column, stats_ref, p_ref)
 
-    pipelined([first, second])
+    @pl.when(needed)
+    def _():
+        bias_scr[...] = bias_of(docs_ref[0:1], offset_of(), 0.0)
+        pipelined([first, second])
+
+    @pl.when(jnp.logical_not(needed))
+    def _():
+        p_ref[...] = jnp.zeros_like(p_ref)
+        dp_ref[...] = jnp.zeros_like(dp_ref)
+        stats_ref[0:1] = jnp.full((1, stats_ref.shape[1]), -1e30, F32)
+        stats_ref[1:3] = jnp.zeros((2, stats_ref.shape[1]), F32)
 
 
 def far_kernel(n_lens, *refs):
@@ -182,7 +197,20 @@
     final_ref, ds_ref, g_ref = refs[7:10]
     bias_scr, s_scr, dp_scr, p_scr, row_scr, w_scr = refs[10:]
     rows = q_ref.shape[0]
-    bias_scr[...] = bias_of(docs_ref[0:1], 3 - 2 * is_odd(), 0.0)
+    offset = 3 - 2 * is_odd()
+    needed = reaches(docs_ref, offset)
+
+    def combined(top, column, total, dot):
+        shares = [jnp.exp2((ref[0:1, column] - top) * RATE) for ref in stats_refs]
+        for ref, share in zip(stats_refs, shares):
+            total = total + ref[1:2, column] * share
+            dot = dot + ref[2:3, column] * share
+        inv = 1.0 / total
+        delta = dot * inv
+        final_ref[0:1, column] = delta
+        for k, share in enumerate(shares):
+            final_ref[k + 1:k + 2, column] = share * inv
+        return inv, delta
 
     def first(i):
         s_scr[i % SLOTS] = scores_of(kv_ref, q_ref, i) + twice(bias_scr[...])
@@ -197,17 +225,9 @@
         p_scr[i % SLOTS] = p
         total = jnp.sum(p, axis=0, keepdims=True)
         dot = jnp.sum(p * dp_scr[i % SLOTS], axis=0, keepdims=True)
-        shares = [jnp.exp2((block_top - top) * RATE) for block_top in tops]
-        for ref, share in zip(stats_refs, shares):
-            total = total + ref[1:2, column] * share
-            dot = dot + ref[2:3, column] * share
-        inv = 1.0 / total
-        delta = dot * inv
+        inv, delta = combined(top, column, total, dot)
         row_scr[i % SLOTS, 0:1] = inv
         row_scr[i % SLOTS, 1:2] = delta
-        final_ref[0:1, column] = delta
-        for k, share in enumerate(shares):
-            final_ref[k + 1:k + 2, column] = share * inv
 
     def third(i):
         w = p_scr[i % SLOTS] * row_scr[i % SLOTS, 0:1]
@@ -226,13 +246,26 @@
         )
         g_ref[:, at(HK + group, HD)] = dv.astype(BF16)
 
-    pipelined([first, second, third, at_group_end(gradients)])
+    @pl.when(needed)
+    def _():
+        bias_scr[...] = bias_of(docs_ref[0:1], offset, 0.0)
+        pipelined([first, second, third, at_group_end(gradients)])
+
+    @pl.when(jnp.logical_not(needed))
+    def _():
+        g_ref[...] = jnp.zeros_like(g_ref)
+        ds_ref[...] = jnp.zeros_like(ds_ref)
+        column = slice(0, final_ref.shape[1])
+        top = functools.reduce(jnp.maximum, [ref[0:1, column] for ref in stats_refs])
+        zero = jnp.zeros_like(top)
+        combined(top, column, zero, zero)
 
 
 def mid_kernel(n_lens, *refs):
-    q_ref, d_ref, p1_ref, dp1_ref, p2_ref, dp2_ref, final_ref, far_ref = refs[:8]
-    near_ref, pair_ref, ds_ref, w_scr = refs[8:]
+    docs_ref, q_ref, d_ref, p1_ref, dp1_ref, p2_ref, dp2_ref, final_ref, far_ref = refs[:9]
+    near_ref, pair_ref, ds_ref, w_scr = refs[9:]
     rows = q_ref.shape[0]
+    needed = reaches(docs_ref, 1 + is_odd())
     pair_ref[rows:] = far_ref[...]
 
     def first(i):
@@ -259,7 +292,15 @@
         near_ref[:, at(HK + group, HD)] = dv[:rows]
         pair_ref[:rows, at(HK + group, HD)] = dv[rows:]
 
-    pipelined([first, at_group_end(key_grads), at_group_end(value_grads)])
+    @pl.when(needed)
+    def _():
+        pipelined([first, at_group_end(key_grads), at_group_end(value_grads)])
+
+    @pl.when(jnp.logical_not(needed))
+    def _():
+        near_ref[...] = jnp.zeros_like(near_ref)
+        pair_ref[:rows] = jnp.zeros_like(near_ref)
+        ds_ref[...] = jnp.zeros_like(ds_ref)
 
 
 def sum_kernel(n_lens, near_ref, pair_ref, *refs):
@@ -376,10 +417,10 @@
         + [pltpu.VMEM((2, rows, GROUP * rows), BF16)],
         4 * rows, 6,
     )
-    relayed = moved(g_far, lambda i: -1 if i % 2 else i - 2)
+    relayed = moved(g_far, lambda i: -1 if i % 2 or i < REACH else i - 2)
     g_near, g_pair, ds_mid = call(
         mid_kernel, (),
-        (q, dout, p_near, dp_near, p_side, dp_side, final, g_far),
+        (docs, q, dout, p_near, dp_near, p_side, dp_side, final, g_far),
         [
             block,
             array((2 * rows, wide), BF16),

time: 45.4 us -> 45.9 us (1.011)
  waiting for transfers between devices: 17.1 us -> 21.5 us
  Pallas kernels: 11.7 us -> 8.91 us
  starting transfers between devices: 15.5 us -> 14.3 us
    ppermute x7, waiting for transfers between devices: 15.9 us -> 20.3 us  [moved(): lax.ppermute(value, 'ctx', [(s, t) for s, t in pairs if 0 <= t < count])]
    pallas_call x11, Pallas kernels: 11.7 us -> 8.91 us  [call(): pl.pallas_call(functools.partial(body, len(lens)), in_specs=specs, out_sp...]
    ppermute x7, starting transfers between devices: 13 us -> 11.8 us  [moved(): lax.ppermute(value, 'ctx', [(s, t) for s, t in pairs if 0 <= t < count])]
  transfers between devices with their start and end apart: 9 -> 9, of which waited for: 4 -> 4; matrix products, arithmetic and copies ran while one was open for 0% -> 0% of each run, Pallas kernels for 16% -> 12%
where the time goes in v7:
time: 45.9 us; the launch traced here: 45.7 us
  waiting for transfers between devices  21.5 us (47%)
  starting transfers between devices  14.3 us (31%)
  Pallas kernels  8.91 us (19%)
  between operations  0.83 us (2%)
    ppermute x7, waiting for transfers between devices, moved(): lax.ppermute(value, 'ctx', [(s, t) for s, t in pairs if 0 <= t < count])  20.3 us
    ppermute x7, starting transfers between devices, moved(): lax.ppermute(value, 'ctx', [(s, t) for s, t in pairs if 0 <= t < count])  11.8 us
    pallas_call x11, Pallas kernels, call(): pl.pallas_call(functools.partial(body, len(lens)), in_specs=specs, out_sp...  8.91 us
    ppermute x2, starting transfers between devices, all_lengths(): lax.ppermute(jnp.concatenate(pieces), 'pipe', [(i, i ^ stride) for i in r...  2.52 us
    ppermute x2, waiting for transfers between devices, all_lengths(): lax.ppermute(jnp.concatenate(pieces), 'pipe', [(i, i ^ stride) for i in r...  1.18 us
  transfers between devices with their start and end apart: 9, of which 4 were waited for; matrix products, arithmetic and copies ran while one was open for 0% of the time, Pallas kernels for 12%

profile of v7, /device:TPU:1, one launch (start us, length us, event | category | flops | bytes accessed | tf_op | source)
XLA Modules:
  0.0 45.7 jit_solution(7608088376168754751)
XLA Ops:
  0.6 0.0 copy-start
  0.6 0.0 copy-start.1
  0.6 0.0 copy-start.2
  0.7 4.7 %collective-permute-start = (bf16[128,1024]{1,0:T(8,128)(2,1)}, bf16[128,1024]{1,0:T(8,128)(2,1)S(1)}, u32[]{:S(2)}, u32[]{:S(2)}) collective-permute-start(bf16[128,1024]{1,0:T(8,128)(2,1)} %bitcast.17), channel_id=1, source_target_pairs={{0,3},{1,2},{2,5},{3,4},{4,7},{5,6},{8,11},{9,10},{10,13},{11,12},... | collective-permute-start | bytes 786440 | tf_op jit(solution)/shard_map/ppermute | solution.py:31
  5.4 3.9 %collective-permute-start.2 = (bf16[128,1024]{1,0:T(8,128)(2,1)}, bf16[128,1024]{1,0:T(8,128)(2,1)S(1)}, u32[]{:S(2)}, u32[]{:S(2)}) collective-permute-start(bf16[128,1024]{1,0:T(8,128)(2,1)} %bitcast.18), channel_id=1, source_target_pairs={{0,1},{1,4},{2,3},{3,6},{4,5},{6,7},{8,9},{9,12},{10,11},{11,14},{... | collective-permute-start | bytes 786440 | tf_op jit(solution)/shard_map/ppermute | solution.py:31
  9.3 1.3 %collective-permute-start.3 = (s32[2]{0:T(128)}, s32[2]{0:T(128)S(1)}, u32[]{:S(2)}, u32[]{:S(2)}) collective-permute-start(s32[2]{0:T(128)} %refs_0_.1), channel_id=1, source_target_pairs={{0,8},{8,0},{16,24},{24,16},{1,9},{9,1},{17,25},{25,17},{2,10},{10... | collective-permute-start | bytes 32 | tf_op jit(solution)/shard_map/ppermute | solution.py:51
  10.6 1.2 %collective-permute-done.refs_3_ = bf16[128,1024]{1,0:T(8,128)(2,1)S(1)} collective-permute-done((bf16[128,1024]{1,0:T(8,128)(2,1)}, bf16[128,1024]{1,0:T(8,128)(2,1)S(1)}, u32[]{:S(2)}, u32[]{:S(2)}) %collective-permute-start) | collective-permute-done | bytes 262176 | tf_op jit(solution)/shard_map/ppermute | solution.py:31
  11.8 0.4 collective-permute-start.1
  12.2 0.0 copy-start.3
  12.2 0.0 copy-done
  12.2 0.0 copy-done.1
  12.3 0.0 copy-done.2
  12.3 0.7 %shard_map.59 = (f32[128,4096]{1,0:T(8,128)S(1)}, f32[128,4096]{1,0:T(8,128)S(1)}) custom-call(bf16[128,4096]{1,0:T(8,128)(2,1)S(1)} %bitcast.5, bf16[128,4096]{1,0:T(8,128)(2,1)S(1)} %bitcast.11, bf16[128,1024]{1,0:T(8,128)(2,1)S(1)} %bitcast.19), custom_call_target="tpu_custom_call" | custom-call | flops 268435456 | bytes 6553600 | tf_op jit(solution)/shard_map/pallas_call | solution.py:365
  13.0 0.0 collective-permute-done.3.refs_1_
  13.0 0.0 copy-done.3
  13.0 0.1 pad_add_fusion
  13.1 1.2 %collective-permute-start.4 = (s32[4]{0:T(128)S(1)}, s32[4]{0:T(128)S(1)}, u32[]{:S(2)}, u32[]{:S(2)}) collective-permute-start(s32[4]{0:T(128)S(1)} %pad_add_fusion), channel_id=1, source_target_pairs={{0,16},{8,24},{16,0},{24,8},{1,17},{9,25},{17,1},{25,9},{2,18},{10... | collective-permute-start | bytes 56 | tf_op jit(solution)/shard_map/ppermute | solution.py:51
  14.3 1.2 %collective-permute-done.4.refs_2_ = s32[4]{0:T(128)S(1)} collective-permute-done((s32[4]{0:T(128)S(1)}, s32[4]{0:T(128)S(1)}, u32[]{:S(2)}, u32[]{:S(2)}) %collective-permute-start.4) | collective-permute-done | bytes 48 | tf_op jit(solution)/shard_map/ppermute | solution.py:51
  15.5 1.3 %shard_map.61 = (f32[8,4096]{1,0:T(8,128)S(1)}, f32[128,4096]{1,0:T(8,128)S(1)}, s32[8,128]{1,0:T(8,128)S(1)}) custom-call(s32[2]{0:T(128)S(1)} %copy-done.3, s32[2]{0:T(128)S(1)} %collective-permute-done.3.refs_1_, s32[4]{0:T(128)S(1)} %collective-permute-done.4.refs_2_, f32[128,4096]{1,0:T(8,128)S(1)} %get-tuple-element.21.refs_3_, ...), custom_call_target="tpu_custom_call" | custom-call | flops 134217728 | bytes 6492160 | tf_op jit(solution)/shard_map/pallas_call | solution.py:365
  16.8 0.3 shard_map.62
  17.1 0.0 collective-permute-done.1.refs_3_.refs_4_
  17.1 0.3 shard_map.63
  17.5 0.0 collective-permute-done.2.refs_3_.refs_5_
  17.5 2.4 %shard_map.64 = (f32[8,4096]{1,0:T(8,128)S(1)}, bf16[128,4096]{1,0:T(8,128)(2,1)S(1)}, bf16[128,1024]{1,0:T(8,128)(2,1)S(1)}) custom-call(s32[8,128]{1,0:T(8,128)S(1)} %get-tuple-element.24.refs_0_, bf16[128,4096]{1,0:T(8,128)(2,1)S(1)} %bitcast.8, bf16[128,4096]{1,0:T(8,128)(2,1)S(1)} %bitcast.14, ...), custom_call_target="tpu_custom_call" | custom-call | flops 536870912 | bytes 4198400 | tf_op jit(solution)/shard_map/pallas_call | solution.py:365
  19.9 0.2 shard_map.65
  20.1 0.1 collective-permute-start.5
  20.2 0.7 %collective-permute-start.7 = (bf16[128,1024]{1,0:T(8,128)(2,1)S(1)}, bf16[128,1024]{1,0:T(8,128)(2,1)S(1)}, u32[]{:S(2)}, u32[]{:S(2)}) collective-permute-start(bf16[128,1024]{1,0:T(8,128)(2,1)S(1)} %get-tuple-element.33.refs_8_), channel_id=1, source_target_pairs={{4,2},{6,4},{12,10},{14,12},{20,18},{22,20},{28,26},{30,28}} | collective-permute-start | bytes 786440 | tf_op jit(solution)/shard_map/ppermute | solution.py:31
  20.9 1.2 %collective-permute-done.5.pair_ref = bf16[256,1024]{1,0:T(8,128)(2,1)S(1)} collective-permute-done((bf16[256,1024]{1,0:T(8,128)(2,1)S(1)}, bf16[256,1024]{1,0:T(8,128)(2,1)S(1)}, u32[]{:S(2)}, u32[]{:S(2)}) %collective-permute-start.5) | collective-permute-done | bytes 524320 | tf_op jit(solution)/shard_map/ppermute | solution.py:31
  22.1 0.1 shard_map.67
  22.1 0.7 %collective-permute-start.6 = (bf16[128,1024]{1,0:T(8,128)(2,1)S(1)}, bf16[128,1024]{1,0:T(8,128)(2,1)S(1)}, u32[]{:S(2)}, u32[]{:S(2)}) collective-permute-start(bf16[128,1024]{1,0:T(8,128)(2,1)S(1)} %shard_map.67), channel_id=1, source_target_pairs={{3,0},{5,2},{7,4},{11,8},{13,10},{15,12},{19,16},{21,18},{23,20},{... | collective-permute-start | bytes 786440 | tf_op jit(solution)/shard_map/ppermute | solution.py:31
  22.8 0.0 collective-permute-done.7.refs_0_
  22.8 0.1 shard_map.68
  22.9 1.3 %collective-permute-start.8 = (bf16[128,1024]{1,0:T(8,128)(2,1)S(1)}, bf16[128,1024]{1,0:T(8,128)(2,1)S(1)}, u32[]{:S(2)}, u32[]{:S(2)}) collective-permute-start(bf16[128,1024]{1,0:T(8,128)(2,1)S(1)} %shard_map.68), channel_id=1, source_target_pairs={{2,1},{4,3},{6,5},{10,9},{12,11},{14,13},{18,17},{20,19},{22,21},{... | collective-permute-start | bytes 786440 | tf_op jit(solution)/shard_map/ppermute | solution.py:31
  24.2 2.7 %shard_map.66 = (bf16[128,4096]{1,0:T(8,128)(2,1)}, f32[128,1024]{1,0:T(8,128)S(1)}) custom-call(bf16[128,4096]{1,0:T(8,128)(2,1)S(1)} %bitcast.10, bf16[128,4096]{1,0:T(8,128)(2,1)S(1)} %bitcast.16, bf16[128,1024]{1,0:T(8,128)(2,1)S(1)} %bitcast.20, bf16[128,1024]{1,0:T(8,128)(2,1)S(1)} %collective-permute-done.refs_3_, ...), custom_call_target="tpu_custom_call" | custom-call | flops 805306368 | bytes 12189696 | tf_op jit(solution)/shard_map/pallas_call | solution.py:365
  26.9 0.0 collective-permute-done.6.odd_ref
  26.9 17.9 %collective-permute-done.8.even_ref = bf16[128,1024]{1,0:T(8,128)(2,1)S(1)} collective-permute-done((bf16[128,1024]{1,0:T(8,128)(2,1)S(1)}, bf16[128,1024]{1,0:T(8,128)(2,1)S(1)}, u32[]{:S(2)}, u32[]{:S(2)}) %collective-permute-start.8) | collective-permute-done | bytes 262176 | tf_op jit(solution)/shard_map/ppermute | solution.py:31
  44.8 0.8 %shard_map.69 = bf16[128,1024]{1,0:T(8,128)(2,1)} custom-call(f32[128,1024]{1,0:T(8,128)S(1)} %get-tuple-element.37.own_ref, bf16[256,1024]{1,0:T(8,128)(2,1)S(1)} %collective-permute-done.5.pair_ref, bf16[128,1024]{1,0:T(8,128)(2,1)S(1)} %collective-permute-done.6.odd_ref, bf16[128,1024]{1,0:T(8,128)(2,1)S(1)} %collective-permute-done.8.even_ref), custom_call_target="tpu_custom_call" | custom-call | flops 1048576 | bytes 1835008 | tf_op jit(solution)/shard_map/pallas_call | solution.py:365
  (1 shorter events, 0.0 us)
Async XLA Ops:
  0.6 11.6 %copy-start = (bf16[1,128,4096]{2,1,0:T(8,128)(2,1)S(1)}, bf16[1,128,4096]{2,1,0:T(8,128)(2,1)}, u32[]{:S(2)}) copy-start(bf16[1,128,4096]{2,1,0:T(8,128)(2,1)} %param.4) | copy-start | bytes 3145732
  0.6 11.6 %copy-start.1 = (bf16[1,128,4096]{2,1,0:T(8,128)(2,1)S(1)}, bf16[1,128,4096]{2,1,0:T(8,128)(2,1)}, u32[]{:S(2)}) copy-start(bf16[1,128,4096]{2,1,0:T(8,128)(2,1)} %param.6) | copy-start | bytes 3145732
  0.6 11.6 %copy-start.2 = (bf16[1,128,1024]{2,1,0:T(8,128)(2,1)S(1)}, bf16[1,128,1024]{2,1,0:T(8,128)(2,1)}, u32[]{:S(2)}) copy-start(bf16[1,128,1024]{2,1,0:T(8,128)(2,1)} %param.5) | copy-start | bytes 786436
  0.7 11.1 %collective-permute-start = (bf16[128,1024]{1,0:T(8,128)(2,1)}, bf16[128,1024]{1,0:T(8,128)(2,1)S(1)}, u32[]{:S(2)}, u32[]{:S(2)}) collective-permute-start(bf16[128,1024]{1,0:T(8,128)(2,1)} %bitcast.17), channel_id=1, source_target_pairs={{0,3},{1,2},{2,5},{3,4},{4,7},{5,6},{8,11},{9,10},{10,13},{11,12},... | collective-permute-start | bytes 786440 | tf_op jit(solution)/shard_map/ppermute | solution.py:31
  5.4 12.1 %collective-permute-start.2 = (bf16[128,1024]{1,0:T(8,128)(2,1)}, bf16[128,1024]{1,0:T(8,128)(2,1)S(1)}, u32[]{:S(2)}, u32[]{:S(2)}) collective-permute-start(bf16[128,1024]{1,0:T(8,128)(2,1)} %bitcast.18), channel_id=1, source_target_pairs={{0,1},{1,4},{2,3},{3,6},{4,5},{6,7},{8,9},{9,12},{10,11},{11,14},{... | collective-permute-start | bytes 786440 | tf_op jit(solution)/shard_map/ppermute | solution.py:31
  9.3 3.7 %collective-permute-start.3 = (s32[2]{0:T(128)}, s32[2]{0:T(128)S(1)}, u32[]{:S(2)}, u32[]{:S(2)}) collective-permute-start(s32[2]{0:T(128)} %refs_0_.1), channel_id=1, source_target_pairs={{0,8},{8,0},{16,24},{24,16},{1,9},{9,1},{17,25},{25,17},{2,10},{10... | collective-permute-start | bytes 32 | tf_op jit(solution)/shard_map/ppermute | solution.py:51
  11.8 5.3 %collective-permute-start.1 = (bf16[128,1024]{1,0:T(8,128)(2,1)S(1)}, bf16[128,1024]{1,0:T(8,128)(2,1)S(1)}, u32[]{:S(2)}, u32[]{:S(2)}) collective-permute-start(bf16[128,1024]{1,0:T(8,128)(2,1)S(1)} %collective-permute-done.refs_3_), channel_id=1, source_target_pairs={{0,1},{1,0},{2,3},{3,2},{4,5},{5,4},{6,7},{7,6},{8,9},{9,8},{10,11... | collective-permute-start | bytes 786440 | tf_op jit(solution)/shard_map/ppermute | solution.py:31
  12.2 0.8 %copy-start.3 = (s32[2]{0:T(128)S(1)}, s32[2]{0:T(128)}, u32[]{:S(2)}) copy-start(s32[2]{0:T(128)} %refs_0_.1) | copy-start | bytes 28
  13.1 2.4 %collective-permute-start.4 = (s32[4]{0:T(128)S(1)}, s32[4]{0:T(128)S(1)}, u32[]{:S(2)}, u32[]{:S(2)}) collective-permute-start(s32[4]{0:T(128)S(1)} %pad_add_fusion), channel_id=1, source_target_pairs={{0,16},{8,24},{16,0},{24,8},{1,17},{9,25},{17,1},{25,9},{2,18},{10... | collective-permute-start | bytes 56 | tf_op jit(solution)/shard_map/ppermute | solution.py:51
  20.1 2.0 %collective-permute-start.5 = (bf16[256,1024]{1,0:T(8,128)(2,1)S(1)}, bf16[256,1024]{1,0:T(8,128)(2,1)S(1)}, u32[]{:S(2)}, u32[]{:S(2)}) collective-permute-start(bf16[256,1024]{1,0:T(8,128)(2,1)S(1)} %get-tuple-element.38), channel_id=1, source_target_pairs={{0,1},{1,0},{2,3},{3,2},{4,5},{5,4},{6,7},{7,6},{8,9},{9,8},{10,11... | collective-permute-start | bytes 1572872 | tf_op jit(solution)/shard_map/ppermute | solution.py:31
  20.2 2.7 %collective-permute-start.7 = (bf16[128,1024]{1,0:T(8,128)(2,1)S(1)}, bf16[128,1024]{1,0:T(8,128)(2,1)S(1)}, u32[]{:S(2)}, u32[]{:S(2)}) collective-permute-start(bf16[128,1024]{1,0:T(8,128)(2,1)S(1)} %get-tuple-element.33.refs_8_), channel_id=1, source_target_pairs={{4,2},{6,4},{12,10},{14,12},{20,18},{22,20},{28,26},{30,28}} | collective-permute-start | bytes 786440 | tf_op jit(solution)/shard_map/ppermute | solution.py:31
  22.1 4.8 %collective-permute-start.6 = (bf16[128,1024]{1,0:T(8,128)(2,1)S(1)}, bf16[128,1024]{1,0:T(8,128)(2,1)S(1)}, u32[]{:S(2)}, u32[]{:S(2)}) collective-permute-start(bf16[128,1024]{1,0:T(8,128)(2,1)S(1)} %shard_map.67), channel_id=1, source_target_pairs={{3,0},{5,2},{7,4},{11,8},{13,10},{15,12},{19,16},{21,18},{23,20},{... | collective-permute-start | bytes 786440 | tf_op jit(solution)/shard_map/ppermute | solution.py:31
  22.9 21.9 %collective-permute-start.8 = (bf16[128,1024]{1,0:T(8,128)(2,1)S(1)}, bf16[128,1024]{1,0:T(8,128)(2,1)S(1)}, u32[]{:S(2)}, u32[]{:S(2)}) collective-permute-start(bf16[128,1024]{1,0:T(8,128)(2,1)S(1)} %shard_map.68), channel_id=1, source_target_pairs={{2,1},{4,3},{6,5},{10,9},{12,11},{14,13},{18,17},{20,19},{22,21},{... | collective-permute-start | bytes 786440 | tf_op jit(solution)/shard_map/ppermute | solution.py:31

commit v8 on v7

--- a/solution.py
+++ b/solution.py
@@ -35,10 +35,6 @@
     return moved(value, lambda i: i + 1 if i % 2 else i + 3)
 
 
-def three_one(value):
-    return moved(value, lambda i: i + 3 if i % 2 else i + 1)
-
-
 def swapped(value):
     return moved(value, lambda i: i ^ 1)
 
@@ -165,10 +161,24 @@
         keep_exponentials(s, dp_ref[:, column], column, stats_ref, p_ref)
 
 
-def block_kernel(offset_of, n_lens, *refs):
-    docs_ref, q_ref, d_ref, kv_ref, stats_ref, p_ref, dp_ref, bias_scr, s_scr = refs
+def pick(even_ref, odd_ref, picked_ref, width):
+    odd = is_odd()
+
+    @pl.when(odd == 0)
+    def _():
+        picked_ref[...] = even_ref[:, :width]
+
+    @pl.when(odd == 1)
+    def _():
+        picked_ref[...] = odd_ref[:, :width]
+
+
+def block_kernel(offset, n_lens, *refs):
+    docs_ref, q_ref, d_ref, even_ref, odd_ref, stats_ref, p_ref, dp_ref = refs[:8]
+    bias_scr, s_scr, kv_scr = refs[8:]
     rows = q_ref.shape[0]
-    needed = reaches(docs_ref, offset_of())
+    needed = reaches(docs_ref, offset)
+    kv_ref = kv_scr if offset == 1 else even_ref
 
     def first(i):
         s_scr[i % SLOTS] = scores_of(kv_ref, q_ref, i) + twice(bias_scr[...])
@@ -180,7 +190,9 @@
 
     @pl.when(needed)
     def _():
-        bias_scr[...] = bias_of(docs_ref[0:1], offset_of(), 0.0)
+        if offset == 1:
+            pick(even_ref, odd_ref, kv_scr, kv_scr.shape[1])
+        bias_scr[...] = bias_of(docs_ref[0:1], offset, 0.0)
         pipelined([first, second])
 
     @pl.when(jnp.logical_not(needed))
@@ -192,13 +204,12 @@
 
 
 def far_kernel(n_lens, *refs):
-    docs_ref, q_ref, d_ref, kv_ref = refs[:4]
-    stats_refs = refs[4:7]
-    final_ref, ds_ref, g_ref = refs[7:10]
-    bias_scr, s_scr, dp_scr, p_scr, row_scr, w_scr = refs[10:]
+    docs_ref, q_ref, d_ref, even_ref, odd_ref = refs[:5]
+    stats_refs = refs[5:8]
+    final_ref, ds_ref, g_ref = refs[8:11]
+    bias_scr, s_scr, dp_scr, p_scr, row_scr, w_scr, kv_ref = refs[11:]
     rows = q_ref.shape[0]
-    offset = 3 - 2 * is_odd()
-    needed = reaches(docs_ref, offset)
+    needed = reaches(docs_ref, REACH)
 
     def combined(top, column, total, dot):
         shares = [jnp.exp2((ref[0:1, column] - top) * RATE) for ref in stats_refs]
@@ -248,7 +259,8 @@
 
     @pl.when(needed)
     def _():
-        bias_scr[...] = bias_of(docs_ref[0:1], offset, 0.0)
+        pick(even_ref, odd_ref, kv_ref, kv_ref.shape[1])
+        bias_scr[...] = bias_of(docs_ref[0:1], REACH, 0.0)
         pipelined([first, second, third, at_group_end(gradients)])
 
     @pl.when(jnp.logical_not(needed))
@@ -262,53 +274,75 @@
 
 
 def mid_kernel(n_lens, *refs):
-    docs_ref, q_ref, d_ref, p1_ref, dp1_ref, p2_ref, dp2_ref, final_ref, far_ref = refs[:9]
-    near_ref, pair_ref, ds_ref, w_scr = refs[9:]
+    docs_ref, q_ref, d_ref, p1_ref, dp1_ref, p2_ref, dp2_ref, final_ref = refs[:8]
+    near_ref, pair_ref, ds_ref, w_scr = refs[8:]
     rows = q_ref.shape[0]
-    needed = reaches(docs_ref, 1 + is_odd())
-    pair_ref[rows:] = far_ref[...]
-
-    def first(i):
-        column = at(i, 2 * rows)
-        for b, (p_ref, dp_ref) in enumerate(((p1_ref, dp1_ref), (p2_ref, dp2_ref))):
-            w = p_ref[:, column] * final_ref[b + 2:b + 3, column]
-            ds = (w * (dp_ref[:, column] - final_ref[0:1, column])).astype(BF16)
-            ds_ref[at(b, rows), column] = ds
-            w_scr[i // PER_GROUP % 2, at(b, rows), at(i % PER_GROUP, 2 * rows)] = w.astype(BF16)
-
-    def key_grads(group):
-        dk = lax.dot_general(
-            ds_ref[:, at(group, GROUP * rows)], stacked(q_ref, group * GROUP, GROUP), NN,
-            preferred_element_type=F32,
-        )
-        dk = (dk * SCALE).astype(BF16)
-        near_ref[:, at(group, HD)] = dk[:rows]
-        pair_ref[:rows, at(group, HD)] = dk[rows:]
-
-    def value_grads(group):
-        dv = lax.dot_general(
-            w_scr[group % 2], stacked(d_ref, group * GROUP, GROUP), NN, preferred_element_type=F32
-        ).astype(BF16)
-        near_ref[:, at(HK + group, HD)] = dv[:rows]
-        pair_ref[:rows, at(HK + group, HD)] = dv[rows:]
-
-    @pl.when(needed)
-    def _():
+    terms = ((p1_ref, dp1_ref), (p2_ref, dp2_ref))
+
+    def gradients_of(count):
+        part = slice(0, count * rows)
+
+        def first(i):
+            column = at(i, 2 * rows)
+            for b, (p_ref, dp_ref) in enumerate(terms[:count]):
+                w = p_ref[:, column] * final_ref[b + 2:b + 3, column]
+                ds = (w * (dp_ref[:, column] - final_ref[0:1, column])).astype(BF16)
+                ds_ref[at(b, rows), column] = ds
+                w_scr[i // PER_GROUP % 2, at(b, rows), at(i % PER_GROUP, 2 * rows)] = w.astype(BF16)
+
+        def write(columns, value):
+            near_ref[:, columns] = value[:rows]
+            pair_ref[rows:, columns] = value[:rows]
+            if count == 2:
+                pair_ref[:rows, columns] = value[rows:]
+
+        def key_grads(group):
+            dk = lax.dot_general(
+                ds_ref[part, at(group, GROUP * rows)], stacked(q_ref, group * GROUP, GROUP), NN,
+                preferred_element_type=F32,
+            )
+            write(at(group, HD), (dk * SCALE).astype(BF16))
+
+        def value_grads(group):
+            dv = lax.dot_general(
+                w_scr[group % 2, part], stacked(d_ref, group * GROUP, GROUP), NN,
+                preferred_element_type=F32,
+            )
+            write(at(HK + group, HD), dv.astype(BF16))
+
         pipelined([first, at_group_end(key_grads), at_group_end(value_grads)])
 
-    @pl.when(jnp.logical_not(needed))
-    def _():
+    near_needed, side_needed = reaches(docs_ref, 1), reaches(docs_ref, 2)
+
+    @pl.when(side_needed)
+    def _():
+        gradients_of(2)
+
+    @pl.when(jnp.logical_not(side_needed))
+    def _():
+        ds_ref[rows:] = jnp.zeros_like(ds_ref[rows:])
+        pair_ref[:rows] = jnp.zeros_like(near_ref)
+
+    @pl.when(jnp.logical_and(near_needed, jnp.logical_not(side_needed)))
+    def _():
+        gradients_of(1)
+
+    @pl.when(jnp.logical_not(near_needed))
+    def _():
+        ds_ref[:rows] = jnp.zeros_like(ds_ref[:rows])
         near_ref[...] = jnp.zeros_like(near_ref)
-        pair_ref[:rows] = jnp.zeros_like(near_ref)
-        ds_ref[...] = jnp.zeros_like(ds_ref)
-
-
-def sum_kernel(n_lens, near_ref, pair_ref, *refs):
+        pair_ref[rows:] = jnp.zeros_like(near_ref)
+
+
+def odd_sum_kernel(n_lens, far_ref, pair_ref, sum_ref):
+    rows = far_ref.shape[0]
+    sum_ref[...] = (far_ref[...].astype(F32) + pair_ref[:rows].astype(F32)).astype(BF16)
+
+
+def even_sum_kernel(n_lens, near_ref, pair_ref, relayed_ref, sum_ref):
     rows = near_ref.shape[0]
     total = near_ref[...].astype(F32) + pair_ref[:rows].astype(F32)
-    for ref in refs[:-1]:
-        total = total + ref[...].astype(F32)
-    refs[-1][...] = total.astype(BF16)
+    sum_ref[...] = (total + relayed_ref[...].astype(F32)).astype(BF16)
 
 
 def finish_kernel(n_lens, own_ref, pair_ref, odd_ref, even_ref, total_ref):
@@ -320,10 +354,13 @@
 
 
 def query_kernel(n_lens, *refs):
-    q_ref, d_ref, kv0_ref, kv1_ref, kv2_ref, kv3_ref = refs[:6]
-    p_ref, dp_ref, final_ref, mid_ref, far_ref, dq_ref, own_ref, kt_scr, ds_scr, w_scr = refs[6:]
+    q_ref, d_ref, kv_ref, across_ref, chip_ref, side_ref, far_ref = refs[:7]
+    p_ref, dp_ref, final_ref, mid_ref, ds_far_ref, dq_ref, own_ref = refs[7:14]
+    kt_scr, ds_scr, w_scr, near_scr, far_scr = refs[14:]
     rows = q_ref.shape[0]
-    kv_refs = [kv0_ref, kv1_ref, kv2_ref, kv3_ref]
+    pick(across_ref, chip_ref, near_scr, near_scr.shape[1])
+    pick(far_ref, across_ref, far_scr, far_scr.shape[1])
+    kv_refs = [kv_ref, near_scr, side_ref, far_scr]
 
     def first(i):
         group = i // PER_GROUP
@@ -340,7 +377,7 @@
         half, part = i // PER_GROUP % 2, at(i % PER_GROUP, 2 * rows)
         column = at(i, 2 * rows)
         ds = jnp.concatenate(
-            [ds_scr[half, :, part], mid_ref[:, column], far_ref[:, column]], axis=0
+            [ds_scr[half, :, part], mid_ref[:, column], ds_far_ref[:, column]], axis=0
         )
         dqt = lax.dot_general(kt_scr[i // PER_GROUP], ds, NN, preferred_element_type=F32)
         dq = (dqt * SCALE).astype(BF16).T
@@ -386,16 +423,21 @@
     square = array((rows, HQ * rows), F32)
     stat = array((8, HQ * rows), F32)
 
-    def exponentials(block_kv, offset_of):
+    def exponentials(even_kv, odd_kv, offset):
         return call(
-            functools.partial(block_kernel, offset_of), (), (docs, q, dout, block_kv),
-            [stat, square, square],
-            [pltpu.VMEM((rows, rows), F32), pltpu.VMEM((SLOTS, rows, 2 * rows), F32)],
+            functools.partial(block_kernel, offset), (),
+            (docs, q, dout, even_kv, odd_kv), [stat, square, square],
+            [
+                pltpu.VMEM((rows, rows), F32),
+                pltpu.VMEM((SLOTS, rows, 2 * rows), F32),
+                pltpu.VMEM((rows, wide), BF16),
+            ],
             2 * rows, 4,
         )
 
-    near = one_three(kv)
-    far = three_one(kv)
+    across = one_three(kv)
+    far = moved(kv, lambda i: i + 3 if i % 2 else -1)
+    chip = swapped(kv)
     lens = all_lengths(doc_lengths)
     (causal,) = call(causal_kernel, (), (), [array((rows, rows), F32)], [], 100 * keys, 1)
     s_own, dp_own = call(products_kernel, (), (q, dout, kv), [square, square], [], 2 * rows, 4)
@@ -404,23 +446,23 @@
         [stat, square, array((8, rows), jnp.int32)], [pltpu.VMEM((rows, rows), F32)],
         rows, 2,
     )
-    side = swapped(near)
-    near_stats, p_near, dp_near = exponentials(near, lambda: 1 + 2 * is_odd())
-    side_stats, p_side, dp_side = exponentials(side, lambda: 2)
+    side = swapped(across)
+    near_stats, p_near, dp_near = exponentials(across, chip, 1)
+    side_stats, p_side, dp_side = exponentials(side, side, 2)
     final, ds_far, g_far = call(
         far_kernel, (),
-        (docs, q, dout, far, own_stats, near_stats, side_stats),
+        (docs, q, dout, far, across, own_stats, near_stats, side_stats),
         [stat, array((rows, HQ * rows), BF16), block],
         [pltpu.VMEM((rows, rows), F32)]
         + [pltpu.VMEM((SLOTS, rows, 2 * rows), F32)] * 3
         + [pltpu.VMEM((SLOTS, 8, 2 * rows), F32)]
-        + [pltpu.VMEM((2, rows, GROUP * rows), BF16)],
+        + [pltpu.VMEM((2, rows, GROUP * rows), BF16), pltpu.VMEM((rows, wide), BF16)],
         4 * rows, 6,
     )
     relayed = moved(g_far, lambda i: -1 if i % 2 or i < REACH else i - 2)
     g_near, g_pair, ds_mid = call(
         mid_kernel, (),
-        (docs, q, dout, p_near, dp_near, p_side, dp_side, final, g_far),
+        (docs, q, dout, p_near, dp_near, p_side, dp_side, final),
         [
             block,
             array((2 * rows, wide), BF16),
@@ -429,16 +471,17 @@
         [pltpu.VMEM((2, 2 * rows, GROUP * rows), BF16)], 4 * rows, 4,
     )
     pair_back = swapped(g_pair)
-    (odd_sum,) = call(sum_kernel, (), (g_near, pair_back), [block], [], 1, 1)
+    (odd_sum,) = call(odd_sum_kernel, (), (g_far, pair_back), [block], [], 1, 1)
     odd_back = moved(odd_sum, lambda i: i - 3 if i % 2 else -1)
-    (joined,) = call(sum_kernel, (), (g_near, pair_back, relayed), [block], [], 1, 1)
+    (joined,) = call(even_sum_kernel, (), (g_near, pair_back, relayed), [block], [], 1, 1)
     even_back = moved(joined, lambda i: -1 if i % 2 else i - 1)
     dq, own = call(
         query_kernel, (),
-        (q, dout, kv, near, side, far, p_own, dp_own, final, ds_mid, ds_far),
+        (q, dout, kv, across, chip, side, far, p_own, dp_own, final, ds_mid, ds_far),
         [array(q.shape, BF16), array((rows, wide), F32)],
         [pltpu.VMEM((HK, HD, keys), BF16)]
-        + [pltpu.VMEM((2, rows, GROUP * rows), BF16)] * 2,
+        + [pltpu.VMEM((2, rows, GROUP * rows), BF16)] * 2
+        + [pltpu.VMEM((rows, HK * HD), BF16)] * 2,
         2 * rows + keys, 6,
     )
     (total,) = call(finish_kernel, (), (own, pair_back, odd_back, even_back), [block], [], 1, 3)

time: 45.9 us -> 46 us (level)
  waiting for transfers between devices: 21.5 us -> 22 us
    ppermute x7 -> x8, waiting for transfers between devices: 20.3 us -> 20.8 us  [moved(): lax.ppermute(value, 'ctx', [(s, t) for s, t in pairs if 0 <= t < count])]
    ppermute x7 -> x8, starting transfers between devices: 11.8 us -> 11.9 us  [moved(): lax.ppermute(value, 'ctx', [(s, t) for s, t in pairs if 0 <= t < count])]
  transfers between devices with their start and end apart: 9 -> 10, of which waited for: 4 -> 4; matrix products, arithmetic and copies ran while one was open for 0% -> 0% of each run, Pallas kernels for 12% -> 14%
where the time goes in v8:
time: 46 us; the launch traced here: 45.9 us
  waiting for transfers between devices  22 us (48%)
  starting transfers between devices  14.4 us (31%)
  Pallas kernels  8.5 us (18%)
  between operations  0.85 us (2%)
    ppermute x8, waiting for transfers between devices, moved(): lax.ppermute(value, 'ctx', [(s, t) for s, t in pairs if 0 <= t < count])  20.8 us
    ppermute x8, starting transfers between devices, moved(): lax.ppermute(value, 'ctx', [(s, t) for s, t in pairs if 0 <= t < count])  11.9 us
    pallas_call x11, Pallas kernels, call(): pl.pallas_call(functools.partial(body, len(lens)), in_specs=specs, out_sp...  8.5 us
    ppermute x2, starting transfers between devices, all_lengths(): lax.ppermute(jnp.concatenate(pieces), 'pipe', [(i, i ^ stride) for i in r...  2.52 us
    ppermute x2, waiting for transfers between devices, all_lengths(): lax.ppermute(jnp.concatenate(pieces), 'pipe', [(i, i ^ stride) for i in r...  1.18 us
  transfers between devices with their start and end apart: 10, of which 4 were waited for; matrix products, arithmetic and copies ran while one was open for 0% of the time, Pallas kernels for 14%

profile of v8, /device:TPU:1, one launch (start us, length us, event | category | flops | bytes accessed | tf_op | source)
XLA Modules:
  0.0 45.9 jit_solution(1834545578465636190)
XLA Ops:
  0.6 0.0 copy-start
  0.6 0.0 copy-start.1
  0.6 0.0 copy-start.2
  0.7 4.7 %collective-permute-start = (bf16[128,1024]{1,0:T(8,128)(2,1)}, bf16[128,1024]{1,0:T(8,128)(2,1)S(1)}, u32[]{:S(2)}, u32[]{:S(2)}) collective-permute-start(bf16[128,1024]{1,0:T(8,128)(2,1)} %bitcast.17), channel_id=1, source_target_pairs={{0,3},{1,2},{2,5},{3,4},{4,7},{5,6},{8,11},{9,10},{10,13},{11,12},... | collective-permute-start | bytes 786440 | tf_op jit(solution)/shard_map/ppermute | solution.py:31
  5.4 3.9 %collective-permute-start.3 = (bf16[128,1024]{1,0:T(8,128)(2,1)}, bf16[128,1024]{1,0:T(8,128)(2,1)S(1)}, u32[]{:S(2)}, u32[]{:S(2)}) collective-permute-start(bf16[128,1024]{1,0:T(8,128)(2,1)} %bitcast.18), channel_id=1, source_target_pairs={{1,4},{3,6},{9,12},{11,14},{17,20},{19,22},{25,28},{27,30}} | collective-permute-start | bytes 786440 | tf_op jit(solution)/shard_map/ppermute | solution.py:31
  9.3 0.1 collective-permute-start.1
  9.4 1.3 %collective-permute-start.4 = (s32[2]{0:T(128)}, s32[2]{0:T(128)S(1)}, u32[]{:S(2)}, u32[]{:S(2)}) collective-permute-start(s32[2]{0:T(128)} %refs_0_.1), channel_id=1, source_target_pairs={{0,8},{8,0},{16,24},{24,16},{1,9},{9,1},{17,25},{25,17},{2,10},{10... | collective-permute-start | bytes 32 | tf_op jit(solution)/shard_map/ppermute | solution.py:47
  10.7 1.1 %collective-permute-done.refs_3_.refs_4_ = bf16[128,1024]{1,0:T(8,128)(2,1)S(1)} collective-permute-done((bf16[128,1024]{1,0:T(8,128)(2,1)}, bf16[128,1024]{1,0:T(8,128)(2,1)S(1)}, u32[]{:S(2)}, u32[]{:S(2)}) %collective-permute-start) | collective-permute-done | bytes 262176 | tf_op jit(solution)/shard_map/ppermute | solution.py:31
  11.8 0.4 collective-permute-start.2
  12.2 0.0 copy-start.3
  12.2 0.0 copy-done
  12.2 0.0 copy-done.1
  12.3 0.0 copy-done.2
  12.3 0.7 %shard_map.59 = (f32[128,4096]{1,0:T(8,128)S(1)}, f32[128,4096]{1,0:T(8,128)S(1)}) custom-call(bf16[128,4096]{1,0:T(8,128)(2,1)S(1)} %bitcast.5, bf16[128,4096]{1,0:T(8,128)(2,1)S(1)} %bitcast.11, bf16[128,1024]{1,0:T(8,128)(2,1)S(1)} %bitcast.20), custom_call_target="tpu_custom_call" | custom-call | flops 268435456 | bytes 6553600 | tf_op jit(solution)/shard_map/pallas_call | solution.py:402
  13.0 0.0 collective-permute-done.4.refs_1_
  13.0 0.0 copy-done.3
  13.0 0.1 pad_add_fusion
  13.1 1.2 %collective-permute-start.5 = (s32[4]{0:T(128)S(1)}, s32[4]{0:T(128)S(1)}, u32[]{:S(2)}, u32[]{:S(2)}) collective-permute-start(s32[4]{0:T(128)S(1)} %pad_add_fusion), channel_id=1, source_target_pairs={{0,16},{8,24},{16,0},{24,8},{1,17},{9,25},{17,1},{25,9},{2,18},{10... | collective-permute-start | bytes 56 | tf_op jit(solution)/shard_map/ppermute | solution.py:47
  14.3 1.2 %collective-permute-done.5.refs_2_ = s32[4]{0:T(128)S(1)} collective-permute-done((s32[4]{0:T(128)S(1)}, s32[4]{0:T(128)S(1)}, u32[]{:S(2)}, u32[]{:S(2)}) %collective-permute-start.5) | collective-permute-done | bytes 48 | tf_op jit(solution)/shard_map/ppermute | solution.py:47
  15.5 1.3 %shard_map.61 = (f32[8,4096]{1,0:T(8,128)S(1)}, f32[128,4096]{1,0:T(8,128)S(1)}, s32[8,128]{1,0:T(8,128)S(1)}) custom-call(s32[2]{0:T(128)S(1)} %copy-done.3, s32[2]{0:T(128)S(1)} %collective-permute-done.4.refs_1_, s32[4]{0:T(128)S(1)} %collective-permute-done.5.refs_2_, f32[128,4096]{1,0:T(8,128)S(1)} %get-tuple-element.21.refs_3_, ...), custom_call_target="tpu_custom_call" | custom-call | flops 134217728 | bytes 6492160 | tf_op jit(solution)/shard_map/pallas_call | solution.py:402
  16.8 0.0 collective-permute-done.1.refs_4_
  16.8 1.3 %shard_map.62 = (f32[8,4096]{1,0:T(8,128)S(1)}, f32[128,4096]{1,0:T(8,128)S(1)}, f32[128,4096]{1,0:T(8,128)S(1)}) custom-call(s32[8,128]{1,0:T(8,128)S(1)} %get-tuple-element.24.refs_0_, bf16[128,4096]{1,0:T(8,128)(2,1)S(1)} %bitcast.6, bf16[128,4096]{1,0:T(8,128)(2,1)S(1)} %bitcast.12, bf16[128,1024]{1,0:T(8,128)(2,1)S(1)} %collective-permute-done.refs_3_.refs_4_, ...), custom_call_target="tpu_custom_call" | custom-call | flops 268435456 | bytes 6950912 | tf_op jit(solution)/shard_map/pallas_call | solution.py:402
  18.1 0.0 collective-permute-done.2.refs_3_.refs_4_.refs_5_
  18.1 0.3 shard_map.63
  18.5 0.0 collective-permute-done.3.refs_3_.refs_6_
  18.5 0.1 shard_map.64
  18.6 1.1 %shard_map.65 = (bf16[128,1024]{1,0:T(8,128)(2,1)S(1)}, bf16[256,1024]{1,0:T(8,128)(2,1)S(1)}, bf16[256,4096]{1,0:T(8,128)(2,1)S(1)}) custom-call(s32[8,128]{1,0:T(8,128)S(1)} %get-tuple-element.24.refs_0_, bf16[128,4096]{1,0:T(8,128)(2,1)S(1)} %bitcast.9, bf16[128,4096]{1,0:T(8,128)(2,1)S(1)} %bitcast.15, f32[128,4096]{1,0:T(8,128)S(1)} %get-tuple-element.29.refs_3_, ...), custom_call_target="tpu_custom_call" | custom-call | flops 536870912 | bytes 13504512 | tf_op jit(solution)/shard_map/pallas_call | solution.py:402
  19.7 0.1 collective-permute-start.6
  19.8 0.7 %collective-permute-start.8 = (bf16[128,1024]{1,0:T(8,128)(2,1)S(1)}, bf16[128,1024]{1,0:T(8,128)(2,1)S(1)}, u32[]{:S(2)}, u32[]{:S(2)}) collective-permute-start(bf16[128,1024]{1,0:T(8,128)(2,1)S(1)} %get-tuple-element.38.far_ref), channel_id=1, source_target_pairs={{4,2},{6,4},{12,10},{14,12},{20,18},{22,20},{28,26},{30,28}} | collective-permute-start | bytes 786440 | tf_op jit(solution)/shard_map/ppermute | solution.py:31
  20.5 1.2 %collective-permute-done.6.pair_ref = bf16[256,1024]{1,0:T(8,128)(2,1)S(1)} collective-permute-done((bf16[256,1024]{1,0:T(8,128)(2,1)S(1)}, bf16[256,1024]{1,0:T(8,128)(2,1)S(1)}, u32[]{:S(2)}, u32[]{:S(2)}) %collective-permute-start.6) | collective-permute-done | bytes 524320 | tf_op jit(solution)/shard_map/ppermute | solution.py:31
  21.7 0.1 shard_map.67
  21.8 0.7 %collective-permute-start.7 = (bf16[128,1024]{1,0:T(8,128)(2,1)S(1)}, bf16[128,1024]{1,0:T(8,128)(2,1)S(1)}, u32[]{:S(2)}, u32[]{:S(2)}) collective-permute-start(bf16[128,1024]{1,0:T(8,128)(2,1)S(1)} %shard_map.67), channel_id=1, source_target_pairs={{3,0},{5,2},{7,4},{11,8},{13,10},{15,12},{19,16},{21,18},{23,20},{... | collective-permute-start | bytes 786440 | tf_op jit(solution)/shard_map/ppermute | solution.py:31
  22.5 0.0 collective-permute-done.8.relayed_ref
  22.5 0.1 shard_map.68
  22.6 1.3 %collective-permute-start.9 = (bf16[128,1024]{1,0:T(8,128)(2,1)S(1)}, bf16[128,1024]{1,0:T(8,128)(2,1)S(1)}, u32[]{:S(2)}, u32[]{:S(2)}) collective-permute-start(bf16[128,1024]{1,0:T(8,128)(2,1)S(1)} %shard_map.68), channel_id=1, source_target_pairs={{2,1},{4,3},{6,5},{10,9},{12,11},{14,13},{18,17},{20,19},{22,21},{... | collective-permute-start | bytes 786440 | tf_op jit(solution)/shard_map/ppermute | solution.py:31
  23.9 2.6 %shard_map.66 = (bf16[128,4096]{1,0:T(8,128)(2,1)}, f32[128,1024]{1,0:T(8,128)S(1)}) custom-call(bf16[128,4096]{1,0:T(8,128)(2,1)S(1)} %bitcast.10, bf16[128,4096]{1,0:T(8,128)(2,1)S(1)} %bitcast.16, bf16[128,1024]{1,0:T(8,128)(2,1)S(1)} %bitcast.21, bf16[128,1024]{1,0:T(8,128)(2,1)S(1)} %collective-permute-done.refs_3_.refs_4_, ...), custom_call_target="tpu_custom_call" | custom-call | flops 805306368 | bytes 12451840 | tf_op jit(solution)/shard_map/pallas_call | solution.py:402
  26.5 0.0 collective-permute-done.7.odd_ref
  26.5 18.5 %collective-permute-done.9.even_ref = bf16[128,1024]{1,0:T(8,128)(2,1)S(1)} collective-permute-done((bf16[128,1024]{1,0:T(8,128)(2,1)S(1)}, bf16[128,1024]{1,0:T(8,128)(2,1)S(1)}, u32[]{:S(2)}, u32[]{:S(2)}) %collective-permute-start.9) | collective-permute-done | bytes 262176 | tf_op jit(solution)/shard_map/ppermute | solution.py:31
  45.0 0.8 %shard_map.69 = bf16[128,1024]{1,0:T(8,128)(2,1)} custom-call(f32[128,1024]{1,0:T(8,128)S(1)} %get-tuple-element.36.own_ref, bf16[256,1024]{1,0:T(8,128)(2,1)S(1)} %collective-permute-done.6.pair_ref, bf16[128,1024]{1,0:T(8,128)(2,1)S(1)} %collective-permute-done.7.odd_ref, bf16[128,1024]{1,0:T(8,128)(2,1)S(1)} %collective-permute-done.9.even_ref), custom_call_target="tpu_custom_call" | custom-call | flops 1048576 | bytes 1835008 | tf_op jit(solution)/shard_map/pallas_call | solution.py:402
  (1 shorter events, 0.0 us)
Async XLA Ops:
  0.6 11.6 %copy-start = (bf16[1,128,4096]{2,1,0:T(8,128)(2,1)S(1)}, bf16[1,128,4096]{2,1,0:T(8,128)(2,1)}, u32[]{:S(2)}) copy-start(bf16[1,128,4096]{2,1,0:T(8,128)(2,1)} %param.4) | copy-start | bytes 3145732
  0.6 11.6 %copy-start.1 = (bf16[1,128,4096]{2,1,0:T(8,128)(2,1)S(1)}, bf16[1,128,4096]{2,1,0:T(8,128)(2,1)}, u32[]{:S(2)}) copy-start(bf16[1,128,4096]{2,1,0:T(8,128)(2,1)} %param.6) | copy-start | bytes 3145732
  0.6 11.6 %copy-start.2 = (bf16[1,128,1024]{2,1,0:T(8,128)(2,1)S(1)}, bf16[1,128,1024]{2,1,0:T(8,128)(2,1)}, u32[]{:S(2)}) copy-start(bf16[1,128,1024]{2,1,0:T(8,128)(2,1)} %param.5) | copy-start | bytes 786436
  0.7 11.1 %collective-permute-start = (bf16[128,1024]{1,0:T(8,128)(2,1)}, bf16[128,1024]{1,0:T(8,128)(2,1)S(1)}, u32[]{:S(2)}, u32[]{:S(2)}) collective-permute-start(bf16[128,1024]{1,0:T(8,128)(2,1)} %bitcast.17), channel_id=1, source_target_pairs={{0,3},{1,2},{2,5},{3,4},{4,7},{5,6},{8,11},{9,10},{10,13},{11,12},... | collective-permute-start | bytes 786440 | tf_op jit(solution)/shard_map/ppermute | solution.py:31
  5.4 13.1 %collective-permute-start.3 = (bf16[128,1024]{1,0:T(8,128)(2,1)}, bf16[128,1024]{1,0:T(8,128)(2,1)S(1)}, u32[]{:S(2)}, u32[]{:S(2)}) collective-permute-start(bf16[128,1024]{1,0:T(8,128)(2,1)} %bitcast.18), channel_id=1, source_target_pairs={{1,4},{3,6},{9,12},{11,14},{17,20},{19,22},{25,28},{27,30}} | collective-permute-start | bytes 786440 | tf_op jit(solution)/shard_map/ppermute | solution.py:31
  9.3 7.5 %collective-permute-start.1 = (bf16[128,1024]{1,0:T(8,128)(2,1)}, bf16[128,1024]{1,0:T(8,128)(2,1)S(1)}, u32[]{:S(2)}, u32[]{:S(2)}) collective-permute-start(bf16[128,1024]{1,0:T(8,128)(2,1)} %bitcast.19), channel_id=1, source_target_pairs={{0,1},{1,0},{2,3},{3,2},{4,5},{5,4},{6,7},{7,6},{8,9},{9,8},{10,11... | collective-permute-start | bytes 786440 | tf_op jit(solution)/shard_map/ppermute | solution.py:31
  9.4 3.6 %collective-permute-start.4 = (s32[2]{0:T(128)}, s32[2]{0:T(128)S(1)}, u32[]{:S(2)}, u32[]{:S(2)}) collective-permute-start(s32[2]{0:T(128)} %refs_0_.1), channel_id=1, source_target_pairs={{0,8},{8,0},{16,24},{24,16},{1,9},{9,1},{17,25},{25,17},{2,10},{10... | collective-permute-start | bytes 32 | tf_op jit(solution)/shard_map/ppermute | solution.py:47
  11.8 6.3 %collective-permute-start.2 = (bf16[128,1024]{1,0:T(8,128)(2,1)S(1)}, bf16[128,1024]{1,0:T(8,128)(2,1)S(1)}, u32[]{:S(2)}, u32[]{:S(2)}) collective-permute-start(bf16[128,1024]{1,0:T(8,128)(2,1)S(1)} %collective-permute-done.refs_3_.refs_4_), channel_id=1, source_target_pairs={{0,1},{1,0},{2,3},{3,2},{4,5},{5,4},{6,7},{7,6},{8,9},{9,8},{10,11... | collective-permute-start | bytes 786440 | tf_op jit(solution)/shard_map/ppermute | solution.py:31
  12.2 0.8 %copy-start.3 = (s32[2]{0:T(128)S(1)}, s32[2]{0:T(128)}, u32[]{:S(2)}) copy-start(s32[2]{0:T(128)} %refs_0_.1) | copy-start | bytes 28
  13.1 2.4 %collective-permute-start.5 = (s32[4]{0:T(128)S(1)}, s32[4]{0:T(128)S(1)}, u32[]{:S(2)}, u32[]{:S(2)}) collective-permute-start(s32[4]{0:T(128)S(1)} %pad_add_fusion), channel_id=1, source_target_pairs={{0,16},{8,24},{16,0},{24,8},{1,17},{9,25},{17,1},{25,9},{2,18},{10... | collective-permute-start | bytes 56 | tf_op jit(solution)/shard_map/ppermute | solution.py:47
  19.7 2.0 %collective-permute-start.6 = (bf16[256,1024]{1,0:T(8,128)(2,1)S(1)}, bf16[256,1024]{1,0:T(8,128)(2,1)S(1)}, u32[]{:S(2)}, u32[]{:S(2)}) collective-permute-start(bf16[256,1024]{1,0:T(8,128)(2,1)S(1)} %get-tuple-element.37), channel_id=1, source_target_pairs={{0,1},{1,0},{2,3},{3,2},{4,5},{5,4},{6,7},{7,6},{8,9},{9,8},{10,11... | collective-permute-start | bytes 1572872 | tf_op jit(solution)/shard_map/ppermute | solution.py:31
  19.8 2.7 %collective-permute-start.8 = (bf16[128,1024]{1,0:T(8,128)(2,1)S(1)}, bf16[128,1024]{1,0:T(8,128)(2,1)S(1)}, u32[]{:S(2)}, u32[]{:S(2)}) collective-permute-start(bf16[128,1024]{1,0:T(8,128)(2,1)S(1)} %get-tuple-element.38.far_ref), channel_id=1, source_target_pairs={{4,2},{6,4},{12,10},{14,12},{20,18},{22,20},{28,26},{30,28}} | collective-permute-start | bytes 786440 | tf_op jit(solution)/shard_map/ppermute | solution.py:31
  21.8 4.7 %collective-permute-start.7 = (bf16[128,1024]{1,0:T(8,128)(2,1)S(1)}, bf16[128,1024]{1,0:T(8,128)(2,1)S(1)}, u32[]{:S(2)}, u32[]{:S(2)}) collective-permute-start(bf16[128,1024]{1,0:T(8,128)(2,1)S(1)} %shard_map.67), channel_id=1, source_target_pairs={{3,0},{5,2},{7,4},{11,8},{13,10},{15,12},{19,16},{21,18},{23,20},{... | collective-permute-start | bytes 786440 | tf_op jit(solution)/shard_map/ppermute | solution.py:31
  22.6 22.4 %collective-permute-start.9 = (bf16[128,1024]{1,0:T(8,128)(2,1)S(1)}, bf16[128,1024]{1,0:T(8,128)(2,1)S(1)}, u32[]{:S(2)}, u32[]{:S(2)}) collective-permute-start(bf16[128,1024]{1,0:T(8,128)(2,1)S(1)} %shard_map.68), channel_id=1, source_target_pairs={{2,1},{4,3},{6,5},{10,9},{12,11},{14,13},{18,17},{20,19},{22,21},{... | collective-permute-start | bytes 786440 | tf_op jit(solution)/shard_map/ppermute | solution.py:31

commit v9 on v8

--- a/solution.py
+++ b/solution.py
@@ -162,15 +162,7 @@
 
 
 def pick(even_ref, odd_ref, picked_ref, width):
-    odd = is_odd()
-
-    @pl.when(odd == 0)
-    def _():
-        picked_ref[...] = even_ref[:, :width]
-
-    @pl.when(odd == 1)
-    def _():
-        picked_ref[...] = odd_ref[:, :width]
+    picked_ref[...] = jnp.where(is_odd() == 1, odd_ref[:, :width], even_ref[:, :width])
 
 
 def block_kernel(offset, n_lens, *refs):
@@ -223,45 +215,62 @@
             final_ref[k + 1:k + 2, column] = share * inv
         return inv, delta
 
-    def first(i):
-        s_scr[i % SLOTS] = scores_of(kv_ref, q_ref, i) + twice(bias_scr[...])
-        dp_scr[i % SLOTS] = dweights_of(kv_ref, d_ref, i)
-
-    def second(i):
-        column = at(i, 2 * rows)
-        s = s_scr[i % SLOTS]
-        tops = [ref[0:1, column] for ref in stats_refs]
-        top = functools.reduce(jnp.maximum, tops, jnp.max(s, axis=0, keepdims=True))
-        p = jnp.exp2((s - top) * RATE)
-        p_scr[i % SLOTS] = p
-        total = jnp.sum(p, axis=0, keepdims=True)
-        dot = jnp.sum(p * dp_scr[i % SLOTS], axis=0, keepdims=True)
-        inv, delta = combined(top, column, total, dot)
-        row_scr[i % SLOTS, 0:1] = inv
-        row_scr[i % SLOTS, 1:2] = delta
-
-    def third(i):
-        w = p_scr[i % SLOTS] * row_scr[i % SLOTS, 0:1]
-        ds = (w * (dp_scr[i % SLOTS] - row_scr[i % SLOTS, 1:2])).astype(BF16)
-        ds_ref[:, at(i, 2 * rows)] = ds
-        w_scr[i // PER_GROUP % 2, :, at(i % PER_GROUP, 2 * rows)] = w.astype(BF16)
-
-    def gradients(group):
-        dk = lax.dot_general(
-            ds_ref[:, at(group, GROUP * rows)], stacked(q_ref, group * GROUP, GROUP), NN,
-            preferred_element_type=F32,
-        )
-        g_ref[:, at(group, HD)] = (dk * SCALE).astype(BF16)
-        dv = lax.dot_general(
-            w_scr[group % 2], stacked(d_ref, group * GROUP, GROUP), NN, preferred_element_type=F32
-        )
-        g_ref[:, at(HK + group, HD)] = dv.astype(BF16)
-
-    @pl.when(needed)
-    def _():
+    def run(skip):
+        used, kept = slice(skip, rows), slice(0, rows - skip)
+        kv_used = kv_ref.at[used]
+
+        def first(i):
+            s_scr[i % SLOTS, kept] = scores_of(kv_used, q_ref, i) + twice(bias_scr[used])
+            dp_scr[i % SLOTS, kept] = dweights_of(kv_used, d_ref, i)
+
+        def second(i):
+            column = at(i, 2 * rows)
+            s = s_scr[i % SLOTS, kept]
+            tops = [ref[0:1, column] for ref in stats_refs]
+            top = functools.reduce(jnp.maximum, tops, jnp.max(s, axis=0, keepdims=True))
+            p = jnp.exp2((s - top) * RATE)
+            p_scr[i % SLOTS, kept] = p
+            total = jnp.sum(p, axis=0, keepdims=True)
+            dot = jnp.sum(p * dp_scr[i % SLOTS, kept], axis=0, keepdims=True)
+            inv, delta = combined(top, column, total, dot)
+            row_scr[i % SLOTS, 0:1] = inv
+            row_scr[i % SLOTS, 1:2] = delta
+
+        def third(i):
+            w = p_scr[i % SLOTS, kept] * row_scr[i % SLOTS, 0:1]
+            ds = (w * (dp_scr[i % SLOTS, kept] - row_scr[i % SLOTS, 1:2])).astype(BF16)
+            ds_ref[used, at(i, 2 * rows)] = ds
+            w_scr[i // PER_GROUP % 2, kept, at(i % PER_GROUP, 2 * rows)] = w.astype(BF16)
+
+        def gradients(group):
+            dk = lax.dot_general(
+                ds_ref[used, at(group, GROUP * rows)], stacked(q_ref, group * GROUP, GROUP), NN,
+                preferred_element_type=F32,
+            )
+            g_ref[used, at(group, HD)] = (dk * SCALE).astype(BF16)
+            dv = lax.dot_general(
+                w_scr[group % 2, kept], stacked(d_ref, group * GROUP, GROUP), NN,
+                preferred_element_type=F32,
+            )
+            g_ref[used, at(HK + group, HD)] = dv.astype(BF16)
+
+        if skip:
+            g_ref[:skip] = jnp.zeros((skip, g_ref.shape[1]), BF16)
+            ds_ref[:skip] = jnp.zeros((skip, ds_ref.shape[1]), BF16)
         pick(even_ref, odd_ref, kv_ref, kv_ref.shape[1])
         bias_scr[...] = bias_of(docs_ref[0:1], REACH, 0.0)
         pipelined([first, second, third, at_group_end(gradients)])
+
+    doc_start = docs_ref[0:1, 0:1][0, 0]
+    middle = (lax.axis_index("ctx") - REACH) * rows + rows // 2
+
+    @pl.when(jnp.logical_and(needed, doc_start < middle))
+    def _():
+        run(0)
+
+    @pl.when(jnp.logical_and(needed, doc_start >= middle))
+    def _():
+        run(rows // 2)
 
     @pl.when(jnp.logical_not(needed))
     def _():
@@ -345,12 +354,22 @@
     sum_ref[...] = (total + relayed_ref[...].astype(F32)).astype(BF16)
 
 
-def finish_kernel(n_lens, own_ref, pair_ref, odd_ref, even_ref, total_ref):
+def finish_kernel(n_lens, own_ref, pair_ref, odd_ref, even_ref, total_hbm, total_scr, sems):
     rows = own_ref.shape[0]
     even = lax.rem(lax.axis_index("ctx"), 2) == 0
-    chip = pair_ref[rows:].astype(F32) + odd_ref[...].astype(F32)
-    moved_in = jnp.where(even, chip, even_ref[...].astype(F32))
-    total_ref[...] = (own_ref[...] + moved_in).astype(BF16)
+    parts = sems.shape[0]
+    step = rows // parts
+    copies = []
+    for k in range(parts):
+        part = at(k, step)
+        chip = pair_ref[rows + k * step:rows + (k + 1) * step].astype(F32)
+        chip = chip + odd_ref[part].astype(F32)
+        moved_in = jnp.where(even, chip, even_ref[part].astype(F32))
+        total_scr[part] = (own_ref[part] + moved_in).astype(BF16)
+        copies.append(pltpu.make_async_copy(total_scr.at[part], total_hbm.at[part], sems.at[k]))
+        copies[k].start()
+    for copy in copies:
+        copy.wait()
 
 
 def query_kernel(n_lens, *refs):
@@ -395,14 +414,14 @@
     pipelined([first, second, at_group_end(own_grads)])
 
 
-def call(body, lens, args, outs, scratch, matmul_rows, grant):
+def call(body, lens, args, outs, scratch, matmul_rows, grant, out_space=pltpu.VMEM):
     specs = [pl.BlockSpec(memory_space=pltpu.SMEM)] * len(lens)
     specs += [pl.BlockSpec(memory_space=pltpu.VMEM)] * len(args)
     docs = sum(x.shape[0] for x in lens)
     return pl.pallas_call(
         functools.partial(body, len(lens)),
         in_specs=specs,
-        out_specs=[pl.BlockSpec(memory_space=pltpu.VMEM)] * len(outs),
+        out_specs=[pl.BlockSpec(memory_space=out_space)] * len(outs),
         out_shape=outs,
         scratch_shapes=([pltpu.SMEM((docs,), jnp.int32)] if lens else []) + scratch,
         cost_estimate=pl.CostEstimate(
@@ -484,7 +503,10 @@
         + [pltpu.VMEM((rows, HK * HD), BF16)] * 2,
         2 * rows + keys, 6,
     )
-    (total,) = call(finish_kernel, (), (own, pair_back, odd_back, even_back), [block], [], 1, 3)
+    (total,) = call(
+        finish_kernel, (), (own, pair_back, odd_back, even_back), [block],
+        [pltpu.VMEM((rows, wide), BF16), pltpu.SemaphoreType.DMA((4,))], 1, 3, pltpu.HBM,
+    )
     return (dq[None], total[None])
 
 

time: 46 us -> 45.4 us (0.987)
  waiting for transfers between devices: 22 us -> 21.4 us
    ppermute x8, waiting for transfers between devices: 20.8 us -> 20.2 us  [moved(): lax.ppermute(value, 'ctx', [(s, t) for s, t in pairs if 0 <= t < count])]
where the time goes in v9:
time: 45.4 us; the launch traced here: 45.2 us
  waiting for transfers between devices  21.4 us (47%)
  starting transfers between devices  14.4 us (32%)
  Pallas kernels  8.49 us (19%)
  between operations  0.85 us (2%)
    ppermute x8, waiting for transfers between devices, moved(): lax.ppermute(value, 'ctx', [(s, t) for s, t in pairs if 0 <= t < count])  20.2 us
    ppermute x8, starting transfers between devices, moved(): lax.ppermute(value, 'ctx', [(s, t) for s, t in pairs if 0 <= t < count])  11.9 us
    pallas_call x11, Pallas kernels, call(): pl.pallas_call(functools.partial(body, len(lens)), in_specs=specs, out_sp...  8.49 us
    ppermute x2, starting transfers between devices, all_lengths(): lax.ppermute(jnp.concatenate(pieces), 'pipe', [(i, i ^ stride) for i in r...  2.52 us
    ppermute x2, waiting for transfers between devices, all_lengths(): lax.ppermute(jnp.concatenate(pieces), 'pipe', [(i, i ^ stride) for i in r...  1.18 us
  transfers between devices with their start and end apart: 10, of which 4 were waited for; matrix products, arithmetic and copies ran while one was open for 0% of the time, Pallas kernels for 14%

profile of v9, /device:TPU:1, one launch (start us, length us, event | category | flops | bytes accessed | tf_op | source)
XLA Modules:
  0.0 45.2 jit_solution(7400926319615834516)
XLA Ops:
  0.6 0.0 copy-start
  0.6 0.0 copy-start.1
  0.6 0.0 copy-start.2
  0.7 4.7 %collective-permute-start = (bf16[128,1024]{1,0:T(8,128)(2,1)}, bf16[128,1024]{1,0:T(8,128)(2,1)S(1)}, u32[]{:S(2)}, u32[]{:S(2)}) collective-permute-start(bf16[128,1024]{1,0:T(8,128)(2,1)} %bitcast.17), channel_id=1, source_target_pairs={{0,3},{1,2},{2,5},{3,4},{4,7},{5,6},{8,11},{9,10},{10,13},{11,12},... | collective-permute-start | bytes 786440 | tf_op jit(solution)/shard_map/ppermute | solution.py:31
  5.4 3.9 %collective-permute-start.3 = (bf16[128,1024]{1,0:T(8,128)(2,1)}, bf16[128,1024]{1,0:T(8,128)(2,1)S(1)}, u32[]{:S(2)}, u32[]{:S(2)}) collective-permute-start(bf16[128,1024]{1,0:T(8,128)(2,1)} %bitcast.18), channel_id=1, source_target_pairs={{1,4},{3,6},{9,12},{11,14},{17,20},{19,22},{25,28},{27,30}} | collective-permute-start | bytes 786440 | tf_op jit(solution)/shard_map/ppermute | solution.py:31
  9.3 0.1 collective-permute-start.1
  9.4 1.3 %collective-permute-start.4 = (s32[2]{0:T(128)}, s32[2]{0:T(128)S(1)}, u32[]{:S(2)}, u32[]{:S(2)}) collective-permute-start(s32[2]{0:T(128)} %refs_0_.1), channel_id=1, source_target_pairs={{0,8},{8,0},{16,24},{24,16},{1,9},{9,1},{17,25},{25,17},{2,10},{10... | collective-permute-start | bytes 32 | tf_op jit(solution)/shard_map/ppermute | solution.py:47
  10.7 1.1 %collective-permute-done.refs_3_.refs_4_ = bf16[128,1024]{1,0:T(8,128)(2,1)S(1)} collective-permute-done((bf16[128,1024]{1,0:T(8,128)(2,1)}, bf16[128,1024]{1,0:T(8,128)(2,1)S(1)}, u32[]{:S(2)}, u32[]{:S(2)}) %collective-permute-start) | collective-permute-done | bytes 262176 | tf_op jit(solution)/shard_map/ppermute | solution.py:31
  11.8 0.4 collective-permute-start.2
  12.2 0.0 copy-start.3
  12.2 0.0 copy-done
  12.2 0.0 copy-done.1
  12.3 0.0 copy-done.2
  12.3 0.7 %shard_map.59 = (f32[128,4096]{1,0:T(8,128)S(1)}, f32[128,4096]{1,0:T(8,128)S(1)}) custom-call(bf16[128,4096]{1,0:T(8,128)(2,1)S(1)} %bitcast.5, bf16[128,4096]{1,0:T(8,128)(2,1)S(1)} %bitcast.11, bf16[128,1024]{1,0:T(8,128)(2,1)S(1)} %bitcast.20), custom_call_target="tpu_custom_call" | custom-call | flops 268435456 | bytes 6553600 | tf_op jit(solution)/shard_map/pallas_call | solution.py:421
  13.0 0.0 collective-permute-done.4.refs_1_
  13.0 0.0 copy-done.3
  13.0 0.1 pad_add_fusion
  13.1 1.2 %collective-permute-start.5 = (s32[4]{0:T(128)S(1)}, s32[4]{0:T(128)S(1)}, u32[]{:S(2)}, u32[]{:S(2)}) collective-permute-start(s32[4]{0:T(128)S(1)} %pad_add_fusion), channel_id=1, source_target_pairs={{0,16},{8,24},{16,0},{24,8},{1,17},{9,25},{17,1},{25,9},{2,18},{10... | collective-permute-start | bytes 56 | tf_op jit(solution)/shard_map/ppermute | solution.py:47
  14.3 1.2 %collective-permute-done.5.refs_2_ = s32[4]{0:T(128)S(1)} collective-permute-done((s32[4]{0:T(128)S(1)}, s32[4]{0:T(128)S(1)}, u32[]{:S(2)}, u32[]{:S(2)}) %collective-permute-start.5) | collective-permute-done | bytes 48 | tf_op jit(solution)/shard_map/ppermute | solution.py:47
  15.5 1.3 %shard_map.61 = (f32[8,4096]{1,0:T(8,128)S(1)}, f32[128,4096]{1,0:T(8,128)S(1)}, s32[8,128]{1,0:T(8,128)S(1)}) custom-call(s32[2]{0:T(128)S(1)} %copy-done.3, s32[2]{0:T(128)S(1)} %collective-permute-done.4.refs_1_, s32[4]{0:T(128)S(1)} %collective-permute-done.5.refs_2_, f32[128,4096]{1,0:T(8,128)S(1)} %get-tuple-element.21.refs_3_, ...), custom_call_target="tpu_custom_call" | custom-call | flops 134217728 | bytes 6492160 | tf_op jit(solution)/shard_map/pallas_call | solution.py:421
  16.8 0.0 collective-permute-done.1.refs_4_
  16.8 1.3 %shard_map.62 = (f32[8,4096]{1,0:T(8,128)S(1)}, f32[128,4096]{1,0:T(8,128)S(1)}, f32[128,4096]{1,0:T(8,128)S(1)}) custom-call(s32[8,128]{1,0:T(8,128)S(1)} %get-tuple-element.24.refs_0_, bf16[128,4096]{1,0:T(8,128)(2,1)S(1)} %bitcast.6, bf16[128,4096]{1,0:T(8,128)(2,1)S(1)} %bitcast.12, bf16[128,1024]{1,0:T(8,128)(2,1)S(1)} %collective-permute-done.refs_3_.refs_4_, ...), custom_call_target="tpu_custom_call" | custom-call | flops 268435456 | bytes 6950912 | tf_op jit(solution)/shard_map/pallas_call | solution.py:421
  18.1 0.0 collective-permute-done.2.refs_3_.refs_4_.refs_5_
  18.1 0.3 shard_map.63
  18.4 0.0 collective-permute-done.3.refs_3_.refs_6_
  18.4 0.1 shard_map.64
  18.6 1.1 %shard_map.65 = (bf16[128,1024]{1,0:T(8,128)(2,1)S(1)}, bf16[256,1024]{1,0:T(8,128)(2,1)S(1)}, bf16[256,4096]{1,0:T(8,128)(2,1)S(1)}) custom-call(s32[8,128]{1,0:T(8,128)S(1)} %get-tuple-element.24.refs_0_, bf16[128,4096]{1,0:T(8,128)(2,1)S(1)} %bitcast.9, bf16[128,4096]{1,0:T(8,128)(2,1)S(1)} %bitcast.15, f32[128,4096]{1,0:T(8,128)S(1)} %get-tuple-element.29.refs_3_, ...), custom_call_target="tpu_custom_call" | custom-call | flops 536870912 | bytes 13504512 | tf_op jit(solution)/shard_map/pallas_call | solution.py:421
  19.7 0.1 collective-permute-start.6
  19.8 0.7 %collective-permute-start.8 = (bf16[128,1024]{1,0:T(8,128)(2,1)S(1)}, bf16[128,1024]{1,0:T(8,128)(2,1)S(1)}, u32[]{:S(2)}, u32[]{:S(2)}) collective-permute-start(bf16[128,1024]{1,0:T(8,128)(2,1)S(1)} %get-tuple-element.38.far_ref), channel_id=1, source_target_pairs={{4,2},{6,4},{12,10},{14,12},{20,18},{22,20},{28,26},{30,28}} | collective-permute-start | bytes 786440 | tf_op jit(solution)/shard_map/ppermute | solution.py:31
  20.5 1.2 %collective-permute-done.6.pair_ref = bf16[256,1024]{1,0:T(8,128)(2,1)S(1)} collective-permute-done((bf16[256,1024]{1,0:T(8,128)(2,1)S(1)}, bf16[256,1024]{1,0:T(8,128)(2,1)S(1)}, u32[]{:S(2)}, u32[]{:S(2)}) %collective-permute-start.6) | collective-permute-done | bytes 524320 | tf_op jit(solution)/shard_map/ppermute | solution.py:31
  21.7 0.1 shard_map.67
  21.8 0.7 %collective-permute-start.7 = (bf16[128,1024]{1,0:T(8,128)(2,1)S(1)}, bf16[128,1024]{1,0:T(8,128)(2,1)S(1)}, u32[]{:S(2)}, u32[]{:S(2)}) collective-permute-start(bf16[128,1024]{1,0:T(8,128)(2,1)S(1)} %shard_map.67), channel_id=1, source_target_pairs={{3,0},{5,2},{7,4},{11,8},{13,10},{15,12},{19,16},{21,18},{23,20},{... | collective-permute-start | bytes 786440 | tf_op jit(solution)/shard_map/ppermute | solution.py:31
  22.4 0.0 collective-permute-done.8.relayed_ref
  22.5 0.1 shard_map.68
  22.6 1.3 %collective-permute-start.9 = (bf16[128,1024]{1,0:T(8,128)(2,1)S(1)}, bf16[128,1024]{1,0:T(8,128)(2,1)S(1)}, u32[]{:S(2)}, u32[]{:S(2)}) collective-permute-start(bf16[128,1024]{1,0:T(8,128)(2,1)S(1)} %shard_map.68), channel_id=1, source_target_pairs={{2,1},{4,3},{6,5},{10,9},{12,11},{14,13},{18,17},{20,19},{22,21},{... | collective-permute-start | bytes 786440 | tf_op jit(solution)/shard_map/ppermute | solution.py:31
  23.9 2.6 %shard_map.66 = (bf16[128,4096]{1,0:T(8,128)(2,1)}, f32[128,1024]{1,0:T(8,128)S(1)}) custom-call(bf16[128,4096]{1,0:T(8,128)(2,1)S(1)} %bitcast.10, bf16[128,4096]{1,0:T(8,128)(2,1)S(1)} %bitcast.16, bf16[128,1024]{1,0:T(8,128)(2,1)S(1)} %bitcast.21, bf16[128,1024]{1,0:T(8,128)(2,1)S(1)} %collective-permute-done.refs_3_.refs_4_, ...), custom_call_target="tpu_custom_call" | custom-call | flops 805306368 | bytes 12451840 | tf_op jit(solution)/shard_map/pallas_call | solution.py:421
  26.5 0.0 collective-permute-done.7.odd_ref
  26.5 17.9 %collective-permute-done.9.even_ref = bf16[128,1024]{1,0:T(8,128)(2,1)S(1)} collective-permute-done((bf16[128,1024]{1,0:T(8,128)(2,1)S(1)}, bf16[128,1024]{1,0:T(8,128)(2,1)S(1)}, u32[]{:S(2)}, u32[]{:S(2)}) %collective-permute-start.9) | collective-permute-done | bytes 262176 | tf_op jit(solution)/shard_map/ppermute | solution.py:31
  44.4 0.8 %shard_map.69 = bf16[128,1024]{1,0:T(8,128)(2,1)} custom-call(f32[128,1024]{1,0:T(8,128)S(1)} %get-tuple-element.36.own_ref, bf16[256,1024]{1,0:T(8,128)(2,1)S(1)} %collective-permute-done.6.pair_ref, bf16[128,1024]{1,0:T(8,128)(2,1)S(1)} %collective-permute-done.7.odd_ref, bf16[128,1024]{1,0:T(8,128)(2,1)S(1)} %collective-permute-done.9.even_ref), custom_call_target="tpu_custom_call" | custom-call | flops 1048576 | bytes 1835008 | tf_op jit(solution)/shard_map/pallas_call | solution.py:421
  (1 shorter events, 0.0 us)
Async XLA Ops:
  0.6 11.6 %copy-start = (bf16[1,128,4096]{2,1,0:T(8,128)(2,1)S(1)}, bf16[1,128,4096]{2,1,0:T(8,128)(2,1)}, u32[]{:S(2)}) copy-start(bf16[1,128,4096]{2,1,0:T(8,128)(2,1)} %param.4) | copy-start | bytes 3145732
  0.6 11.6 %copy-start.1 = (bf16[1,128,4096]{2,1,0:T(8,128)(2,1)S(1)}, bf16[1,128,4096]{2,1,0:T(8,128)(2,1)}, u32[]{:S(2)}) copy-start(bf16[1,128,4096]{2,1,0:T(8,128)(2,1)} %param.6) | copy-start | bytes 3145732
  0.6 11.6 %copy-start.2 = (bf16[1,128,1024]{2,1,0:T(8,128)(2,1)S(1)}, bf16[1,128,1024]{2,1,0:T(8,128)(2,1)}, u32[]{:S(2)}) copy-start(bf16[1,128,1024]{2,1,0:T(8,128)(2,1)} %param.5) | copy-start | bytes 786436
  0.7 11.1 %collective-permute-start = (bf16[128,1024]{1,0:T(8,128)(2,1)}, bf16[128,1024]{1,0:T(8,128)(2,1)S(1)}, u32[]{:S(2)}, u32[]{:S(2)}) collective-permute-start(bf16[128,1024]{1,0:T(8,128)(2,1)} %bitcast.17), channel_id=1, source_target_pairs={{0,3},{1,2},{2,5},{3,4},{4,7},{5,6},{8,11},{9,10},{10,13},{11,12},... | collective-permute-start | bytes 786440 | tf_op jit(solution)/shard_map/ppermute | solution.py:31
  5.4 13.0 %collective-permute-start.3 = (bf16[128,1024]{1,0:T(8,128)(2,1)}, bf16[128,1024]{1,0:T(8,128)(2,1)S(1)}, u32[]{:S(2)}, u32[]{:S(2)}) collective-permute-start(bf16[128,1024]{1,0:T(8,128)(2,1)} %bitcast.18), channel_id=1, source_target_pairs={{1,4},{3,6},{9,12},{11,14},{17,20},{19,22},{25,28},{27,30}} | collective-permute-start | bytes 786440 | tf_op jit(solution)/shard_map/ppermute | solution.py:31
  9.3 7.5 %collective-permute-start.1 = (bf16[128,1024]{1,0:T(8,128)(2,1)}, bf16[128,1024]{1,0:T(8,128)(2,1)S(1)}, u32[]{:S(2)}, u32[]{:S(2)}) collective-permute-start(bf16[128,1024]{1,0:T(8,128)(2,1)} %bitcast.19), channel_id=1, source_target_pairs={{0,1},{1,0},{2,3},{3,2},{4,5},{5,4},{6,7},{7,6},{8,9},{9,8},{10,11... | collective-permute-start | bytes 786440 | tf_op jit(solution)/shard_map/ppermute | solution.py:31
  9.4 3.6 %collective-permute-start.4 = (s32[2]{0:T(128)}, s32[2]{0:T(128)S(1)}, u32[]{:S(2)}, u32[]{:S(2)}) collective-permute-start(s32[2]{0:T(128)} %refs_0_.1), channel_id=1, source_target_pairs={{0,8},{8,0},{16,24},{24,16},{1,9},{9,1},{17,25},{25,17},{2,10},{10... | collective-permute-start | bytes 32 | tf_op jit(solution)/shard_map/ppermute | solution.py:47
  11.8 6.3 %collective-permute-start.2 = (bf16[128,1024]{1,0:T(8,128)(2,1)S(1)}, bf16[128,1024]{1,0:T(8,128)(2,1)S(1)}, u32[]{:S(2)}, u32[]{:S(2)}) collective-permute-start(bf16[128,1024]{1,0:T(8,128)(2,1)S(1)} %collective-permute-done.refs_3_.refs_4_), channel_id=1, source_target_pairs={{0,1},{1,0},{2,3},{3,2},{4,5},{5,4},{6,7},{7,6},{8,9},{9,8},{10,11... | collective-permute-start | bytes 786440 | tf_op jit(solution)/shard_map/ppermute | solution.py:31
  12.2 0.8 %copy-start.3 = (s32[2]{0:T(128)S(1)}, s32[2]{0:T(128)}, u32[]{:S(2)}) copy-start(s32[2]{0:T(128)} %refs_0_.1) | copy-start | bytes 28
  13.1 2.4 %collective-permute-start.5 = (s32[4]{0:T(128)S(1)}, s32[4]{0:T(128)S(1)}, u32[]{:S(2)}, u32[]{:S(2)}) collective-permute-start(s32[4]{0:T(128)S(1)} %pad_add_fusion), channel_id=1, source_target_pairs={{0,16},{8,24},{16,0},{24,8},{1,17},{9,25},{17,1},{25,9},{2,18},{10... | collective-permute-start | bytes 56 | tf_op jit(solution)/shard_map/ppermute | solution.py:47
  19.7 2.0 %collective-permute-start.6 = (bf16[256,1024]{1,0:T(8,128)(2,1)S(1)}, bf16[256,1024]{1,0:T(8,128)(2,1)S(1)}, u32[]{:S(2)}, u32[]{:S(2)}) collective-permute-start(bf16[256,1024]{1,0:T(8,128)(2,1)S(1)} %get-tuple-element.37), channel_id=1, source_target_pairs={{0,1},{1,0},{2,3},{3,2},{4,5},{5,4},{6,7},{7,6},{8,9},{9,8},{10,11... | collective-permute-start | bytes 1572872 | tf_op jit(solution)/shard_map/ppermute | solution.py:31
  19.8 2.7 %collective-permute-start.8 = (bf16[128,1024]{1,0:T(8,128)(2,1)S(1)}, bf16[128,1024]{1,0:T(8,128)(2,1)S(1)}, u32[]{:S(2)}, u32[]{:S(2)}) collective-permute-start(bf16[128,1024]{1,0:T(8,128)(2,1)S(1)} %get-tuple-element.38.far_ref), channel_id=1, source_target_pairs={{4,2},{6,4},{12,10},{14,12},{20,18},{22,20},{28,26},{30,28}} | collective-permute-start | bytes 786440 | tf_op jit(solution)/shard_map/ppermute | solution.py:31
  21.8 4.7 %collective-permute-start.7 = (bf16[128,1024]{1,0:T(8,128)(2,1)S(1)}, bf16[128,1024]{1,0:T(8,128)(2,1)S(1)}, u32[]{:S(2)}, u32[]{:S(2)}) collective-permute-start(bf16[128,1024]{1,0:T(8,128)(2,1)S(1)} %shard_map.67), channel_id=1, source_target_pairs={{3,0},{5,2},{7,4},{11,8},{13,10},{15,12},{19,16},{21,18},{23,20},{... | collective-permute-start | bytes 786440 | tf_op jit(solution)/shard_map/ppermute | solution.py:31
  22.6 21.9 %collective-permute-start.9 = (bf16[128,1024]{1,0:T(8,128)(2,1)S(1)}, bf16[128,1024]{1,0:T(8,128)(2,1)S(1)}, u32[]{:S(2)}, u32[]{:S(2)}) collective-permute-start(bf16[128,1024]{1,0:T(8,128)(2,1)S(1)} %shard_map.68), channel_id=1, source_target_pairs={{2,1},{4,3},{6,5},{10,9},{12,11},{14,13},{18,17},{20,19},{22,21},{... | collective-permute-start | bytes 786440 | tf_op jit(solution)/shard_map/ppermute | solution.py:31
